TPU v7x, 512 devices: a whole 4x4x16 slice. The times are simulated.
512 devices in a mesh: section: 4 (over z_hi, core), ctx: 16 (over y, x), tp: 8 (over z_lo).
Axes of the slice: x: 4, y: 4, z: 16 (z_hi: 2, z_lo: 8; z = z_hi * 8 + z_lo), core: 2. Of those that a mesh axis runs over, the one named last changes fastest.
Arguments:
- query_heads: bfloat16 [8192, 8, 1024], P('ctx', 'tp', 'section'), may hold values from -10 to 10
- key_cache: bfloat16 [16, 512, 1024], P('ctx', ('section', 'tp')), may hold values from -4 to 4
- value_cache: bfloat16 [16, 512, 1024], P('ctx', ('section', 'tp')), may hold values from -6 to 6
- doc_lengths: int32 [4], replicated, may hold values from 1 to 5120, 8192 in all
Outputs:
- attended: bfloat16 [8192, 8, 1024], P('ctx', 'tp', 'section')
All inputs are finite; a program needn't handle non-finite values.
Results may differ from a plain program's by a relative error of at most 0.0044.
Values may be sent and summed in bfloat16 or wider, within the bound.
No kernel may reach another device: no remote copies, remote signals or barrier semaphores. Data moves between devices by JAX's collectives and lax.ppermute only.
A program may use at most 64 MiB of HBM per device.

v0:
```python
import jax
import jax.numpy as jnp
from jax import lax
from jax.sharding import PartitionSpec as P

HD = 128


def from_behind(shard, axis, by):
    count = lax.axis_size(axis)
    pairs = [(i, i + by) for i in range(count) if 0 <= i + by < count]
    return lax.ppermute(shard, axis, pairs)


def segment_of(positions, doc_ends):
    return jnp.sum((positions[:, None] >= doc_ends[None, :]).astype(jnp.int32), axis=1)


def attend_block(carried, queries, key_block, value_block, query_pos, query_seg, key_pos, key_seg):
    running_max, running_sum, accumulator = carried
    scale_factor = queries.shape[-1] ** (-0.5)
    scores = (
        jnp.einsum("qkhd,pkd->khqp", queries, key_block, preferred_element_type=jnp.float32)
        * scale_factor
    )
    allowed = (
        (key_pos[None, :] <= query_pos[:, None])
        & (key_seg[None, :] == query_seg[:, None])
        & (key_pos[None, :] >= 0)
    )
    masked = jnp.where(allowed, scores, -1e30)
    new_max = jnp.maximum(running_max, jnp.max(masked, axis=-1))
    weights = jnp.where(allowed, jnp.exp(scores - new_max[..., None]), 0.0)
    rescale = jnp.exp(running_max - new_max)
    running_sum = running_sum * rescale + jnp.sum(weights, axis=-1)
    accumulator = accumulator * rescale[..., None] + jnp.einsum(
        "khqp,pkd->khqd",
        weights.astype(jnp.bfloat16),
        value_block,
        preferred_element_type=jnp.float32,
    )
    return (new_max, running_sum, accumulator)


def shards(query_heads, key_cache, value_cache, doc_lengths):
    block_rows = query_heads.shape[0]
    local_groups = query_heads.shape[1]
    head_size = HD
    heads_here = query_heads.shape[2] // head_size
    queries = query_heads.reshape(block_rows, local_groups, heads_here, head_size)
    cycle_length = lax.axis_size("ctx")
    key_part, value_part = (
        lax.all_to_all(key_cache, "tp", split_axis=2, concat_axis=1, tiled=True),
        lax.all_to_all(value_cache, "tp", split_axis=2, concat_axis=1, tiled=True),
    )
    key_rows, value_rows = (
        lax.all_gather(key_part, "section", axis=1, tiled=True),
        lax.all_gather(value_part, "section", axis=1, tiled=True),
    )
    doc_ends = jnp.cumsum(doc_lengths)
    block_index = lax.axis_index("ctx")
    query_pos = block_index * block_rows + jnp.arange(block_rows, dtype=jnp.int32)
    query_seg = segment_of(query_pos, doc_ends)
    start_state = (
        jnp.full((local_groups, heads_here, block_rows), -1e30, jnp.float32),
        jnp.zeros((local_groups, heads_here, block_rows), jnp.float32),
        jnp.zeros((local_groups, heads_here, block_rows, head_size), jnp.float32),
    )

    def visit_block(carried, key_block, value_block, which_block):
        key_pos = which_block * block_rows + jnp.arange(block_rows, dtype=jnp.int32)
        return attend_block(
            carried,
            queries,
            key_block.reshape(block_rows, local_groups, head_size),
            value_block.reshape(block_rows, local_groups, head_size),
            query_pos,
            query_seg,
            key_pos,
            segment_of(key_pos, doc_ends),
        )

    stacked = jnp.concatenate((key_rows, value_rows), axis=0)
    own_state = visit_block(start_state, stacked[0], stacked[1], block_index)

    def hop_once(step_index, carried):
        state_now, travelling = carried
        travelling = from_behind(travelling, "ctx", 1)
        state_now = visit_block(
            state_now, travelling[0], travelling[1], block_index - step_index - 1
        )
        return (state_now, travelling)

    final_state, unused = lax.fori_loop(0, cycle_length - 1, hop_once, (own_state, stacked))
    running_max, running_sum, accumulator = final_state
    attended = accumulator / running_sum[..., None]
    return (
        attended.transpose(2, 0, 1, 3)
        .reshape(block_rows, local_groups, heads_here * head_size)
        .astype(jnp.bfloat16)
    )


def solution(mesh):
    placed = (
        P("ctx", "tp", "section"),
        P("ctx", ("section", "tp"), None),
        P("ctx", ("section", "tp"), None),
        P(),
    )
    return jax.shard_map(
        shards, mesh=mesh, in_specs=placed, out_specs=P("ctx", "tp", "section"), check_vma=False
    )
```

profile of v0, /device:TPU:56, one launch (start us, length us, event | category | flops | bytes accessed | tf_op | source)
XLA Modules:
  0.0 263.9 jit_solution(17596082021875644668)
XLA Ops:
  1.7 2.3 reduce.14
  4.9 12.6 %all-to-all-start = ((bf16[8,2,1024]{2,1,0:T(2,128)(2,1)}), bf16[8,2,1024]{2,1,0:T(2,128)(2,1)S(1)}, u32[]{:S(2)}, u32[]{:S(2)}) async-start(bf16[8,2,1024]{2,1,0:T(2,128)(2,1)} %reshape.235), calls=%async_computation | async-start | bytes 65536 | tf_op jit(solution)/shard_map/all_to_all | solution.py:53
  19.5 2.3 reduce.15
  22.8 3.8 %all-to-all-done = bf16[8,2,1024]{2,1,0:T(2,128)(2,1)S(1)} async-done(((bf16[8,2,1024]{2,1,0:T(2,128)(2,1)}), bf16[8,2,1024]{2,1,0:T(2,128)(2,1)S(1)}, u32[]{:S(2)}, u32[]{:S(2)}) %all-to-all-start) | async-done | bytes 32800 | tf_op jit(solution)/shard_map/all_to_all | solution.py:53
  26.7 6.1 %all-to-all-start.1 = ((bf16[8,2,1024]{2,1,0:T(2,128)(2,1)}), bf16[8,2,1024]{2,1,0:T(2,128)(2,1)S(1)}, u32[]{:S(2)}, u32[]{:S(2)}) async-start(bf16[8,2,1024]{2,1,0:T(2,128)(2,1)} %reshape.237), calls=%async_computation.1 | async-start | bytes 65536 | tf_op jit(solution)/shard_map/all_to_all | solution.py:54
  33.5 14.2 %all_gather.6 = bf16[1,512,128]{2,1,0:T(8,128)(2,1)S(1)} all-gather(bf16[1,128,128]{2,1,0:T(8,128)(2,1)S(1)} %bitcast.151), channel_id=1, replica_groups=mesh['section'=4,'ctx'=16,'tp'=8] {'section'}, dimensions={1}, use_global_device_ids=true | all-gather | bytes 163840 | tf_op jit(solution)/shard_map/all_gather | solution.py:57
  49.7 14.1 %all_gather.7 = bf16[1,512,128]{2,1,0:T(8,128)(2,1)S(1)} all-gather(bf16[1,128,128]{2,1,0:T(8,128)(2,1)S(1)} %bitcast.153), channel_id=1, replica_groups=mesh['section'=4,'ctx'=16,'tp'=8] {'section'}, dimensions={1}, use_global_device_ids=true | all-gather | bytes 163840 | tf_op jit(solution)/shard_map/all_gather | solution.py:58
  65.2 197.8 %while.22 = (s32[]{:T(128)}, f32[1,2,512]{2,1,0:T(2,128)S(1)}, f32[1,2,512]{2,1,0:T(2,128)S(1)}, f32[1,2,512,128]{3,2,1,0:T(8,128)S(1)}, bf16[2,512,128]{2,1,0:T...) while((s32[]{:T(128)}, f32[1,2,512]{2,1,0:T(2,128)S(1)}, ...), condition=%wide.region_8.9_spmd.clone, body=%wide.region_4.0_spmd.clone.sunk | while | flops 275524096 | bytes 10568933 | solution.py:94
  65.2 3.4 %collective-permute-start = (bf16[2,512,128]{2,1,0:T(8,128)(2,1)S(1)}, bf16[2,512,128]{2,1,0:T(8,128)(2,1)S(1)}, u32[]{:S(2)}, u32[]{:S(2)}) collective-permute-start(bf16[2,512,128]{2,1,0:T(8,128)(2,1)S(1)} %get-tuple-element.434), channel_id=1, source_target_pairs={{0,8},{8,16},{16,24},{24,32},{32,40},{40,48},{48,56},{56,64},{64,7... | collective-permute-start | bytes 786440 | tf_op jit(solution)/shard_map/while/body/eval_jaxpr/ppermute | solution.py:12
  69.0 8.7 %collective-permute-done = bf16[2,512,128]{2,1,0:T(8,128)(2,1)S(1)} collective-permute-done((bf16[2,512,128]{2,1,0:T(8,128)(2,1)S(1)}, bf16[2,512,128]{2,1,0:T(8,128)(2,1)S(1)}, u32[]{:S(2)}, u32[]{:S(2)}) %collective-permute-start) | collective-permute-done | bytes 262176 | tf_op jit(solution)/shard_map/while/body/eval_jaxpr/ppermute | solution.py:12
  82.1 9.4 %collective-permute-done = bf16[2,512,128]{2,1,0:T(8,128)(2,1)S(1)} collective-permute-done((bf16[2,512,128]{2,1,0:T(8,128)(2,1)S(1)}, bf16[2,512,128]{2,1,0:T(8,128)(2,1)S(1)}, u32[]{:S(2)}, u32[]{:S(2)}) %collective-permute-start) | collective-permute-done | bytes 262176 | tf_op jit(solution)/shard_map/while/body/eval_jaxpr/ppermute | solution.py:12
  95.8 8.5 %collective-permute-done = bf16[2,512,128]{2,1,0:T(8,128)(2,1)S(1)} collective-permute-done((bf16[2,512,128]{2,1,0:T(8,128)(2,1)S(1)}, bf16[2,512,128]{2,1,0:T(8,128)(2,1)S(1)}, u32[]{:S(2)}, u32[]{:S(2)}) %collective-permute-start) | collective-permute-done | bytes 262176 | tf_op jit(solution)/shard_map/while/body/eval_jaxpr/ppermute | solution.py:12
  108.7 8.0 %collective-permute-done = bf16[2,512,128]{2,1,0:T(8,128)(2,1)S(1)} collective-permute-done((bf16[2,512,128]{2,1,0:T(8,128)(2,1)S(1)}, bf16[2,512,128]{2,1,0:T(8,128)(2,1)S(1)}, u32[]{:S(2)}, u32[]{:S(2)}) %collective-permute-start) | collective-permute-done | bytes 262176 | tf_op jit(solution)/shard_map/while/body/eval_jaxpr/ppermute | solution.py:12
  121.0 8.0 %collective-permute-done = bf16[2,512,128]{2,1,0:T(8,128)(2,1)S(1)} collective-permute-done((bf16[2,512,128]{2,1,0:T(8,128)(2,1)S(1)}, bf16[2,512,128]{2,1,0:T(8,128)(2,1)S(1)}, u32[]{:S(2)}, u32[]{:S(2)}) %collective-permute-start) | collective-permute-done | bytes 262176 | tf_op jit(solution)/shard_map/while/body/eval_jaxpr/ppermute | solution.py:12
  133.4 8.0 %collective-permute-done = bf16[2,512,128]{2,1,0:T(8,128)(2,1)S(1)} collective-permute-done((bf16[2,512,128]{2,1,0:T(8,128)(2,1)S(1)}, bf16[2,512,128]{2,1,0:T(8,128)(2,1)S(1)}, u32[]{:S(2)}, u32[]{:S(2)}) %collective-permute-start) | collective-permute-done | bytes 262176 | tf_op jit(solution)/shard_map/while/body/eval_jaxpr/ppermute | solution.py:12
  145.8 8.0 %collective-permute-done = bf16[2,512,128]{2,1,0:T(8,128)(2,1)S(1)} collective-permute-done((bf16[2,512,128]{2,1,0:T(8,128)(2,1)S(1)}, bf16[2,512,128]{2,1,0:T(8,128)(2,1)S(1)}, u32[]{:S(2)}, u32[]{:S(2)}) %collective-permute-start) | collective-permute-done | bytes 262176 | tf_op jit(solution)/shard_map/while/body/eval_jaxpr/ppermute | solution.py:12
  158.1 8.0 %collective-permute-done = bf16[2,512,128]{2,1,0:T(8,128)(2,1)S(1)} collective-permute-done((bf16[2,512,128]{2,1,0:T(8,128)(2,1)S(1)}, bf16[2,512,128]{2,1,0:T(8,128)(2,1)S(1)}, u32[]{:S(2)}, u32[]{:S(2)}) %collective-permute-start) | collective-permute-done | bytes 262176 | tf_op jit(solution)/shard_map/while/body/eval_jaxpr/ppermute | solution.py:12
  170.5 8.6 %collective-permute-done = bf16[2,512,128]{2,1,0:T(8,128)(2,1)S(1)} collective-permute-done((bf16[2,512,128]{2,1,0:T(8,128)(2,1)S(1)}, bf16[2,512,128]{2,1,0:T(8,128)(2,1)S(1)}, u32[]{:S(2)}, u32[]{:S(2)}) %collective-permute-start) | collective-permute-done | bytes 262176 | tf_op jit(solution)/shard_map/while/body/eval_jaxpr/ppermute | solution.py:12
  183.4 9.7 %collective-permute-done = bf16[2,512,128]{2,1,0:T(8,128)(2,1)S(1)} collective-permute-done((bf16[2,512,128]{2,1,0:T(8,128)(2,1)S(1)}, bf16[2,512,128]{2,1,0:T(8,128)(2,1)S(1)}, u32[]{:S(2)}, u32[]{:S(2)}) %collective-permute-start) | collective-permute-done | bytes 262176 | tf_op jit(solution)/shard_map/while/body/eval_jaxpr/ppermute | solution.py:12
  197.5 10.8 %collective-permute-done = bf16[2,512,128]{2,1,0:T(8,128)(2,1)S(1)} collective-permute-done((bf16[2,512,128]{2,1,0:T(8,128)(2,1)S(1)}, bf16[2,512,128]{2,1,0:T(8,128)(2,1)S(1)}, u32[]{:S(2)}, u32[]{:S(2)}) %collective-permute-start) | collective-permute-done | bytes 262176 | tf_op jit(solution)/shard_map/while/body/eval_jaxpr/ppermute | solution.py:12
  212.6 10.0 %collective-permute-done = bf16[2,512,128]{2,1,0:T(8,128)(2,1)S(1)} collective-permute-done((bf16[2,512,128]{2,1,0:T(8,128)(2,1)S(1)}, bf16[2,512,128]{2,1,0:T(8,128)(2,1)S(1)}, u32[]{:S(2)}, u32[]{:S(2)}) %collective-permute-start) | collective-permute-done | bytes 262176 | tf_op jit(solution)/shard_map/while/body/eval_jaxpr/ppermute | solution.py:12
  226.9 9.1 %collective-permute-done = bf16[2,512,128]{2,1,0:T(8,128)(2,1)S(1)} collective-permute-done((bf16[2,512,128]{2,1,0:T(8,128)(2,1)S(1)}, bf16[2,512,128]{2,1,0:T(8,128)(2,1)S(1)}, u32[]{:S(2)}, u32[]{:S(2)}) %collective-permute-start) | collective-permute-done | bytes 262176 | tf_op jit(solution)/shard_map/while/body/eval_jaxpr/ppermute | solution.py:12
  240.4 8.2 %collective-permute-done = bf16[2,512,128]{2,1,0:T(8,128)(2,1)S(1)} collective-permute-done((bf16[2,512,128]{2,1,0:T(8,128)(2,1)S(1)}, bf16[2,512,128]{2,1,0:T(8,128)(2,1)S(1)}, u32[]{:S(2)}, u32[]{:S(2)}) %collective-permute-start) | collective-permute-done | bytes 262176 | tf_op jit(solution)/shard_map/while/body/eval_jaxpr/ppermute | solution.py:12
  252.9 8.0 %collective-permute-done = bf16[2,512,128]{2,1,0:T(8,128)(2,1)S(1)} collective-permute-done((bf16[2,512,128]{2,1,0:T(8,128)(2,1)S(1)}, bf16[2,512,128]{2,1,0:T(8,128)(2,1)S(1)}, u32[]{:S(2)}, u32[]{:S(2)}) %collective-permute-start) | collective-permute-done | bytes 262176 | tf_op jit(solution)/shard_map/while/body/eval_jaxpr/ppermute | solution.py:12
  (220 shorter events, 72.4 us)
Async XLA Ops:
  0.0 18.8 %copy-start = (bf16[512,1,256]{2,0,1:T(8,128)(2,1)S(1)}, bf16[512,1,256]{2,0,1:T(8,128)(2,1)}, u32[]{:S(2)}) copy-start(bf16[512,1,256]{2,0,1:T(8,128)(2,1)} %param.6) | copy-start | bytes 786436
  0.0 19.1 %copy-start.1 = (bf16[1,16,1024]{2,1,0:T(8,128)(2,1)S(1)}, bf16[1,16,1024]{2,1,0:T(8,128)(2,1)}, u32[]{:S(2)}) copy-start(bf16[1,16,1024]{2,1,0:T(8,128)(2,1)} %param.8) | copy-start | bytes 98308
  4.9 21.7 %all-to-all-start = ((bf16[8,2,1024]{2,1,0:T(2,128)(2,1)}), bf16[8,2,1024]{2,1,0:T(2,128)(2,1)S(1)}, u32[]{:S(2)}, u32[]{:S(2)}) async-start(bf16[8,2,1024]{2,1,0:T(2,128)(2,1)} %reshape.235), calls=%async_computation | async-start | bytes 65536 | tf_op jit(solution)/shard_map/all_to_all | solution.py:53
  26.7 22.2 %all-to-all-start.1 = ((bf16[8,2,1024]{2,1,0:T(2,128)(2,1)}), bf16[8,2,1024]{2,1,0:T(2,128)(2,1)S(1)}, u32[]{:S(2)}, u32[]{:S(2)}) async-start(bf16[8,2,1024]{2,1,0:T(2,128)(2,1)} %reshape.237), calls=%async_computation.1 | async-start | bytes 65536 | tf_op jit(solution)/shard_map/all_to_all | solution.py:54
  48.3 1.3 copy-start.2
  49.6 14.7 %copy-start.4 = (f32[2,512]{1,0:T(2,128)S(1)}, f32[2,512]{1,0:T(2,128)}, u32[]{:S(2)}) copy-start(f32[2,512]{1,0:T(2,128)} %get-tuple-element.339) | copy-start | bytes 12292
  64.4 0.8 copy-start.3
  65.2 12.6 %collective-permute-start = (bf16[2,512,128]{2,1,0:T(8,128)(2,1)S(1)}, bf16[2,512,128]{2,1,0:T(8,128)(2,1)S(1)}, u32[]{:S(2)}, u32[]{:S(2)}) collective-permute-start(bf16[2,512,128]{2,1,0:T(8,128)(2,1)S(1)} %get-tuple-element.434), channel_id=1, source_target_pairs={{0,8},{8,16},{16,24},{24,32},{32,40},{40,48},{48,56},{56,64},{64,7... | collective-permute-start | bytes 786440 | tf_op jit(solution)/shard_map/while/body/eval_jaxpr/ppermute | solution.py:12
  79.7 11.8 %collective-permute-start = (bf16[2,512,128]{2,1,0:T(8,128)(2,1)S(1)}, bf16[2,512,128]{2,1,0:T(8,128)(2,1)S(1)}, u32[]{:S(2)}, u32[]{:S(2)}) collective-permute-start(bf16[2,512,128]{2,1,0:T(8,128)(2,1)S(1)} %get-tuple-element.434), channel_id=1, source_target_pairs={{0,8},{8,16},{16,24},{24,32},{32,40},{40,48},{48,56},{56,64},{64,7... | collective-permute-start | bytes 786440 | tf_op jit(solution)/shard_map/while/body/eval_jaxpr/ppermute | solution.py:12
  93.5 10.8 %collective-permute-start = (bf16[2,512,128]{2,1,0:T(8,128)(2,1)S(1)}, bf16[2,512,128]{2,1,0:T(8,128)(2,1)S(1)}, u32[]{:S(2)}, u32[]{:S(2)}) collective-permute-start(bf16[2,512,128]{2,1,0:T(8,128)(2,1)S(1)} %get-tuple-element.434), channel_id=1, source_target_pairs={{0,8},{8,16},{16,24},{24,32},{32,40},{40,48},{48,56},{56,64},{64,7... | collective-permute-start | bytes 786440 | tf_op jit(solution)/shard_map/while/body/eval_jaxpr/ppermute | solution.py:12
  106.3 10.4 %collective-permute-start = (bf16[2,512,128]{2,1,0:T(8,128)(2,1)S(1)}, bf16[2,512,128]{2,1,0:T(8,128)(2,1)S(1)}, u32[]{:S(2)}, u32[]{:S(2)}) collective-permute-start(bf16[2,512,128]{2,1,0:T(8,128)(2,1)S(1)} %get-tuple-element.434), channel_id=1, source_target_pairs={{0,8},{8,16},{16,24},{24,32},{32,40},{40,48},{48,56},{56,64},{64,7... | collective-permute-start | bytes 786440 | tf_op jit(solution)/shard_map/while/body/eval_jaxpr/ppermute | solution.py:12
  118.7 10.4 %collective-permute-start = (bf16[2,512,128]{2,1,0:T(8,128)(2,1)S(1)}, bf16[2,512,128]{2,1,0:T(8,128)(2,1)S(1)}, u32[]{:S(2)}, u32[]{:S(2)}) collective-permute-start(bf16[2,512,128]{2,1,0:T(8,128)(2,1)S(1)} %get-tuple-element.434), channel_id=1, source_target_pairs={{0,8},{8,16},{16,24},{24,32},{32,40},{40,48},{48,56},{56,64},{64,7... | collective-permute-start | bytes 786440 | tf_op jit(solution)/shard_map/while/body/eval_jaxpr/ppermute | solution.py:12
  131.0 10.4 %collective-permute-start = (bf16[2,512,128]{2,1,0:T(8,128)(2,1)S(1)}, bf16[2,512,128]{2,1,0:T(8,128)(2,1)S(1)}, u32[]{:S(2)}, u32[]{:S(2)}) collective-permute-start(bf16[2,512,128]{2,1,0:T(8,128)(2,1)S(1)} %get-tuple-element.434), channel_id=1, source_target_pairs={{0,8},{8,16},{16,24},{24,32},{32,40},{40,48},{48,56},{56,64},{64,7... | collective-permute-start | bytes 786440 | tf_op jit(solution)/shard_map/while/body/eval_jaxpr/ppermute | solution.py:12
  143.4 10.4 %collective-permute-start = (bf16[2,512,128]{2,1,0:T(8,128)(2,1)S(1)}, bf16[2,512,128]{2,1,0:T(8,128)(2,1)S(1)}, u32[]{:S(2)}, u32[]{:S(2)}) collective-permute-start(bf16[2,512,128]{2,1,0:T(8,128)(2,1)S(1)} %get-tuple-element.434), channel_id=1, source_target_pairs={{0,8},{8,16},{16,24},{24,32},{32,40},{40,48},{48,56},{56,64},{64,7... | collective-permute-start | bytes 786440 | tf_op jit(solution)/shard_map/while/body/eval_jaxpr/ppermute | solution.py:12
  155.8 10.4 %collective-permute-start = (bf16[2,512,128]{2,1,0:T(8,128)(2,1)S(1)}, bf16[2,512,128]{2,1,0:T(8,128)(2,1)S(1)}, u32[]{:S(2)}, u32[]{:S(2)}) collective-permute-start(bf16[2,512,128]{2,1,0:T(8,128)(2,1)S(1)} %get-tuple-element.434), channel_id=1, source_target_pairs={{0,8},{8,16},{16,24},{24,32},{32,40},{40,48},{48,56},{56,64},{64,7... | collective-permute-start | bytes 786440 | tf_op jit(solution)/shard_map/while/body/eval_jaxpr/ppermute | solution.py:12
  168.1 10.9 %collective-permute-start = (bf16[2,512,128]{2,1,0:T(8,128)(2,1)S(1)}, bf16[2,512,128]{2,1,0:T(8,128)(2,1)S(1)}, u32[]{:S(2)}, u32[]{:S(2)}) collective-permute-start(bf16[2,512,128]{2,1,0:T(8,128)(2,1)S(1)} %get-tuple-element.434), channel_id=1, source_target_pairs={{0,8},{8,16},{16,24},{24,32},{32,40},{40,48},{48,56},{56,64},{64,7... | collective-permute-start | bytes 786440 | tf_op jit(solution)/shard_map/while/body/eval_jaxpr/ppermute | solution.py:12
  181.1 12.0 %collective-permute-start = (bf16[2,512,128]{2,1,0:T(8,128)(2,1)S(1)}, bf16[2,512,128]{2,1,0:T(8,128)(2,1)S(1)}, u32[]{:S(2)}, u32[]{:S(2)}) collective-permute-start(bf16[2,512,128]{2,1,0:T(8,128)(2,1)S(1)} %get-tuple-element.434), channel_id=1, source_target_pairs={{0,8},{8,16},{16,24},{24,32},{32,40},{40,48},{48,56},{56,64},{64,7... | collective-permute-start | bytes 786440 | tf_op jit(solution)/shard_map/while/body/eval_jaxpr/ppermute | solution.py:12
  195.1 13.2 %collective-permute-start = (bf16[2,512,128]{2,1,0:T(8,128)(2,1)S(1)}, bf16[2,512,128]{2,1,0:T(8,128)(2,1)S(1)}, u32[]{:S(2)}, u32[]{:S(2)}) collective-permute-start(bf16[2,512,128]{2,1,0:T(8,128)(2,1)S(1)} %get-tuple-element.434), channel_id=1, source_target_pairs={{0,8},{8,16},{16,24},{24,32},{32,40},{40,48},{48,56},{56,64},{64,7... | collective-permute-start | bytes 786440 | tf_op jit(solution)/shard_map/while/body/eval_jaxpr/ppermute | solution.py:12
  210.3 12.3 %collective-permute-start = (bf16[2,512,128]{2,1,0:T(8,128)(2,1)S(1)}, bf16[2,512,128]{2,1,0:T(8,128)(2,1)S(1)}, u32[]{:S(2)}, u32[]{:S(2)}) collective-permute-start(bf16[2,512,128]{2,1,0:T(8,128)(2,1)S(1)} %get-tuple-element.434), channel_id=1, source_target_pairs={{0,8},{8,16},{16,24},{24,32},{32,40},{40,48},{48,56},{56,64},{64,7... | collective-permute-start | bytes 786440 | tf_op jit(solution)/shard_map/while/body/eval_jaxpr/ppermute | solution.py:12
  224.6 11.5 %collective-permute-start = (bf16[2,512,128]{2,1,0:T(8,128)(2,1)S(1)}, bf16[2,512,128]{2,1,0:T(8,128)(2,1)S(1)}, u32[]{:S(2)}, u32[]{:S(2)}) collective-permute-start(bf16[2,512,128]{2,1,0:T(8,128)(2,1)S(1)} %get-tuple-element.434), channel_id=1, source_target_pairs={{0,8},{8,16},{16,24},{24,32},{32,40},{40,48},{48,56},{56,64},{64,7... | collective-permute-start | bytes 786440 | tf_op jit(solution)/shard_map/while/body/eval_jaxpr/ppermute | solution.py:12
  238.0 10.6 %collective-permute-start = (bf16[2,512,128]{2,1,0:T(8,128)(2,1)S(1)}, bf16[2,512,128]{2,1,0:T(8,128)(2,1)S(1)}, u32[]{:S(2)}, u32[]{:S(2)}) collective-permute-start(bf16[2,512,128]{2,1,0:T(8,128)(2,1)S(1)} %get-tuple-element.434), channel_id=1, source_target_pairs={{0,8},{8,16},{16,24},{24,32},{32,40},{40,48},{48,56},{56,64},{64,7... | collective-permute-start | bytes 786440 | tf_op jit(solution)/shard_map/while/body/eval_jaxpr/ppermute | solution.py:12
  250.6 10.4 %collective-permute-start = (bf16[2,512,128]{2,1,0:T(8,128)(2,1)S(1)}, bf16[2,512,128]{2,1,0:T(8,128)(2,1)S(1)}, u32[]{:S(2)}, u32[]{:S(2)}) collective-permute-start(bf16[2,512,128]{2,1,0:T(8,128)(2,1)S(1)} %get-tuple-element.434), channel_id=1, source_target_pairs={{0,8},{8,16},{16,24},{24,32},{32,40},{40,48},{48,56},{56,64},{64,7... | collective-permute-start | bytes 786440 | tf_op jit(solution)/shard_map/while/body/eval_jaxpr/ppermute | solution.py:12
where the time goes:
time: 265 us; the launch traced here: 264 us
  waiting for transfers between devices  135 us (51%)
  starting transfers between devices  49 us (18%)
  blocking collectives  28.3 us (11%)
  matrix products  22.2 us (8%)
  other arithmetic  21.9 us (8%)
  local copies, waits for them, and re-layouts  6.07 us (2%)
    ppermute x15, waiting for transfers between devices, from_behind(): return lax.ppermute(shard, axis, pairs)  131 us
    ppermute x15, starting transfers between devices, from_behind(): return lax.ppermute(shard, axis, pairs)  30.3 us
    all_gather x1, blocking collectives, shards(): lax.all_gather(key_part, 'section', axis=1, tiled=True)  14.2 us
    all_gather x1, blocking collectives, shards(): lax.all_gather(value_part, 'section', axis=1, tiled=True)  14.1 us
    dot_general x16, matrix products, attend_block(): jnp.einsum('khqp,pkd->khqd', weights.astype(jnp.bfloat16), value_block, p...  13.3 us
    all_to_all x1, starting transfers between devices, shards(): lax.all_to_all(key_cache, 'tp', split_axis=2, concat_axis=1, tiled=True)  12.6 us
    dot_general x16, matrix products, attend_block(): jnp.einsum('qkhd,pkd->khqp', queries, key_block, preferred_element_type=j...  8.84 us
    reduce_sum x16, other arithmetic, attend_block(): running_sum = running_sum * rescale + jnp.sum(weights, axis=-1)  7.94 us
  transfers between devices with their start and end apart: 17, of which 16 were waited for; matrix products, arithmetic and copies ran while one was open for 5% of the time, Pallas kernels for 0%

commit v1 on v0

v1 whole, which is shorter than its diff:
```python
import math

import jax
import jax.numpy as jnp
from jax import lax
from jax.experimental import pallas as pl
from jax.experimental.pallas import tpu as pltpu
from jax.sharding import Mesh
from jax.sharding import PartitionSpec as P

HD = 128
NDOC = 4
ROWS = 512
LOW = -1e29
HIDDEN = -1e30
STEP = math.log2(math.e) / math.sqrt(HD)
HOPS = ((1, 4), (2, 8), (3, 7), (5, 6), (9, 10))


def attend_block(q_ref, blk_ref, which, block, starts, state, first_needed, last_start):
    m_ref, l_ref, acc_ref = state
    base = which * ROWS
    heads = q_ref.shape[1] // HD

    def visit(masked):
        keys = blk_ref[:, 0].reshape(ROWS, HD)
        values = blk_ref[:, 1].reshape(ROWS, HD)
        if masked:
            n = lax.broadcasted_iota(jnp.int32, (ROWS, ROWS), 0)
            row = (n & 127) + ((n >> 7) & 1) * 256 + (n >> 8) * 128 + base
            query = block * ROWS + lax.broadcasted_iota(jnp.int32, (1, ROWS), 1)
            begin = jnp.zeros_like(query)
            for s in starts:
                begin = jnp.where(query >= s, s, begin)
            allowed = (row <= query) & (row >= begin)
        for h in range(heads):
            scores = lax.dot_general(
                keys,
                q_ref[:, h * HD : (h + 1) * HD],
                (((1,), (1,)), ((), ())),
                preferred_element_type=jnp.float32,
            )
            if masked:
                scores = jnp.where(allowed, scores, HIDDEN)
            old = m_ref[h]
            new = jnp.maximum(old, jnp.max(scores, axis=0, keepdims=True))
            weights = jnp.exp2((scores - new) * STEP)
            rescale = jnp.exp2((old - new) * STEP)
            m_ref[h] = new
            l_ref[h] = l_ref[h] * rescale + jnp.sum(weights, axis=0, keepdims=True)
            acc_ref[h] = acc_ref[h] * rescale + lax.dot_general(
                values,
                weights.astype(jnp.bfloat16),
                (((0,), (0,)), ((), ())),
                preferred_element_type=jnp.float32,
            )

    needed = (which >= 0) & (base + ROWS > first_needed)
    whole = (which < block) & (base >= last_start)

    @pl.when(needed & whole)
    def _():
        visit(False)

    @pl.when(needed & jnp.logical_not(whole))
    def _():
        visit(True)


def doc_starts(lengths_ref):
    starts = []
    total = 0
    for d in range(NDOC - 1):
        total = total + lengths_ref[d]
        starts.append(total)
    return starts


def start_of(position, starts):
    begin = 0
    for s in starts:
        begin = jnp.where(position >= s, s, begin)
    return begin


def own_kernel(lengths_ref, q_ref, blk_ref, m_ref, l_ref, acc_ref):
    block = lax.axis_index("ctx")
    starts = doc_starts(lengths_ref)
    m_ref[...] = jnp.full(m_ref.shape, LOW, jnp.float32)
    l_ref[...] = jnp.zeros(l_ref.shape, jnp.float32)
    acc_ref[...] = jnp.zeros(acc_ref.shape, jnp.float32)
    attend_block(
        q_ref, blk_ref, block, block, starts, (m_ref, l_ref, acc_ref),
        start_of(block * ROWS, starts), start_of(block * ROWS + ROWS - 1, starts),
    )


def rest_kernel(hops, lengths_ref, q_ref, *refs):
    blocks = refs[: len(hops)]
    m_in, l_in, acc_in, out_ref, m_ref, l_ref, acc_ref = refs[len(hops) :]
    block = lax.axis_index("ctx")
    core = lax.axis_index("core")
    starts = doc_starts(lengths_ref)
    m_ref[...] = m_in[...]
    l_ref[...] = l_in[...]
    acc_ref[...] = acc_in[...]
    for blk_ref, (k0, k1) in zip(blocks, hops):
        attend_block(
            q_ref, blk_ref, block - jnp.where(core == 0, k0, k1), block, starts,
            (m_ref, l_ref, acc_ref),
            start_of(block * ROWS, starts), start_of(block * ROWS + ROWS - 1, starts),
        )
    for h in range(acc_ref.shape[0]):
        attended = acc_ref[h] / l_ref[h]
        out_ref[:, h * HD : (h + 1) * HD] = attended.T.astype(jnp.bfloat16)


def in_vmem(n):
    return [pl.BlockSpec(memory_space=pltpu.VMEM)] * n


def shards(query_heads, key_cache, value_cache, doc_lengths):
    rows, _, width = query_heads.shape
    queries = query_heads.reshape(rows, width)
    heads = width // HD
    part = key_cache.shape[1]
    tp = lax.axis_size("tp")
    blocks = lax.axis_size("ctx")

    def by_head(cache):
        return cache.reshape(part, tp, HD).transpose(1, 0, 2)

    send = jnp.stack((by_head(key_cache), by_head(value_cache)), axis=1)
    send = jnp.concatenate((send, send), axis=0)
    half = lax.all_to_all(send, ("zhi", "tp"), split_axis=0, concat_axis=0, tiled=True)
    own = lax.all_gather(half, "core", axis=0, tiled=True)

    arrived = []
    for k0, k1 in HOPS:
        pairs = [(b, b + k0) for b in range(blocks - k0)]
        pairs += [(blocks + b, blocks + b + k1) for b in range(blocks - k1)]
        arrived.append(lax.ppermute(own, ("core", "ctx"), pairs))
    swapped = [lax.ppermute(a, "core", [(0, 1), (1, 0)]) for a in arrived]

    state_shape = (
        jax.ShapeDtypeStruct((heads, 1, rows), jnp.float32),
        jax.ShapeDtypeStruct((heads, 1, rows), jnp.float32),
        jax.ShapeDtypeStruct((heads, HD, rows), jnp.float32),
    )
    smem = [pl.BlockSpec(memory_space=pltpu.SMEM)]
    state = pl.pallas_call(
        own_kernel,
        out_shape=state_shape,
        in_specs=smem + in_vmem(2),
        out_specs=tuple(in_vmem(3)),
        name="own_block",
    )(doc_lengths, queries, own)
    hops = list(HOPS) + [(k1, k0) for k0, k1 in HOPS]
    out = pl.pallas_call(
        lambda *refs: rest_kernel(hops, *refs),
        out_shape=jax.ShapeDtypeStruct((rows, width), jnp.bfloat16),
        in_specs=smem + in_vmem(1 + len(hops) + 3),
        out_specs=in_vmem(1)[0],
        scratch_shapes=[pltpu.VMEM(s.shape, s.dtype) for s in state_shape],
        name="earlier_blocks",
    )(doc_lengths, queries, *arrived, *swapped, *state)
    return out.reshape(query_heads.shape)


def solution(mesh):
    cut = Mesh(
        mesh.devices.reshape(2, 2, *mesh.devices.shape[1:]), ("zhi", "core", "ctx", "tp")
    )
    cache = P("ctx", ("zhi", "core", "tp"), None)
    heads = P("ctx", "tp", ("zhi", "core"))
    return jax.shard_map(
        shards, mesh=cut, in_specs=(heads, cache, cache, P()), out_specs=heads, check_vma=False
    )
```

time: 265 us -> 82 us (0.31)
  the two profiles are of different devices: /device:TPU:56 before, /device:TPU:19 now
where the time goes in v1:
time: 82 us; the launch traced here: 81.5 us
  blocking collectives  32 us (39%)
  starting transfers between devices  25.3 us (31%)
  waiting for transfers between devices  12.2 us (15%)
  Pallas kernels  9.93 us (12%)
  local copies, waits for them, and re-layouts  1.79 us (2%)
    all_to_all x1, blocking collectives, shards(): lax.all_to_all(send, ('zhi', 'tp'), split_axis=0, concat_axis=0, tiled=True)  26.7 us
    ppermute x5, starting transfers between devices, shards(): swapped = [lax.ppermute(a, 'core', [(0, 1), (1, 0)]) for a in arrived]  16.3 us
    ppermute x5, waiting for transfers between devices, shards(): arrived.append(lax.ppermute(own, ('core', 'ctx'), pairs))  12.2 us
    ppermute x5, starting transfers between devices, shards(): arrived.append(lax.ppermute(own, ('core', 'ctx'), pairs))  9.01 us
    pallas_call x1, Pallas kernels, shards(): pl.pallas_call(lambda *refs: rest_kernel(hops, *refs), out_shape=jax.Shap...  6.67 us
    all_gather x1, blocking collectives, shards(): own = lax.all_gather(half, 'core', axis=0, tiled=True)  5.27 us
    pallas_call x1, Pallas kernels, shards(): pl.pallas_call(own_kernel, out_shape=state_shape, in_specs=smem + in_vmem...  3.27 us
    unnamed x26, local copies, waits for them, and re-layouts  1.75 us
  transfers between devices with their start and end apart: 10, of which 1 were waited for; matrix products, arithmetic and copies ran while one was open for 0% of the time, Pallas kernels for 4%

profile of v1, /device:TPU:19, one launch (start us, length us, event | category | flops | bytes accessed | tf_op | source)
XLA Modules:
  0.0 81.5 jit_solution(14688534420401458327)
XLA Ops:
  0.0 0.8 copy.9
  0.9 26.7 %all_to_all.5 = bf16[16,2,16,128]{3,2,1,0:T(8,128)(2,1)S(1)} all-to-all(bf16[16,2,16,128]{3,2,1,0:T(8,128)(2,1)S(1)} %copy.8), channel_id=1, replica_groups=mesh['zhi'=2,'core'=2,'ctx'=16,'tp'=8] {'zhi','tp'}, dimensions={0} | all-to-all | bytes 262144 | tf_op jit(solution)/shard_map/all_to_all | solution.py:135
  27.6 5.3 %all_gather.3.blk_ref = bf16[32,2,16,128]{3,2,1,0:T(8,128)(2,1)S(1)} all-gather(bf16[16,2,16,128]{3,2,1,0:T(8,128)(2,1)S(1)} %all_to_all.5), channel_id=1, replica_groups=mesh['zhi'=2,'core'=2,'ctx'=16,'tp'=8] {'core'}, dimensions={0}, use_global_device_ids=true | all-gather | bytes 393216 | tf_op jit(solution)/shard_map/all_gather | solution.py:136
  32.9 2.9 %collective-permute-start = (bf16[32,2,16,128]{3,2,1,0:T(8,128)(2,1)S(1)}, bf16[32,2,16,128]{3,2,1,0:T(8,128)(2,1)S(1)}, u32[]{:S(2)}, u32[]{:S(2)}) collective-permute-start(bf16[32,2,16,128]{3,2,1,0:T(8,128)(2,1)S(1)} %all_gather.3.blk_ref), channel_id=1, source_target_pairs={{0,8},{8,16},{16,24},{24,32},{32,40},{40,48},{48,56},{56,64},{64,7... | collective-permute-start | bytes 786440 | tf_op jit(solution)/shard_map/ppermute | solution.py:142
  35.8 1.3 %collective-permute-start.1 = (bf16[32,2,16,128]{3,2,1,0:T(8,128)(2,1)S(1)}, bf16[32,2,16,128]{3,2,1,0:T(8,128)(2,1)S(1)}, u32[]{:S(2)}, u32[]{:S(2)}) collective-permute-start(bf16[32,2,16,128]{3,2,1,0:T(8,128)(2,1)S(1)} %all_gather.3.blk_ref), channel_id=1, source_target_pairs={{0,16},{8,24},{16,32},{24,40},{32,48},{40,56},{48,64},{56,72},{64,... | collective-permute-start | bytes 786440 | tf_op jit(solution)/shard_map/ppermute | solution.py:142
  37.1 1.3 %collective-permute-start.2 = (bf16[32,2,16,128]{3,2,1,0:T(8,128)(2,1)S(1)}, bf16[32,2,16,128]{3,2,1,0:T(8,128)(2,1)S(1)}, u32[]{:S(2)}, u32[]{:S(2)}) collective-permute-start(bf16[32,2,16,128]{3,2,1,0:T(8,128)(2,1)S(1)} %all_gather.3.blk_ref), channel_id=1, source_target_pairs={{0,24},{8,32},{16,40},{24,48},{32,56},{40,64},{48,72},{56,80},{64,... | collective-permute-start | bytes 786440 | tf_op jit(solution)/shard_map/ppermute | solution.py:142
  38.4 2.9 %collective-permute-start.3 = (bf16[32,2,16,128]{3,2,1,0:T(8,128)(2,1)S(1)}, bf16[32,2,16,128]{3,2,1,0:T(8,128)(2,1)S(1)}, u32[]{:S(2)}, u32[]{:S(2)}) collective-permute-start(bf16[32,2,16,128]{3,2,1,0:T(8,128)(2,1)S(1)} %all_gather.3.blk_ref), channel_id=1, source_target_pairs={{0,40},{8,48},{16,56},{24,64},{32,72},{40,80},{48,88},{56,96},{64,... | collective-permute-start | bytes 786440 | tf_op jit(solution)/shard_map/ppermute | solution.py:142
  41.2 0.7 collective-permute-start.4
  41.9 7.7 %collective-permute-start.5 = (bf16[32,2,16,128]{3,2,1,0:T(8,128)(2,1)S(1)}, bf16[32,2,16,128]{3,2,1,0:T(8,128)(2,1)S(1)}, u32[]{:S(2)}, u32[]{:S(2)}) collective-permute-start(bf16[32,2,16,128]{3,2,1,0:T(8,128)(2,1)S(1)} %collective-permute-done.refs_2_), channel_id=1, source_target_pairs={{0,128},{128,0},{1,129},{129,1},{2,130},{130,2},{3,131},{131,3},{4... | collective-permute-start | bytes 786440 | tf_op jit(solution)/shard_map/ppermute | solution.py:143
  49.6 12.2 %collective-permute-done.1.refs_3_ = bf16[32,2,16,128]{3,2,1,0:T(8,128)(2,1)S(1)} collective-permute-done((bf16[32,2,16,128]{3,2,1,0:T(8,128)(2,1)S(1)}, bf16[32,2,16,128]{3,2,1,0:T(8,128)(2,1)S(1)}, u32[]{:S(2)}, u32[]{:S(2)}) %collective-permute-start.1) | collective-permute-done | bytes 262176 | tf_op jit(solution)/shard_map/ppermute | solution.py:142
  61.8 1.9 %collective-permute-start.6 = (bf16[32,2,16,128]{3,2,1,0:T(8,128)(2,1)S(1)}, bf16[32,2,16,128]{3,2,1,0:T(8,128)(2,1)S(1)}, u32[]{:S(2)}, u32[]{:S(2)}) collective-permute-start(bf16[32,2,16,128]{3,2,1,0:T(8,128)(2,1)S(1)} %collective-permute-done.1.refs_3_), channel_id=1, source_target_pairs={{0,128},{128,0},{1,129},{129,1},{2,130},{130,2},{3,131},{131,3},{4... | collective-permute-start | bytes 786440 | tf_op jit(solution)/shard_map/ppermute | solution.py:143
  63.7 0.0 collective-permute-done.2.refs_4_
  63.7 2.4 %collective-permute-start.7 = (bf16[32,2,16,128]{3,2,1,0:T(8,128)(2,1)S(1)}, bf16[32,2,16,128]{3,2,1,0:T(8,128)(2,1)S(1)}, u32[]{:S(2)}, u32[]{:S(2)}) collective-permute-start(bf16[32,2,16,128]{3,2,1,0:T(8,128)(2,1)S(1)} %collective-permute-done.2.refs_4_), channel_id=1, source_target_pairs={{0,128},{128,0},{1,129},{129,1},{2,130},{130,2},{3,131},{131,3},{4... | collective-permute-start | bytes 786440 | tf_op jit(solution)/shard_map/ppermute | solution.py:143
  66.1 1.9 %collective-permute-start.8 = (bf16[32,2,16,128]{3,2,1,0:T(8,128)(2,1)S(1)}, bf16[32,2,16,128]{3,2,1,0:T(8,128)(2,1)S(1)}, u32[]{:S(2)}, u32[]{:S(2)}) collective-permute-start(bf16[32,2,16,128]{3,2,1,0:T(8,128)(2,1)S(1)} %collective-permute-done.3.refs_5_), channel_id=1, source_target_pairs={{0,128},{128,0},{1,129},{129,1},{2,130},{130,2},{3,131},{131,3},{4... | collective-permute-start | bytes 786440 | tf_op jit(solution)/shard_map/ppermute | solution.py:143
  68.1 0.0 collective-permute-done.4.refs_6_
  68.1 2.4 %collective-permute-start.9 = (bf16[32,2,16,128]{3,2,1,0:T(8,128)(2,1)S(1)}, bf16[32,2,16,128]{3,2,1,0:T(8,128)(2,1)S(1)}, u32[]{:S(2)}, u32[]{:S(2)}) collective-permute-start(bf16[32,2,16,128]{3,2,1,0:T(8,128)(2,1)S(1)} %collective-permute-done.4.refs_6_), channel_id=1, source_target_pairs={{0,128},{128,0},{1,129},{129,1},{2,130},{130,2},{3,131},{131,3},{4... | collective-permute-start | bytes 786440 | tf_op jit(solution)/shard_map/ppermute | solution.py:143
  70.5 3.3 %own_block.1 = (f32[2,1,512]{2,1,0:T(1,128)}, f32[2,1,512]{2,1,0:T(1,128)}, f32[2,128,512]{2,1,0:T(8,128)}) custom-call(s32[4]{0:T(128)} %refs_0_.1, bf16[512,256]{1,0:T(8,128)(2,1)} %bitcast.16, bf16[32,2,16,128]{3,2,1,0:T(8,128)(2,1)} %copy-done), custom_call_target="tpu_custom_call" | custom-call | tf_op jit(solution)/shard_map/own_block/pallas_call | solution.py:151
  73.8 0.0 collective-permute-done.6.refs_8_
  73.9 0.6 copy-done.6
  74.5 0.1 copy-done.7
  74.6 0.1 copy-done.8
  74.7 0.1 copy-done.9
  74.8 0.1 copy-done.10
  74.9 6.7 %earlier_blocks.1 = bf16[512,256]{1,0:T(8,128)(2,1)} custom-call(s32[4]{0:T(128)} %refs_0_.1, bf16[512,256]{1,0:T(8,128)(2,1)} %bitcast.17, bf16[32,2,16,128]{3,2,1,0:T(8,128)(2,1)} %copy-done.1, bf16[32,2,16,128]{3,2,1,0:T(8,128)(2,1)} %copy-done.2, bf16[32,2,16,128]{3,2,1,0:T(8,128)(2,1)} %copy-done.3, bf16[32,2,16,128]{3,2,1,0:T(8,128)(2,1)} %copy-done.4, ...), custom_call_target="tpu_custom_call" | custom-call | tf_op jit(solution)/shard_map/earlier_blocks/pallas_call | solution.py:159
  (28 shorter events, 0.1 us)
Async XLA Ops:
  0.0 0.8 copy-start.11
  32.9 37.6 %copy-start = (bf16[32,2,16,128]{3,2,1,0:T(8,128)(2,1)}, bf16[32,2,16,128]{3,2,1,0:T(8,128)(2,1)S(1)}, u32[]{:S(2)}) copy-start(bf16[32,2,16,128]{3,2,1,0:T(8,128)(2,1)S(1)} %all_gather.3.blk_ref) | copy-start | bytes 786436
  32.9 9.1 %collective-permute-start = (bf16[32,2,16,128]{3,2,1,0:T(8,128)(2,1)S(1)}, bf16[32,2,16,128]{3,2,1,0:T(8,128)(2,1)S(1)}, u32[]{:S(2)}, u32[]{:S(2)}) collective-permute-start(bf16[32,2,16,128]{3,2,1,0:T(8,128)(2,1)S(1)} %all_gather.3.blk_ref), channel_id=1, source_target_pairs={{0,8},{8,16},{16,24},{24,32},{32,40},{40,48},{48,56},{56,64},{64,7... | collective-permute-start | bytes 786440 | tf_op jit(solution)/shard_map/ppermute | solution.py:142
  35.8 26.0 %collective-permute-start.1 = (bf16[32,2,16,128]{3,2,1,0:T(8,128)(2,1)S(1)}, bf16[32,2,16,128]{3,2,1,0:T(8,128)(2,1)S(1)}, u32[]{:S(2)}, u32[]{:S(2)}) collective-permute-start(bf16[32,2,16,128]{3,2,1,0:T(8,128)(2,1)S(1)} %all_gather.3.blk_ref), channel_id=1, source_target_pairs={{0,16},{8,24},{16,32},{24,40},{32,48},{40,56},{48,64},{56,72},{64,... | collective-permute-start | bytes 786440 | tf_op jit(solution)/shard_map/ppermute | solution.py:142
  37.1 26.6 %collective-permute-start.2 = (bf16[32,2,16,128]{3,2,1,0:T(8,128)(2,1)S(1)}, bf16[32,2,16,128]{3,2,1,0:T(8,128)(2,1)S(1)}, u32[]{:S(2)}, u32[]{:S(2)}) collective-permute-start(bf16[32,2,16,128]{3,2,1,0:T(8,128)(2,1)S(1)} %all_gather.3.blk_ref), channel_id=1, source_target_pairs={{0,24},{8,32},{16,40},{24,48},{32,56},{40,64},{48,72},{56,80},{64,... | collective-permute-start | bytes 786440 | tf_op jit(solution)/shard_map/ppermute | solution.py:142
  38.4 27.8 %collective-permute-start.3 = (bf16[32,2,16,128]{3,2,1,0:T(8,128)(2,1)S(1)}, bf16[32,2,16,128]{3,2,1,0:T(8,128)(2,1)S(1)}, u32[]{:S(2)}, u32[]{:S(2)}) collective-permute-start(bf16[32,2,16,128]{3,2,1,0:T(8,128)(2,1)S(1)} %all_gather.3.blk_ref), channel_id=1, source_target_pairs={{0,40},{8,48},{16,56},{24,64},{32,72},{40,80},{48,88},{56,96},{64,... | collective-permute-start | bytes 786440 | tf_op jit(solution)/shard_map/ppermute | solution.py:142
  41.2 26.8 %collective-permute-start.4 = (bf16[32,2,16,128]{3,2,1,0:T(8,128)(2,1)S(1)}, bf16[32,2,16,128]{3,2,1,0:T(8,128)(2,1)S(1)}, u32[]{:S(2)}, u32[]{:S(2)}) collective-permute-start(bf16[32,2,16,128]{3,2,1,0:T(8,128)(2,1)S(1)} %all_gather.3.blk_ref), channel_id=1, source_target_pairs={{0,72},{8,80},{16,88},{24,96},{32,104},{40,112},{48,120},{128,208}... | collective-permute-start | bytes 786440 | tf_op jit(solution)/shard_map/ppermute | solution.py:142
  41.9 31.9 %copy-start.1 = (bf16[32,2,16,128]{3,2,1,0:T(8,128)(2,1)}, bf16[32,2,16,128]{3,2,1,0:T(8,128)(2,1)S(1)}, u32[]{:S(2)}) copy-start(bf16[32,2,16,128]{3,2,1,0:T(8,128)(2,1)S(1)} %collective-permute-done.refs_2_) | copy-start | bytes 786436
  41.9 31.9 %collective-permute-start.5 = (bf16[32,2,16,128]{3,2,1,0:T(8,128)(2,1)S(1)}, bf16[32,2,16,128]{3,2,1,0:T(8,128)(2,1)S(1)}, u32[]{:S(2)}, u32[]{:S(2)}) collective-permute-start(bf16[32,2,16,128]{3,2,1,0:T(8,128)(2,1)S(1)} %collective-permute-done.refs_2_), channel_id=1, source_target_pairs={{0,128},{128,0},{1,129},{129,1},{2,130},{130,2},{3,131},{131,3},{4... | collective-permute-start | bytes 786440 | tf_op jit(solution)/shard_map/ppermute | solution.py:143
  61.8 12.0 %copy-start.2 = (bf16[32,2,16,128]{3,2,1,0:T(8,128)(2,1)}, bf16[32,2,16,128]{3,2,1,0:T(8,128)(2,1)S(1)}, u32[]{:S(2)}) copy-start(bf16[32,2,16,128]{3,2,1,0:T(8,128)(2,1)S(1)} %collective-permute-done.1.refs_3_) | copy-start | bytes 786436
  61.8 12.0 %collective-permute-start.6 = (bf16[32,2,16,128]{3,2,1,0:T(8,128)(2,1)S(1)}, bf16[32,2,16,128]{3,2,1,0:T(8,128)(2,1)S(1)}, u32[]{:S(2)}, u32[]{:S(2)}) collective-permute-start(bf16[32,2,16,128]{3,2,1,0:T(8,128)(2,1)S(1)} %collective-permute-done.1.refs_3_), channel_id=1, source_target_pairs={{0,128},{128,0},{1,129},{129,1},{2,130},{130,2},{3,131},{131,3},{4... | collective-permute-start | bytes 786440 | tf_op jit(solution)/shard_map/ppermute | solution.py:143
  63.7 10.2 %copy-start.3 = (bf16[32,2,16,128]{3,2,1,0:T(8,128)(2,1)}, bf16[32,2,16,128]{3,2,1,0:T(8,128)(2,1)S(1)}, u32[]{:S(2)}) copy-start(bf16[32,2,16,128]{3,2,1,0:T(8,128)(2,1)S(1)} %collective-permute-done.2.refs_4_) | copy-start | bytes 786436
  63.7 10.1 %collective-permute-start.7 = (bf16[32,2,16,128]{3,2,1,0:T(8,128)(2,1)S(1)}, bf16[32,2,16,128]{3,2,1,0:T(8,128)(2,1)S(1)}, u32[]{:S(2)}, u32[]{:S(2)}) collective-permute-start(bf16[32,2,16,128]{3,2,1,0:T(8,128)(2,1)S(1)} %collective-permute-done.2.refs_4_), channel_id=1, source_target_pairs={{0,128},{128,0},{1,129},{129,1},{2,130},{130,2},{3,131},{131,3},{4... | collective-permute-start | bytes 786440 | tf_op jit(solution)/shard_map/ppermute | solution.py:143
  66.1 7.8 %copy-start.4 = (bf16[32,2,16,128]{3,2,1,0:T(8,128)(2,1)}, bf16[32,2,16,128]{3,2,1,0:T(8,128)(2,1)S(1)}, u32[]{:S(2)}) copy-start(bf16[32,2,16,128]{3,2,1,0:T(8,128)(2,1)S(1)} %collective-permute-done.3.refs_5_) | copy-start | bytes 786436
  66.1 7.7 %collective-permute-start.8 = (bf16[32,2,16,128]{3,2,1,0:T(8,128)(2,1)S(1)}, bf16[32,2,16,128]{3,2,1,0:T(8,128)(2,1)S(1)}, u32[]{:S(2)}, u32[]{:S(2)}) collective-permute-start(bf16[32,2,16,128]{3,2,1,0:T(8,128)(2,1)S(1)} %collective-permute-done.3.refs_5_), channel_id=1, source_target_pairs={{0,128},{128,0},{1,129},{129,1},{2,130},{130,2},{3,131},{131,3},{4... | collective-permute-start | bytes 786440 | tf_op jit(solution)/shard_map/ppermute | solution.py:143
  68.1 5.8 %copy-start.5 = (bf16[32,2,16,128]{3,2,1,0:T(8,128)(2,1)}, bf16[32,2,16,128]{3,2,1,0:T(8,128)(2,1)S(1)}, u32[]{:S(2)}) copy-start(bf16[32,2,16,128]{3,2,1,0:T(8,128)(2,1)S(1)} %collective-permute-done.4.refs_6_) | copy-start | bytes 786436
  68.1 5.8 %collective-permute-start.9 = (bf16[32,2,16,128]{3,2,1,0:T(8,128)(2,1)S(1)}, bf16[32,2,16,128]{3,2,1,0:T(8,128)(2,1)S(1)}, u32[]{:S(2)}, u32[]{:S(2)}) collective-permute-start(bf16[32,2,16,128]{3,2,1,0:T(8,128)(2,1)S(1)} %collective-permute-done.4.refs_6_), channel_id=1, source_target_pairs={{0,128},{128,0},{1,129},{129,1},{2,130},{130,2},{3,131},{131,3},{4... | collective-permute-start | bytes 786440 | tf_op jit(solution)/shard_map/ppermute | solution.py:143
  73.8 0.7 copy-start.6
  73.8 0.8 copy-start.7
  73.8 0.8 %copy-start.8 = (bf16[32,2,16,128]{3,2,1,0:T(8,128)(2,1)}, bf16[32,2,16,128]{3,2,1,0:T(8,128)(2,1)S(1)}, u32[]{:S(2)}) copy-start(bf16[32,2,16,128]{3,2,1,0:T(8,128)(2,1)S(1)} %collective-permute-done.7.refs_9_) | copy-start | bytes 786436
  73.9 0.9 %copy-start.9 = (bf16[32,2,16,128]{3,2,1,0:T(8,128)(2,1)}, bf16[32,2,16,128]{3,2,1,0:T(8,128)(2,1)S(1)}, u32[]{:S(2)}) copy-start(bf16[32,2,16,128]{3,2,1,0:T(8,128)(2,1)S(1)} %collective-permute-done.8.refs_10_) | copy-start | bytes 786436
  73.9 1.0 %copy-start.10 = (bf16[32,2,16,128]{3,2,1,0:T(8,128)(2,1)}, bf16[32,2,16,128]{3,2,1,0:T(8,128)(2,1)S(1)}, u32[]{:S(2)}) copy-start(bf16[32,2,16,128]{3,2,1,0:T(8,128)(2,1)S(1)} %collective-permute-done.9.refs_11_) | copy-start | bytes 786436

commit v2 on v1

--- a/solution.py
+++ b/solution.py
@@ -83,40 +83,49 @@
     return begin
 
 
-def own_kernel(lengths_ref, q_ref, blk_ref, m_ref, l_ref, acc_ref):
-    block = lax.axis_index("ctx")
-    starts = doc_starts(lengths_ref)
-    m_ref[...] = jnp.full(m_ref.shape, LOW, jnp.float32)
-    l_ref[...] = jnp.zeros(l_ref.shape, jnp.float32)
-    acc_ref[...] = jnp.zeros(acc_ref.shape, jnp.float32)
-    attend_block(
-        q_ref, blk_ref, block, block, starts, (m_ref, l_ref, acc_ref),
-        start_of(block * ROWS, starts), start_of(block * ROWS + ROWS - 1, starts),
-    )
-
-
-def rest_kernel(hops, lengths_ref, q_ref, *refs):
-    blocks = refs[: len(hops)]
-    m_in, l_in, acc_in, out_ref, m_ref, l_ref, acc_ref = refs[len(hops) :]
+def stage_kernel(hops, first, last, lengths_ref, q_ref, *refs):
+    blocks, refs = refs[: len(hops)], refs[len(hops) :]
+    before, refs = ((), refs) if first else (refs[:3], refs[3:])
+    out_ref, refs = (refs[0], refs[1:]) if last else (None, refs)
+    state = refs
+    m_ref, l_ref, acc_ref = state
     block = lax.axis_index("ctx")
     core = lax.axis_index("core")
     starts = doc_starts(lengths_ref)
-    m_ref[...] = m_in[...]
-    l_ref[...] = l_in[...]
-    acc_ref[...] = acc_in[...]
+    if first:
+        m_ref[...] = jnp.full(m_ref.shape, LOW, jnp.float32)
+        l_ref[...] = jnp.zeros(l_ref.shape, jnp.float32)
+        acc_ref[...] = jnp.zeros(acc_ref.shape, jnp.float32)
+    else:
+        for ref, was in zip(state, before):
+            ref[...] = was[...]
+    first_needed = start_of(block * ROWS, starts)
+    last_start = start_of(block * ROWS + ROWS - 1, starts)
     for blk_ref, (k0, k1) in zip(blocks, hops):
-        attend_block(
-            q_ref, blk_ref, block - jnp.where(core == 0, k0, k1), block, starts,
-            (m_ref, l_ref, acc_ref),
-            start_of(block * ROWS, starts), start_of(block * ROWS + ROWS - 1, starts),
-        )
-    for h in range(acc_ref.shape[0]):
-        attended = acc_ref[h] / l_ref[h]
-        out_ref[:, h * HD : (h + 1) * HD] = attended.T.astype(jnp.bfloat16)
+        which = block - (k0 if k0 == k1 else jnp.where(core == 0, k0, k1))
+        attend_block(q_ref, blk_ref, which, block, starts, state, first_needed, last_start)
+    if last:
+        for h in range(acc_ref.shape[0]):
+            attended = acc_ref[h] / l_ref[h]
+            out_ref[:, h * HD : (h + 1) * HD] = attended.T.astype(jnp.bfloat16)
 
 
-def in_vmem(n):
-    return [pl.BlockSpec(memory_space=pltpu.VMEM)] * n
+def attend(lengths, queries, blocks, hops, state, last):
+    rows, width = queries.shape
+    heads = width // HD
+    row = jax.ShapeDtypeStruct((heads, 1, rows), jnp.float32)
+    state_shape = (row, row, jax.ShapeDtypeStruct((heads, HD, rows), jnp.float32))
+    out_shape = jax.ShapeDtypeStruct((rows, width), jnp.bfloat16) if last else state_shape
+    vmem = pl.BlockSpec(memory_space=pltpu.VMEM)
+    return pl.pallas_call(
+        lambda *refs: stage_kernel(hops, not state, last, *refs),
+        out_shape=out_shape,
+        in_specs=[pl.BlockSpec(memory_space=pltpu.SMEM)]
+        + [vmem] * (1 + len(blocks) + len(state)),
+        out_specs=vmem if last else (vmem,) * 3,
+        scratch_shapes=[pltpu.VMEM(s.shape, s.dtype) for s in state_shape] if last else [],
+        name="attend_last" if last else "attend",
+    )(lengths, queries, *blocks, *state)
 
 
 def shards(query_heads, key_cache, value_cache, doc_lengths):
@@ -140,30 +149,28 @@
         pairs = [(b, b + k0) for b in range(blocks - k0)]
         pairs += [(blocks + b, blocks + b + k1) for b in range(blocks - k1)]
         arrived.append(lax.ppermute(own, ("core", "ctx"), pairs))
-    swapped = [lax.ppermute(a, "core", [(0, 1), (1, 0)]) for a in arrived]
+    crossed = [(k1, k0) for k0, k1 in HOPS]
+    swapped = []
 
-    state_shape = (
-        jax.ShapeDtypeStruct((heads, 1, rows), jnp.float32),
-        jax.ShapeDtypeStruct((heads, 1, rows), jnp.float32),
-        jax.ShapeDtypeStruct((heads, HD, rows), jnp.float32),
-    )
-    smem = [pl.BlockSpec(memory_space=pltpu.SMEM)]
-    state = pl.pallas_call(
-        own_kernel,
-        out_shape=state_shape,
-        in_specs=smem + in_vmem(2),
-        out_specs=tuple(in_vmem(3)),
-        name="own_block",
-    )(doc_lengths, queries, own)
-    hops = list(HOPS) + [(k1, k0) for k0, k1 in HOPS]
-    out = pl.pallas_call(
-        lambda *refs: rest_kernel(hops, *refs),
-        out_shape=jax.ShapeDtypeStruct((rows, width), jnp.bfloat16),
-        in_specs=smem + in_vmem(1 + len(hops) + 3),
-        out_specs=in_vmem(1)[0],
-        scratch_shapes=[pltpu.VMEM(s.shape, s.dtype) for s in state_shape],
-        name="earlier_blocks",
-    )(doc_lengths, queries, *arrived, *swapped, *state)
+    def swap(i, state):
+        held, state = lax.optimization_barrier((arrived[i], state))
+        arrived[i] = held
+        swapped.append(lax.ppermute(held, "core", [(0, 1), (1, 0)]))
+        return state
+
+    def step(blocks, hops, state, last=False):
+        return attend(doc_lengths, queries, blocks, hops, state, last)
+
+    state = step([own], [(0, 0)], ())
+    state = swap(0, state)
+    state = swap(1, state)
+    state = step(arrived[:2], HOPS[:2], state)
+    state = swap(2, state)
+    state = swap(3, state)
+    state = step(arrived[2:4] + swapped[:2], HOPS[2:4] + tuple(crossed[:2]), state)
+    state = swap(4, state)
+    state = step(arrived[4:] + swapped[2:4], HOPS[4:] + tuple(crossed[2:4]), state)
+    out = step(swapped[4:], crossed[4:], state, last=True)
     return out.reshape(query_heads.shape)
 
 

time: 82 us -> 92.7 us (1.13)
  Pallas kernels: 9.93 us -> 18.4 us
  starting transfers between devices: 25.3 us -> 22.7 us
  local copies, waits for them, and re-layouts: 1.79 us -> 4.26 us
  waiting for transfers between devices: 12.2 us -> 14.5 us
    pallas_call x2 -> x5, Pallas kernels: 9.93 us -> 18.4 us  [attend(): pl.pallas_call(lambda *refs: stage_kernel(hops, not state, last, *refs),...]
    ppermute x5, starting transfers between devices: 16.3 us -> 13.7 us  [swap(): swapped.append(lax.ppermute(held, 'core', [(0, 1), (1, 0)]))]
    unnamed x26, local copies, waits for them, and re-layouts: 1.75 us -> 4.22 us
    ppermute x5, waiting for transfers between devices: 12.2 us -> 14.5 us  [shards(): arrived.append(lax.ppermute(own, ('core', 'ctx'), pairs))]
  transfers between devices with their start and end apart: 10 -> 10, of which waited for: 1 -> 1; matrix products, arithmetic and copies ran while one was open for 0% -> 0% of each run, Pallas kernels for 4% -> 18%
where the time goes in v2:
time: 92.7 us; the launch traced here: 92.1 us
  blocking collectives  32 us (35%)
  starting transfers between devices  22.7 us (24%)
  Pallas kernels  18.4 us (20%)
  waiting for transfers between devices  14.5 us (16%)
  local copies, waits for them, and re-layouts  4.26 us (5%)
    all_to_all x1, blocking collectives, shards(): lax.all_to_all(send, ('zhi', 'tp'), split_axis=0, concat_axis=0, tiled=True)  26.7 us
    pallas_call x5, Pallas kernels, attend(): pl.pallas_call(lambda *refs: stage_kernel(hops, not state, last, *refs),...  18.4 us
    ppermute x5, waiting for transfers between devices, shards(): arrived.append(lax.ppermute(own, ('core', 'ctx'), pairs))  14.5 us
    ppermute x5, starting transfers between devices, swap(): swapped.append(lax.ppermute(held, 'core', [(0, 1), (1, 0)]))  13.7 us
    ppermute x5, starting transfers between devices, shards(): arrived.append(lax.ppermute(own, ('core', 'ctx'), pairs))  9.01 us
    all_gather x1, blocking collectives, shards(): own = lax.all_gather(half, 'core', axis=0, tiled=True)  5.27 us
    unnamed x26, local copies, waits for them, and re-layouts  4.22 us
  transfers between devices with their start and end apart: 10, of which 1 were waited for; matrix products, arithmetic and copies ran while one was open for 0% of the time, Pallas kernels for 18%

profile of v2, /device:TPU:19, one launch (start us, length us, event | category | flops | bytes accessed | tf_op | source)
XLA Modules:
  0.0 92.1 jit_solution(4828990146746699566)
XLA Ops:
  0.0 0.8 copy.9
  0.9 26.7 %all_to_all.5 = bf16[16,2,16,128]{3,2,1,0:T(8,128)(2,1)S(1)} all-to-all(bf16[16,2,16,128]{3,2,1,0:T(8,128)(2,1)S(1)} %copy.8), channel_id=1, replica_groups=mesh['zhi'=2,'core'=2,'ctx'=16,'tp'=8] {'zhi','tp'}, dimensions={0} | all-to-all | bytes 262144 | tf_op jit(solution)/shard_map/all_to_all | solution.py:144
  27.6 5.3 %all_gather.3.refs_2_ = bf16[32,2,16,128]{3,2,1,0:T(8,128)(2,1)S(1)} all-gather(bf16[16,2,16,128]{3,2,1,0:T(8,128)(2,1)S(1)} %all_to_all.5), channel_id=1, replica_groups=mesh['zhi'=2,'core'=2,'ctx'=16,'tp'=8] {'core'}, dimensions={0}, use_global_device_ids=true | all-gather | bytes 393216 | tf_op jit(solution)/shard_map/all_gather | solution.py:145
  32.9 2.9 %collective-permute-start.2 = (bf16[32,2,16,128]{3,2,1,0:T(8,128)(2,1)S(1)}, bf16[32,2,16,128]{3,2,1,0:T(8,128)(2,1)S(1)}, u32[]{:S(2)}, u32[]{:S(2)}) collective-permute-start(bf16[32,2,16,128]{3,2,1,0:T(8,128)(2,1)S(1)} %all_gather.3.refs_2_), channel_id=1, source_target_pairs={{0,8},{8,16},{16,24},{24,32},{32,40},{40,48},{48,56},{56,64},{64,7... | collective-permute-start | bytes 786440 | tf_op jit(solution)/shard_map/ppermute | solution.py:151
  35.8 1.3 %collective-permute-start.3 = (bf16[32,2,16,128]{3,2,1,0:T(8,128)(2,1)S(1)}, bf16[32,2,16,128]{3,2,1,0:T(8,128)(2,1)S(1)}, u32[]{:S(2)}, u32[]{:S(2)}) collective-permute-start(bf16[32,2,16,128]{3,2,1,0:T(8,128)(2,1)S(1)} %all_gather.3.refs_2_), channel_id=1, source_target_pairs={{0,16},{8,24},{16,32},{24,40},{32,48},{40,56},{48,64},{56,72},{64,... | collective-permute-start | bytes 786440 | tf_op jit(solution)/shard_map/ppermute | solution.py:151
  37.1 1.3 %collective-permute-start.1 = (bf16[32,2,16,128]{3,2,1,0:T(8,128)(2,1)S(1)}, bf16[32,2,16,128]{3,2,1,0:T(8,128)(2,1)S(1)}, u32[]{:S(2)}, u32[]{:S(2)}) collective-permute-start(bf16[32,2,16,128]{3,2,1,0:T(8,128)(2,1)S(1)} %all_gather.3.refs_2_), channel_id=1, source_target_pairs={{0,24},{8,32},{16,40},{24,48},{32,56},{40,64},{48,72},{56,80},{64,... | collective-permute-start | bytes 786440 | tf_op jit(solution)/shard_map/ppermute | solution.py:151
  38.4 2.9 %collective-permute-start.4 = (bf16[32,2,16,128]{3,2,1,0:T(8,128)(2,1)S(1)}, bf16[32,2,16,128]{3,2,1,0:T(8,128)(2,1)S(1)}, u32[]{:S(2)}, u32[]{:S(2)}) collective-permute-start(bf16[32,2,16,128]{3,2,1,0:T(8,128)(2,1)S(1)} %all_gather.3.refs_2_), channel_id=1, source_target_pairs={{0,40},{8,48},{16,56},{24,64},{32,72},{40,80},{48,88},{56,96},{64,... | collective-permute-start | bytes 786440 | tf_op jit(solution)/shard_map/ppermute | solution.py:151
  41.2 3.3 %attend.4 = (f32[2,1,512]{2,1,0:T(1,128)}, f32[2,1,512]{2,1,0:T(1,128)}, f32[2,128,512]{2,1,0:T(8,128)}) custom-call(s32[4]{0:T(128)} %refs_0_.9, bf16[512,256]{1,0:T(8,128)(2,1)} %bitcast.16, bf16[32,2,16,128]{3,2,1,0:T(8,128)(2,1)} %copy-done), custom_call_target="tpu_custom_call" | custom-call | tf_op jit(solution)/shard_map/attend/pallas_call | solution.py:120
  44.5 14.5 %collective-permute-done.3.refs_3_ = bf16[32,2,16,128]{3,2,1,0:T(8,128)(2,1)S(1)} collective-permute-done((bf16[32,2,16,128]{3,2,1,0:T(8,128)(2,1)S(1)}, bf16[32,2,16,128]{3,2,1,0:T(8,128)(2,1)S(1)}, u32[]{:S(2)}, u32[]{:S(2)}) %collective-permute-start.3) | collective-permute-done | bytes 262176 | tf_op jit(solution)/shard_map/ppermute | solution.py:151
  59.0 1.9 %collective-permute-start.6 = (bf16[32,2,16,128]{3,2,1,0:T(8,128)(2,1)S(1)}, bf16[32,2,16,128]{3,2,1,0:T(8,128)(2,1)S(1)}, u32[]{:S(2)}, u32[]{:S(2)}) collective-permute-start(bf16[32,2,16,128]{3,2,1,0:T(8,128)(2,1)S(1)} %collective-permute-done.3.refs_3_), channel_id=1, source_target_pairs={{0,128},{128,0},{1,129},{129,1},{2,130},{130,2},{3,131},{131,3},{4... | collective-permute-start | bytes 786440 | tf_op jit(solution)/shard_map/ppermute | solution.py:158
  60.9 2.4 %collective-permute-start.5 = (bf16[32,2,16,128]{3,2,1,0:T(8,128)(2,1)S(1)}, bf16[32,2,16,128]{3,2,1,0:T(8,128)(2,1)S(1)}, u32[]{:S(2)}, u32[]{:S(2)}) collective-permute-start(bf16[32,2,16,128]{3,2,1,0:T(8,128)(2,1)S(1)} %collective-permute-done.2.refs_2_), channel_id=1, source_target_pairs={{0,128},{128,0},{1,129},{129,1},{2,130},{130,2},{3,131},{131,3},{4... | collective-permute-start | bytes 786440 | tf_op jit(solution)/shard_map/ppermute | solution.py:158
  63.3 0.7 collective-permute-start
  64.0 3.4 %attend.5 = (f32[2,1,512]{2,1,0:T(1,128)}, f32[2,1,512]{2,1,0:T(1,128)}, f32[2,128,512]{2,1,0:T(8,128)}) custom-call(s32[4]{0:T(128)} %refs_0_.9, bf16[512,256]{1,0:T(8,128)(2,1)} %bitcast.17, bf16[32,2,16,128]{3,2,1,0:T(8,128)(2,1)} %copy-done.1, bf16[32,2,16,128]{3,2,1,0:T(8,128)(2,1)} %copy-done.2, f32[2,1,512]{2,1,0:T(1,128)} %get-tuple-element.45.refs_4_, ...), custom_call_target="tpu_custom_call" | custom-call | tf_op jit(solution)/shard_map/attend/pallas_call | solution.py:120
  67.4 3.7 %collective-permute-start.9 = (bf16[32,2,16,128]{3,2,1,0:T(8,128)(2,1)S(1)}, bf16[32,2,16,128]{3,2,1,0:T(8,128)(2,1)S(1)}, u32[]{:S(2)}, u32[]{:S(2)}) collective-permute-start(bf16[32,2,16,128]{3,2,1,0:T(8,128)(2,1)S(1)} %collective-permute-done.4.refs_3_), channel_id=1, source_target_pairs={{0,128},{128,0},{1,129},{129,1},{2,130},{130,2},{3,131},{131,3},{4... | collective-permute-start | bytes 786440 | tf_op jit(solution)/shard_map/ppermute | solution.py:158
  71.1 1.9 %collective-permute-start.8 = (bf16[32,2,16,128]{3,2,1,0:T(8,128)(2,1)S(1)}, bf16[32,2,16,128]{3,2,1,0:T(8,128)(2,1)S(1)}, u32[]{:S(2)}, u32[]{:S(2)}) collective-permute-start(bf16[32,2,16,128]{3,2,1,0:T(8,128)(2,1)S(1)} %collective-permute-done.1.refs_2_), channel_id=1, source_target_pairs={{0,128},{128,0},{1,129},{129,1},{2,130},{130,2},{3,131},{131,3},{4... | collective-permute-start | bytes 786440 | tf_op jit(solution)/shard_map/ppermute | solution.py:158
  73.1 0.7 copy-done.7
  73.7 0.7 copy-done.9
  74.4 4.9 %attend.6 = (f32[2,1,512]{2,1,0:T(1,128)}, f32[2,1,512]{2,1,0:T(1,128)}, f32[2,128,512]{2,1,0:T(8,128)}) custom-call(s32[4]{0:T(128)} %refs_0_.9, bf16[512,256]{1,0:T(8,128)(2,1)} %bitcast.18, bf16[32,2,16,128]{3,2,1,0:T(8,128)(2,1)} %copy-done.4, bf16[32,2,16,128]{3,2,1,0:T(8,128)(2,1)} %copy-done.5, bf16[32,2,16,128]{3,2,1,0:T(8,128)(2,1)} %copy-done.9, ...), custom_call_target="tpu_custom_call" | custom-call | tf_op jit(solution)/shard_map/attend/pallas_call | solution.py:120
  79.3 3.8 %collective-permute-start.7 = (bf16[32,2,16,128]{3,2,1,0:T(8,128)(2,1)S(1)}, bf16[32,2,16,128]{3,2,1,0:T(8,128)(2,1)S(1)}, u32[]{:S(2)}, u32[]{:S(2)}) collective-permute-start(bf16[32,2,16,128]{3,2,1,0:T(8,128)(2,1)S(1)} %collective-permute-done.refs_2_), channel_id=1, source_target_pairs={{0,128},{128,0},{1,129},{129,1},{2,130},{130,2},{3,131},{131,3},{4... | collective-permute-start | bytes 786440 | tf_op jit(solution)/shard_map/ppermute | solution.py:158
  83.1 0.7 copy-done.8
  83.8 0.7 copy-done.10
  84.5 4.8 %attend.7 = (f32[2,1,512]{2,1,0:T(1,128)}, f32[2,1,512]{2,1,0:T(1,128)}, f32[2,128,512]{2,1,0:T(8,128)}) custom-call(s32[4]{0:T(128)} %refs_0_.9, bf16[512,256]{1,0:T(8,128)(2,1)} %bitcast.19, bf16[32,2,16,128]{3,2,1,0:T(8,128)(2,1)} %copy-done.6, bf16[32,2,16,128]{3,2,1,0:T(8,128)(2,1)} %copy-done.10, bf16[32,2,16,128]{3,2,1,0:T(8,128)(2,1)} %copy-done.8, ...), custom_call_target="tpu_custom_call" | custom-call | tf_op jit(solution)/shard_map/attend/pallas_call | solution.py:120
  89.3 0.7 copy-done.3
  90.0 2.1 %attend_last.1 = bf16[512,256]{1,0:T(8,128)(2,1)} custom-call(s32[4]{0:T(128)} %refs_0_.9, bf16[512,256]{1,0:T(8,128)(2,1)} %bitcast.20, bf16[32,2,16,128]{3,2,1,0:T(8,128)(2,1)} %copy-done.3, f32[2,1,512]{2,1,0:T(1,128)} %get-tuple-element.66.refs_3_, f32[2,1,512]{2,1,0:T(1,128)} %get-tuple-element.67.refs_4_, f32[2,128,512]{2,1,0:T(8,128)} %get-tuple-element.68.refs_5_), custom_call_target="tpu_custom_call" | custom-call | tf_op jit(solution)/shard_map/attend_last/pallas_call | solution.py:120
  (31 shorter events, 0.1 us)
Async XLA Ops:
  0.0 0.8 copy-start.11
  32.9 8.4 %copy-start = (bf16[32,2,16,128]{3,2,1,0:T(8,128)(2,1)}, bf16[32,2,16,128]{3,2,1,0:T(8,128)(2,1)S(1)}, u32[]{:S(2)}) copy-start(bf16[32,2,16,128]{3,2,1,0:T(8,128)(2,1)S(1)} %all_gather.3.refs_2_) | copy-start | bytes 786436
  32.9 11.6 %collective-permute-start.2 = (bf16[32,2,16,128]{3,2,1,0:T(8,128)(2,1)S(1)}, bf16[32,2,16,128]{3,2,1,0:T(8,128)(2,1)S(1)}, u32[]{:S(2)}, u32[]{:S(2)}) collective-permute-start(bf16[32,2,16,128]{3,2,1,0:T(8,128)(2,1)S(1)} %all_gather.3.refs_2_), channel_id=1, source_target_pairs={{0,8},{8,16},{16,24},{24,32},{32,40},{40,48},{48,56},{56,64},{64,7... | collective-permute-start | bytes 786440 | tf_op jit(solution)/shard_map/ppermute | solution.py:151
  35.8 23.2 %collective-permute-start.3 = (bf16[32,2,16,128]{3,2,1,0:T(8,128)(2,1)S(1)}, bf16[32,2,16,128]{3,2,1,0:T(8,128)(2,1)S(1)}, u32[]{:S(2)}, u32[]{:S(2)}) collective-permute-start(bf16[32,2,16,128]{3,2,1,0:T(8,128)(2,1)S(1)} %all_gather.3.refs_2_), channel_id=1, source_target_pairs={{0,16},{8,24},{16,32},{24,40},{32,48},{40,56},{48,64},{56,72},{64,... | collective-permute-start | bytes 786440 | tf_op jit(solution)/shard_map/ppermute | solution.py:151
  37.1 30.3 %collective-permute-start.1 = (bf16[32,2,16,128]{3,2,1,0:T(8,128)(2,1)S(1)}, bf16[32,2,16,128]{3,2,1,0:T(8,128)(2,1)S(1)}, u32[]{:S(2)}, u32[]{:S(2)}) collective-permute-start(bf16[32,2,16,128]{3,2,1,0:T(8,128)(2,1)S(1)} %all_gather.3.refs_2_), channel_id=1, source_target_pairs={{0,24},{8,32},{16,40},{24,48},{32,56},{40,64},{48,72},{56,80},{64,... | collective-permute-start | bytes 786440 | tf_op jit(solution)/shard_map/ppermute | solution.py:151
  38.4 29.0 %collective-permute-start.4 = (bf16[32,2,16,128]{3,2,1,0:T(8,128)(2,1)S(1)}, bf16[32,2,16,128]{3,2,1,0:T(8,128)(2,1)S(1)}, u32[]{:S(2)}, u32[]{:S(2)}) collective-permute-start(bf16[32,2,16,128]{3,2,1,0:T(8,128)(2,1)S(1)} %all_gather.3.refs_2_), channel_id=1, source_target_pairs={{0,40},{8,48},{16,56},{24,64},{32,72},{40,80},{48,88},{56,96},{64,... | collective-permute-start | bytes 786440 | tf_op jit(solution)/shard_map/ppermute | solution.py:151
  44.5 19.5 %copy-start.1 = (bf16[32,2,16,128]{3,2,1,0:T(8,128)(2,1)}, bf16[32,2,16,128]{3,2,1,0:T(8,128)(2,1)S(1)}, u32[]{:S(2)}) copy-start(bf16[32,2,16,128]{3,2,1,0:T(8,128)(2,1)S(1)} %collective-permute-done.2.refs_2_) | copy-start | bytes 786436
  59.0 5.0 %copy-start.2 = (bf16[32,2,16,128]{3,2,1,0:T(8,128)(2,1)}, bf16[32,2,16,128]{3,2,1,0:T(8,128)(2,1)S(1)}, u32[]{:S(2)}) copy-start(bf16[32,2,16,128]{3,2,1,0:T(8,128)(2,1)S(1)} %collective-permute-done.3.refs_3_) | copy-start | bytes 786436
  59.0 14.1 %collective-permute-start.6 = (bf16[32,2,16,128]{3,2,1,0:T(8,128)(2,1)S(1)}, bf16[32,2,16,128]{3,2,1,0:T(8,128)(2,1)S(1)}, u32[]{:S(2)}, u32[]{:S(2)}) collective-permute-start(bf16[32,2,16,128]{3,2,1,0:T(8,128)(2,1)S(1)} %collective-permute-done.3.refs_3_), channel_id=1, source_target_pairs={{0,128},{128,0},{1,129},{129,1},{2,130},{130,2},{3,131},{131,3},{4... | collective-permute-start | bytes 786440 | tf_op jit(solution)/shard_map/ppermute | solution.py:158
  60.9 12.2 %collective-permute-start.5 = (bf16[32,2,16,128]{3,2,1,0:T(8,128)(2,1)S(1)}, bf16[32,2,16,128]{3,2,1,0:T(8,128)(2,1)S(1)}, u32[]{:S(2)}, u32[]{:S(2)}) collective-permute-start(bf16[32,2,16,128]{3,2,1,0:T(8,128)(2,1)S(1)} %collective-permute-done.2.refs_2_), channel_id=1, source_target_pairs={{0,128},{128,0},{1,129},{129,1},{2,130},{130,2},{3,131},{131,3},{4... | collective-permute-start | bytes 786440 | tf_op jit(solution)/shard_map/ppermute | solution.py:158
  63.3 16.0 %collective-permute-start = (bf16[32,2,16,128]{3,2,1,0:T(8,128)(2,1)}, bf16[32,2,16,128]{3,2,1,0:T(8,128)(2,1)S(1)}, u32[]{:S(2)}, u32[]{:S(2)}) collective-permute-start(bf16[32,2,16,128]{3,2,1,0:T(8,128)(2,1)} %copy-done), channel_id=1, source_target_pairs={{0,72},{8,80},{16,88},{24,96},{32,104},{40,112},{48,120},{128,208}... | collective-permute-start | bytes 786440 | tf_op jit(solution)/shard_map/ppermute | solution.py:151
  67.3 5.7 %copy-start.4 = (bf16[32,2,16,128]{3,2,1,0:T(8,128)(2,1)}, bf16[32,2,16,128]{3,2,1,0:T(8,128)(2,1)S(1)}, u32[]{:S(2)}) copy-start(bf16[32,2,16,128]{3,2,1,0:T(8,128)(2,1)S(1)} %collective-permute-done.1.refs_2_) | copy-start | bytes 786436
  67.4 5.7 %copy-start.5 = (bf16[32,2,16,128]{3,2,1,0:T(8,128)(2,1)}, bf16[32,2,16,128]{3,2,1,0:T(8,128)(2,1)S(1)}, u32[]{:S(2)}) copy-start(bf16[32,2,16,128]{3,2,1,0:T(8,128)(2,1)S(1)} %collective-permute-done.4.refs_3_) | copy-start | bytes 786436
  67.4 15.7 %collective-permute-start.9 = (bf16[32,2,16,128]{3,2,1,0:T(8,128)(2,1)S(1)}, bf16[32,2,16,128]{3,2,1,0:T(8,128)(2,1)S(1)}, u32[]{:S(2)}, u32[]{:S(2)}) collective-permute-start(bf16[32,2,16,128]{3,2,1,0:T(8,128)(2,1)S(1)} %collective-permute-done.4.refs_3_), channel_id=1, source_target_pairs={{0,128},{128,0},{1,129},{129,1},{2,130},{130,2},{3,131},{131,3},{4... | collective-permute-start | bytes 786440 | tf_op jit(solution)/shard_map/ppermute | solution.py:158
  71.1 12.0 %collective-permute-start.8 = (bf16[32,2,16,128]{3,2,1,0:T(8,128)(2,1)S(1)}, bf16[32,2,16,128]{3,2,1,0:T(8,128)(2,1)S(1)}, u32[]{:S(2)}, u32[]{:S(2)}) collective-permute-start(bf16[32,2,16,128]{3,2,1,0:T(8,128)(2,1)S(1)} %collective-permute-done.1.refs_2_), channel_id=1, source_target_pairs={{0,128},{128,0},{1,129},{129,1},{2,130},{130,2},{3,131},{131,3},{4... | collective-permute-start | bytes 786440 | tf_op jit(solution)/shard_map/ppermute | solution.py:158
  73.0 0.7 copy-start.7
  73.7 0.7 copy-start.9
  79.3 3.8 %copy-start.6 = (bf16[32,2,16,128]{3,2,1,0:T(8,128)(2,1)}, bf16[32,2,16,128]{3,2,1,0:T(8,128)(2,1)S(1)}, u32[]{:S(2)}) copy-start(bf16[32,2,16,128]{3,2,1,0:T(8,128)(2,1)S(1)} %collective-permute-done.refs_2_) | copy-start | bytes 786436
  79.3 10.0 %collective-permute-start.7 = (bf16[32,2,16,128]{3,2,1,0:T(8,128)(2,1)S(1)}, bf16[32,2,16,128]{3,2,1,0:T(8,128)(2,1)S(1)}, u32[]{:S(2)}, u32[]{:S(2)}) collective-permute-start(bf16[32,2,16,128]{3,2,1,0:T(8,128)(2,1)S(1)} %collective-permute-done.refs_2_), channel_id=1, source_target_pairs={{0,128},{128,0},{1,129},{129,1},{2,130},{130,2},{3,131},{131,3},{4... | collective-permute-start | bytes 786440 | tf_op jit(solution)/shard_map/ppermute | solution.py:158
  83.1 0.7 copy-start.8
  83.8 0.7 copy-start.10
  89.3 0.7 copy-start.3

commit v3 on v2

v3 whole, which is shorter than its diff:
```python
import math

import jax
import jax.numpy as jnp
from jax import lax
from jax.experimental import pallas as pl
from jax.experimental.pallas import tpu as pltpu
from jax.sharding import Mesh
from jax.sharding import PartitionSpec as P

HD = 128
NDOC = 4
ROWS = 512
REACH = 5120 // ROWS + 1
LOW = -1e29
HIDDEN = -1e30
STEP = math.log2(math.e) / math.sqrt(HD)


def start_of(position, starts):
    begin = jnp.zeros_like(position)
    for s in starts:
        begin = jnp.where(position >= s, s, begin)
    return begin


def attend_kernel(other, lengths_ref, q_ref, cache_ref, *refs):
    before, refs = (refs[:3], refs[3:]) if other else ((), refs)
    out_ref, refs = (refs[0], refs[1:]) if other else (None, refs)
    m_ref, l_ref, acc_ref, buf_ref, sems = refs
    keys_here = buf_ref.shape[1] * buf_ref.shape[3]
    rows, width = q_ref.shape
    heads = width // HD
    block = lax.axis_index("ctx")
    core = lax.axis_index("core")
    held_by = 1 - core if other else core
    starts = []
    total = 0
    for d in range(NDOC - 1):
        total = total + lengths_ref[d]
        starts.append(total)
    first_needed = start_of(block * rows, starts)
    last_start = start_of(block * rows + rows - 1, starts)
    lowest = jnp.maximum(first_needed // rows, block - REACH + 1)

    def fetch(j):
        return pltpu.make_async_copy(cache_ref.at[j], buf_ref.at[j], sems.at[j])

    def begin_fetch(i, carry):
        fetch(block - i).start()
        return carry

    count = block - lowest + 1
    lax.fori_loop(0, count, begin_fetch, 0)
    if other:
        for ref, was in zip((m_ref, l_ref, acc_ref), before):
            ref[...] = was[...]
    else:
        m_ref[...] = jnp.full(m_ref.shape, LOW, jnp.float32)
        l_ref[...] = jnp.zeros(l_ref.shape, jnp.float32)
        acc_ref[...] = jnp.zeros(acc_ref.shape, jnp.float32)

    def visit(j, masked):
        keys = buf_ref[j, :, 0].reshape(keys_here, HD)
        values = buf_ref[j, :, 1].reshape(keys_here, HD)
        if masked:
            n = lax.broadcasted_iota(jnp.int32, (keys_here, rows), 0)
            key = (n & 127) + (n >> 7) * 256 + held_by * 128 + j * rows
            query = block * rows + lax.broadcasted_iota(jnp.int32, (1, rows), 1)
            allowed = (key <= query) & (key >= start_of(query, starts))
        for h in range(heads):
            scores = lax.dot_general(
                keys,
                q_ref[:, h * HD : (h + 1) * HD],
                (((1,), (1,)), ((), ())),
                preferred_element_type=jnp.float32,
            )
            if masked:
                scores = jnp.where(allowed, scores, HIDDEN)
            old = m_ref[h]
            new = jnp.maximum(old, jnp.max(scores, axis=0, keepdims=True))
            weights = jnp.exp2((scores - new) * STEP)
            rescale = jnp.exp2((old - new) * STEP)
            m_ref[h] = new
            l_ref[h] = l_ref[h] * rescale + jnp.sum(weights, axis=0, keepdims=True)
            acc_ref[h] = acc_ref[h] * rescale + lax.dot_general(
                values,
                weights.astype(jnp.bfloat16),
                (((0,), (0,)), ((), ())),
                preferred_element_type=jnp.float32,
            )

    def step(i, carry):
        j = block - i
        fetch(j).wait()
        whole = (j < block) & (j * rows >= last_start)

        @pl.when(whole)
        def _():
            visit(j, False)

        @pl.when(jnp.logical_not(whole))
        def _():
            visit(j, True)

        return carry

    lax.fori_loop(0, count, step, 0)
    if other:
        for h in range(heads):
            attended = acc_ref[h] / l_ref[h]
            out_ref[:, h * HD : (h + 1) * HD] = attended.T.astype(jnp.bfloat16)


def attend(lengths, queries, cache, state):
    other = bool(state)
    rows, width = queries.shape
    heads = width // HD
    row = jax.ShapeDtypeStruct((heads, 1, rows), jnp.float32)
    state_shape = (row, row, jax.ShapeDtypeStruct((heads, HD, rows), jnp.float32))
    vmem = pl.BlockSpec(memory_space=pltpu.VMEM)
    scratch = [pltpu.VMEM(s.shape, s.dtype) for s in state_shape] if other else []
    return pl.pallas_call(
        lambda *refs: attend_kernel(other, *refs),
        out_shape=jax.ShapeDtypeStruct((rows, width), jnp.bfloat16) if other else state_shape,
        in_specs=[
            pl.BlockSpec(memory_space=pltpu.SMEM),
            vmem,
            pl.BlockSpec(memory_space=pl.ANY),
            *[vmem] * len(state),
        ],
        out_specs=vmem if other else (vmem,) * 3,
        scratch_shapes=scratch
        + [pltpu.VMEM(cache.shape, cache.dtype), pltpu.SemaphoreType.DMA((cache.shape[0],))],
        name="attend_other" if other else "attend_own",
    )(lengths, queries, cache, *state)


def shards(query_heads, key_cache, value_cache, doc_lengths):
    rows, _, width = query_heads.shape
    queries = query_heads.reshape(rows, width)
    part = key_cache.shape[1]
    tp = lax.axis_size("tp")
    blocks = lax.axis_size("ctx")

    def by_head(cache):
        return cache.reshape(part, tp, HD).transpose(1, 0, 2)

    send = jnp.stack((by_head(key_cache), by_head(value_cache)), axis=1)
    send = jnp.concatenate((send, send), axis=0)
    half = lax.all_to_all(send, ("zhi", "tp"), split_axis=0, concat_axis=0, tiled=True)
    copies = jnp.broadcast_to(half[None], (blocks, *half.shape))
    mine = lax.all_to_all(copies, "ctx", split_axis=0, concat_axis=0, tiled=True)
    theirs = lax.ppermute(mine, "core", [(0, 1), (1, 0)])
    state = attend(doc_lengths, queries, mine, ())
    out = attend(doc_lengths, queries, theirs, state)
    return out.reshape(query_heads.shape)


def solution(mesh):
    cut = Mesh(
        mesh.devices.reshape(2, 2, *mesh.devices.shape[1:]), ("zhi", "core", "ctx", "tp")
    )
    cache = P("ctx", ("zhi", "core", "tp"), None)
    heads = P("ctx", "tp", ("zhi", "core"))
    return jax.shard_map(
        shards, mesh=cut, in_specs=(heads, cache, cache, P()), out_specs=heads, check_vma=False
    )
```

time: 92.7 us -> 90.7 us (0.978)
  the two profiles are of different devices: /device:TPU:19 before, /device:TPU:25 now
where the time goes in v3:
time: 90.7 us; the launch traced here: 90.3 us
  blocking collectives  55.7 us (61%)
  Pallas kernels  25.8 us (28%)
  starting transfers between devices  6.71 us (7%)
  local copies, waits for them, and re-layouts  1.94 us (2%)
    all_to_all x1, blocking collectives, shards(): lax.all_to_all(copies, 'ctx', split_axis=0, concat_axis=0, tiled=True)  29 us
    all_to_all x1, blocking collectives, shards(): lax.all_to_all(send, ('zhi', 'tp'), split_axis=0, concat_axis=0, tiled=True)  26.7 us
    pallas_call x2, Pallas kernels, attend(): pl.pallas_call(lambda *refs: attend_kernel(other, *refs), out_shape=jax.S...  25.8 us
    ppermute x1, starting transfers between devices, shards(): theirs = lax.ppermute(mine, 'core', [(0, 1), (1, 0)])  6.71 us
  transfers between devices with their start and end apart: 1, of which 0 were waited for; matrix products, arithmetic and copies ran while one was open for 0% of the time, Pallas kernels for 14%

profile of v3, /device:TPU:25, one launch (start us, length us, event | category | flops | bytes accessed | tf_op | source)
XLA Modules:
  0.0 90.3 jit_solution(4026144535570715745)
XLA Ops:
  0.0 0.8 copy.8
  0.8 0.8 copy.7
  1.6 26.7 %all_to_all.10 = bf16[16,2,16,128]{3,2,1,0:T(8,128)(2,1)S(1)} all-to-all(bf16[16,2,16,128]{3,2,1,0:T(8,128)(2,1)S(1)} %maximum_maximum_fusion), channel_id=1, replica_groups=mesh['zhi'=2,'core'=2,'ctx'=16,'tp'=8] {'zhi','tp'}, dimensions={0} | all-to-all | bytes 262144 | tf_op jit(solution)/shard_map/all_to_all | solution.py:151
  28.3 0.4 broadcast_in_dim.2
  28.7 29.0 %all_to_all.11.refs_2_ = bf16[16,16,2,16,128]{4,3,2,1,0:T(8,128)(2,1)S(1)} all-to-all(bf16[16,16,2,16,128]{4,3,2,1,0:T(8,128)(2,1)S(1)} %broadcast_in_dim.2), channel_id=1, replica_groups=mesh['zhi'=2,'core'=2,'ctx'=16,'tp'=8] {'ctx'}, dimensions={0} | all-to-all | bytes 4194304 | tf_op jit(solution)/shard_map/all_to_all | solution.py:153
  57.7 0.0 copy-start
  57.7 6.7 %collective-permute-start = (bf16[16,16,2,16,128]{4,3,2,1,0:T(8,128)(2,1)S(1)}, bf16[16,16,2,16,128]{4,3,2,1,0:T(8,128)(2,1)}, u32[]{:S(2)}, u32[]{:S(2)}) collective-permute-start(bf16[16,16,2,16,128]{4,3,2,1,0:T(8,128)(2,1)S(1)} %all_to_all.11.refs_2_), channel_id=1, source_target_pairs={{0,128},{128,0},{1,129},{129,1},{2,130},{130,2},{3,131},{131,3},{4... | collective-permute-start | bytes 6291464 | tf_op jit(solution)/shard_map/ppermute | solution.py:154
  64.4 0.0 copy-done
  64.4 12.8 %attend_own.1 = (f32[2,1,512]{2,1,0:T(1,128)}, f32[2,1,512]{2,1,0:T(1,128)}, f32[2,128,512]{2,1,0:T(8,128)}) custom-call(s32[4]{0:T(128)} %refs_0_.3, bf16[512,256]{1,0:T(8,128)(2,1)} %bitcast.16, bf16[16,16,2,16,128]{4,3,2,1,0:T(8,128)(2,1)} %copy-done), custom_call_target="tpu_custom_call" | custom-call | tf_op jit(solution)/shard_map/attend_own/pallas_call | solution.py:123
  77.2 0.0 collective-permute-done.refs_2_
  77.2 13.1 %attend_other.1 = bf16[512,256]{1,0:T(8,128)(2,1)} custom-call(s32[4]{0:T(128)} %refs_0_.3, bf16[512,256]{1,0:T(8,128)(2,1)} %bitcast.17, bf16[16,16,2,16,128]{4,3,2,1,0:T(8,128)(2,1)} %collective-permute-done.refs_2_, f32[2,1,512]{2,1,0:T(1,128)} %get-tuple-element.8.refs_3_, f32[2,1,512]{2,1,0:T(1,128)} %get-tuple-element.9.refs_4_, ...), custom_call_target="tpu_custom_call" | custom-call | tf_op jit(solution)/shard_map/attend_other/pallas_call | solution.py:123
  (2 shorter events, 0.0 us)
Async XLA Ops:
  57.7 6.7 %copy-start = (bf16[16,16,2,16,128]{4,3,2,1,0:T(8,128)(2,1)}, bf16[16,16,2,16,128]{4,3,2,1,0:T(8,128)(2,1)S(1)}, u32[]{:S(2)}) copy-start(bf16[16,16,2,16,128]{4,3,2,1,0:T(8,128)(2,1)S(1)} %all_to_all.11.refs_2_) | copy-start | bytes 6291460
  57.7 19.5 %collective-permute-start = (bf16[16,16,2,16,128]{4,3,2,1,0:T(8,128)(2,1)S(1)}, bf16[16,16,2,16,128]{4,3,2,1,0:T(8,128)(2,1)}, u32[]{:S(2)}, u32[]{:S(2)}) collective-permute-start(bf16[16,16,2,16,128]{4,3,2,1,0:T(8,128)(2,1)S(1)} %all_to_all.11.refs_2_), channel_id=1, source_target_pairs={{0,128},{128,0},{1,129},{129,1},{2,130},{130,2},{3,131},{131,3},{4... | collective-permute-start | bytes 6291464 | tf_op jit(solution)/shard_map/ppermute | solution.py:154

commit v4 on v1

v4 whole, which is shorter than its diff:
```python
import math

import jax
import jax.numpy as jnp
from jax import lax
from jax.experimental import pallas as pl
from jax.experimental.pallas import tpu as pltpu
from jax.sharding import Mesh
from jax.sharding import PartitionSpec as P

HD = 128
NDOC = 4
HIDDEN = -1e30
NEVER = 1e30
ROOM = 2.0**60
STEP = math.log2(math.e) / math.sqrt(HD)
HOPS = ((1, 4), (2, 8), (3, 7), (5, 6), (9, 10))


def doc_starts(lengths_ref):
    starts = []
    total = 0
    for d in range(NDOC - 1):
        total = total + lengths_ref[d]
        starts.append(total)
    return starts


def start_of(position, starts):
    begin = jnp.zeros_like(position)
    for s in starts:
        begin = jnp.where(position >= s, s, begin)
    return begin


def key_rows(shape):
    n = lax.broadcasted_iota(jnp.int32, shape, 0)
    return (n & 127) + ((n >> 7) & 1) * 256 + (n >> 8) * 128


def stack_heads(q_ref, stacked_ref):
    rows, width = q_ref.shape
    for h in range(width // HD):
        stacked_ref[h * rows : (h + 1) * rows] = q_ref[:, h * HD : (h + 1) * HD]


def score(keys, queries):
    return lax.dot_general(
        keys, queries, (((1,), (1,)), ((), ())), preferred_element_type=jnp.float32
    )


def mix(values, weights):
    return lax.dot_general(
        values,
        weights.astype(jnp.bfloat16),
        (((0,), (0,)), ((), ())),
        preferred_element_type=jnp.float32,
    )


def fold(weights):
    n, width = weights.shape
    return jnp.sum(weights.reshape(n // 8, 8, width), axis=0)


def own_kernel(lengths_ref, q_ref, blk_ref, m_ref, l_ref, acc_ref):
    rows, width = q_ref.shape
    block = lax.axis_index("ctx")
    starts = doc_starts(lengths_ref)
    keys = blk_ref[:, 0].reshape(rows, HD)
    values = blk_ref[:, 1].reshape(rows, HD)
    key = key_rows((rows, rows)) + block * rows
    query = block * rows + lax.broadcasted_iota(jnp.int32, (1, rows), 1)
    allowed = (key <= query) & (key >= start_of(query, starts))
    for h in range(width // HD):
        at = slice(h * rows, (h + 1) * rows)
        scores = jnp.where(allowed, score(keys, q_ref[:, h * HD : (h + 1) * HD]), HIDDEN)
        top = jnp.max(scores, axis=0, keepdims=True)
        weights = jnp.exp2((scores - top) * STEP)
        m_ref[:, at] = top
        l_ref[:, at] = fold(weights)
        acc_ref[:, at] = mix(values, weights)


def earlier_kernel(lengths_ref, q_ref, m_in, l_in, acc_in, *refs):
    pieces, refs = refs[: len(HOPS)], refs[len(HOPS) :]
    out_ref, stacked_ref, m_ref, l_ref, acc_ref, buf_ref, sems = refs
    rows, width = q_ref.shape
    heads = width // HD
    block = lax.axis_index("ctx")
    starts = doc_starts(lengths_ref)
    count = block - start_of(block * rows, starts) // rows
    part = buf_ref.shape[1]

    for piece, hops in zip(pieces, HOPS):
        for c, k in enumerate(hops):

            @pl.when(k <= count)
            def _():
                pltpu.make_async_copy(
                    piece.at[c * part : (c + 1) * part], buf_ref.at[k - 1], sems.at[k - 1]
                ).start()

    stack_heads(q_ref, stacked_ref)
    l_ref[...] = l_in[...]
    acc_ref[...] = acc_in[...]
    query = block * rows + lax.broadcasted_iota(jnp.int32, (1, rows), 1)
    begin = jnp.concatenate([start_of(query, starts)] * heads, axis=1)

    def load(i):
        keys = buf_ref[i, :, 0].reshape(rows, HD)
        values = buf_ref[i, :, 1].reshape(rows, HD)
        return keys, values, (block - 1 - i) * rows

    def step(i, carry):
        pltpu.make_async_copy(pieces[0].at[0:part], buf_ref.at[i], sems.at[i]).wait()
        keys, values, base = load(i)
        cut = False
        for s in starts:
            cut = cut | ((s > base) & (s < base + rows))

        @pl.when(jnp.logical_not(cut))
        def _():
            top = jnp.where(begin <= base, m_in[...], NEVER)
            weights = jnp.exp2((score(keys, stacked_ref[...]) - top) * STEP)
            l_ref[...] += fold(weights)
            acc_ref[...] += mix(values, weights)

        @pl.when(cut)
        def _():
            key = key_rows((rows, rows)) + base
            for h in range(heads):
                at = slice(h * rows, (h + 1) * rows)
                scores = score(keys, stacked_ref[at])
                weights = jnp.exp2((scores - m_in[:, at]) * STEP)
                weights = jnp.where(key >= begin[:, at], weights, 0.0)
                l_ref[:, at] += fold(weights)
                acc_ref[:, at] += mix(values, weights)

        return carry

    lax.fori_loop(0, count, step, 0)

    fits = jnp.sum(l_ref[...], axis=0, keepdims=True) < ROOM

    @pl.when(jnp.min(fits.astype(jnp.float32)) < 0.5)
    def _():
        m_ref[...] = m_in[...]
        l_ref[...] = l_in[...]
        acc_ref[...] = acc_in[...]

        def again(i, carry):
            keys, values, base = load(i)
            key = key_rows((rows, rows)) + base
            for h in range(heads):
                at = slice(h * rows, (h + 1) * rows)
                scores = score(keys, stacked_ref[at])
                scores = jnp.where(key >= begin[:, at], scores, HIDDEN)
                old = m_ref[:, at]
                top = jnp.maximum(old, jnp.max(scores, axis=0, keepdims=True))
                weights = jnp.exp2((scores - top) * STEP)
                shrink = jnp.exp2((old - top) * STEP)
                m_ref[:, at] = top
                l_ref[:, at] = l_ref[:, at] * shrink + fold(weights)
                acc_ref[:, at] = acc_ref[:, at] * shrink + mix(values, weights)
            return carry

        lax.fori_loop(0, count, again, 0)

    total = jnp.sum(l_ref[...], axis=0, keepdims=True)
    for h in range(heads):
        at = slice(h * rows, (h + 1) * rows)
        attended = acc_ref[:, at] / total[:, at]
        out_ref[:, h * HD : (h + 1) * HD] = attended.T.astype(jnp.bfloat16)


def attend_own(lengths, queries, own):
    rows, width = queries.shape
    columns = rows * (width // HD)
    vmem = pl.BlockSpec(memory_space=pltpu.VMEM)
    return pl.pallas_call(
        own_kernel,
        out_shape=tuple(
            jax.ShapeDtypeStruct((n, columns), jnp.float32) for n in (1, 8, HD)
        ),
        in_specs=[pl.BlockSpec(memory_space=pltpu.SMEM), vmem, vmem],
        out_specs=(vmem,) * 3,
        name="attend_own",
    )(lengths, queries, own)


def attend_earlier(lengths, queries, state, pieces):
    rows, width = queries.shape
    columns = rows * (width // HD)
    shape = pieces[0].shape
    count = 2 * len(pieces)
    vmem = pl.BlockSpec(memory_space=pltpu.VMEM)
    return pl.pallas_call(
        earlier_kernel,
        out_shape=jax.ShapeDtypeStruct((rows, width), jnp.bfloat16),
        in_specs=[pl.BlockSpec(memory_space=pltpu.SMEM)]
        + [vmem] * 4
        + [pl.BlockSpec(memory_space=pl.ANY)] * len(pieces),
        out_specs=vmem,
        scratch_shapes=[pltpu.VMEM((columns, HD), jnp.bfloat16)]
        + [pltpu.VMEM((n, columns), jnp.float32) for n in (1, 8, HD)]
        + [
            pltpu.VMEM((count, shape[0] // 2, *shape[1:]), jnp.bfloat16),
            pltpu.SemaphoreType.DMA((count,)),
        ],
        name="attend_earlier",
    )(lengths, queries, *state, *pieces)


def shards(query_heads, key_cache, value_cache, doc_lengths):
    rows, _, width = query_heads.shape
    queries = query_heads.reshape(rows, width)
    part = key_cache.shape[1]
    tp = lax.axis_size("tp")
    blocks = lax.axis_size("ctx")

    def by_head(cache):
        return cache.reshape(part, tp, HD).transpose(1, 0, 2)

    send = jnp.stack((by_head(key_cache), by_head(value_cache)), axis=1)
    send = jnp.concatenate((send, send), axis=0)
    half = lax.all_to_all(send, ("zhi", "tp"), split_axis=0, concat_axis=0, tiled=True)
    own = lax.all_gather(half, "core", axis=0, tiled=True)

    arrived = []
    for k0, k1 in HOPS:
        pairs = [(b, b + k0) for b in range(blocks - k0)]
        pairs += [(blocks + b, blocks + b + k1) for b in range(blocks - k1)]
        arrived.append(lax.ppermute(own, ("core", "ctx"), pairs))
    state = attend_own(doc_lengths, queries, own)
    pieces = []
    token = state
    for a in arrived:
        a, token = lax.optimization_barrier((a, token))
        both = lax.all_gather(a, "core", axis=0, tiled=True)
        pieces.append(both)
        token = both
    out = attend_earlier(doc_lengths, queries, state, pieces)
    return out.reshape(query_heads.shape)


def solution(mesh):
    cut = Mesh(
        mesh.devices.reshape(2, 2, *mesh.devices.shape[1:]), ("zhi", "core", "ctx", "tp")
    )
    cache = P("ctx", ("zhi", "core", "tp"), None)
    heads = P("ctx", "tp", ("zhi", "core"))
    return jax.shard_map(
        shards, mesh=cut, in_specs=(heads, cache, cache, P()), out_specs=heads, check_vma=False
    )
```

time: 82 us -> 77.3 us (0.943)
  starting transfers between devices: 25.3 us -> 9.63 us
  blocking collectives: 32 us -> 47.6 us
  waiting for transfers between devices: 12.2 us -> 8.47 us
  local copies, waits for them, and re-layouts: 1.79 us -> 0.82 us
    ppermute x5 -> x0, starting transfers between devices: 16.3 us -> none  [shards(): swapped = [lax.ppermute(a, 'core', [(0, 1), (1, 0)]) for a in arrived]]
    all_gather x0 -> x5, blocking collectives: none -> 15.6 us  [shards(): both = lax.all_gather(a, 'core', axis=0, tiled=True)]
    ppermute x5, waiting for transfers between devices: 12.2 us -> 8.47 us  [shards(): arrived.append(lax.ppermute(own, ('core', 'ctx'), pairs))]
    unnamed x26 -> x6, local copies, waits for them, and re-layouts: 1.75 us -> 0.79 us
  transfers between devices with their start and end apart: 10 -> 5, of which waited for: 1 -> 1; matrix products, arithmetic and copies ran while one was open for 0% -> 0% of each run, Pallas kernels for 4% -> 4%
where the time goes in v4:
time: 77.3 us; the launch traced here: 76.9 us
  blocking collectives  47.6 us (62%)
  Pallas kernels  10.2 us (13%)
  starting transfers between devices  9.63 us (12%)
  waiting for transfers between devices  8.47 us (11%)
  local copies, waits for them, and re-layouts  0.82 us (1%)
    all_to_all x1, blocking collectives, shards(): lax.all_to_all(send, ('zhi', 'tp'), split_axis=0, concat_axis=0, tiled=True)  26.7 us
    all_gather x5, blocking collectives, shards(): both = lax.all_gather(a, 'core', axis=0, tiled=True)  15.6 us
    ppermute x5, starting transfers between devices, shards(): arrived.append(lax.ppermute(own, ('core', 'ctx'), pairs))  9.63 us
    ppermute x5, waiting for transfers between devices, shards(): arrived.append(lax.ppermute(own, ('core', 'ctx'), pairs))  8.47 us
    pallas_call x1, Pallas kernels, attend_earlier(): pl.pallas_call(earlier_kernel, out_shape=jax.ShapeDtypeStruct((rows, widt...  7.03 us
    all_gather x1, blocking collectives, shards(): own = lax.all_gather(half, 'core', axis=0, tiled=True)  5.27 us
    pallas_call x1, Pallas kernels, attend_own(): pl.pallas_call(own_kernel, out_shape=tuple((jax.ShapeDtypeStruct((n, colu...  3.17 us
  transfers between devices with their start and end apart: 5, of which 1 were waited for; matrix products, arithmetic and copies ran while one was open for 0% of the time, Pallas kernels for 4%

profile of v4, /device:TPU:19, one launch (start us, length us, event | category | flops | bytes accessed | tf_op | source)
XLA Modules:
  0.0 76.9 jit_solution(5694357150032834008)
XLA Ops:
  0.0 0.0 copy-start.1
  0.0 0.8 %copy.9 = bf16[2,8,8,128]{3,2,1,0:T(8,128)(2,1)S(1)} copy(bf16[2,8,8,128]{3,1,2,0:T(8,128)(2,1)} %bitcast.20) | data formatting | bytes 65536
  0.8 0.0 copy-done.1
  0.9 26.7 %all_to_all.5 = bf16[16,2,16,128]{3,2,1,0:T(8,128)(2,1)S(1)} all-to-all(bf16[16,2,16,128]{3,2,1,0:T(8,128)(2,1)S(1)} %copy.8), channel_id=1, replica_groups=mesh['zhi'=2,'core'=2,'ctx'=16,'tp'=8] {'zhi','tp'}, dimensions={0} | all-to-all | bytes 262144 | tf_op jit(solution)/shard_map/all_to_all | solution.py:228
  27.6 5.3 %all_gather.18.blk_ref = bf16[32,2,16,128]{3,2,1,0:T(8,128)(2,1)S(1)} all-gather(bf16[16,2,16,128]{3,2,1,0:T(8,128)(2,1)S(1)} %all_to_all.5), channel_id=1, replica_groups=mesh['zhi'=2,'core'=2,'ctx'=16,'tp'=8] {'core'}, dimensions={0}, use_global_device_ids=true | all-gather | bytes 393216 | tf_op jit(solution)/shard_map/all_gather | solution.py:229
  32.9 0.0 copy-start
  32.9 2.9 %collective-permute-start = (bf16[32,2,16,128]{3,2,1,0:T(8,128)(2,1)S(1)}, bf16[32,2,16,128]{3,2,1,0:T(8,128)(2,1)S(1)}, u32[]{:S(2)}, u32[]{:S(2)}) collective-permute-start(bf16[32,2,16,128]{3,2,1,0:T(8,128)(2,1)S(1)} %all_gather.18.blk_ref), channel_id=1, source_target_pairs={{0,8},{8,16},{16,24},{24,32},{32,40},{40,48},{48,56},{56,64},{64,7... | collective-permute-start | bytes 786440 | tf_op jit(solution)/shard_map/ppermute | solution.py:235
  35.8 1.3 %collective-permute-start.1 = (bf16[32,2,16,128]{3,2,1,0:T(8,128)(2,1)S(1)}, bf16[32,2,16,128]{3,2,1,0:T(8,128)(2,1)S(1)}, u32[]{:S(2)}, u32[]{:S(2)}) collective-permute-start(bf16[32,2,16,128]{3,2,1,0:T(8,128)(2,1)S(1)} %all_gather.18.blk_ref), channel_id=1, source_target_pairs={{0,16},{8,24},{16,32},{24,40},{32,48},{40,56},{48,64},{56,72},{64,... | collective-permute-start | bytes 786440 | tf_op jit(solution)/shard_map/ppermute | solution.py:235
  37.1 0.7 collective-permute-start.4
  37.7 3.5 %collective-permute-start.3 = (bf16[32,2,16,128]{3,2,1,0:T(8,128)(2,1)S(1)}, bf16[32,2,16,128]{3,2,1,0:T(8,128)(2,1)S(1)}, u32[]{:S(2)}, u32[]{:S(2)}) collective-permute-start(bf16[32,2,16,128]{3,2,1,0:T(8,128)(2,1)S(1)} %all_gather.18.blk_ref), channel_id=1, source_target_pairs={{0,40},{8,48},{16,56},{24,64},{32,72},{40,80},{48,88},{56,96},{64,... | collective-permute-start | bytes 786440 | tf_op jit(solution)/shard_map/ppermute | solution.py:235
  41.2 1.3 %collective-permute-start.2 = (bf16[32,2,16,128]{3,2,1,0:T(8,128)(2,1)S(1)}, bf16[32,2,16,128]{3,2,1,0:T(8,128)(2,1)S(1)}, u32[]{:S(2)}, u32[]{:S(2)}) collective-permute-start(bf16[32,2,16,128]{3,2,1,0:T(8,128)(2,1)S(1)} %all_gather.18.blk_ref), channel_id=1, source_target_pairs={{0,24},{8,32},{16,40},{24,48},{32,56},{40,64},{48,72},{56,80},{64,... | collective-permute-start | bytes 786440 | tf_op jit(solution)/shard_map/ppermute | solution.py:235
  42.5 0.0 copy-done
  42.5 3.2 %attend_own.1 = (f32[1,1024]{1,0:T(1,128)}, f32[8,1024]{1,0:T(8,128)}, f32[128,1024]{1,0:T(8,128)}) custom-call(s32[4]{0:T(128)} %lengths_ref.3, bf16[512,256]{1,0:T(8,128)(2,1)} %bitcast.16, bf16[32,2,16,128]{3,2,1,0:T(8,128)(2,1)} %copy-done), custom_call_target="tpu_custom_call" | custom-call | tf_op jit(solution)/shard_map/attend_own/pallas_call | solution.py:182
  45.7 0.0 collective-permute-done
  45.7 6.4 %all_gather.19.refs_0_ = bf16[64,2,16,128]{3,2,1,0:T(8,128)(2,1)} all-gather(bf16[32,2,16,128]{3,2,1,0:T(8,128)(2,1)S(1)} %collective-permute-done), channel_id=1, replica_groups=mesh['zhi'=2,'core'=2,'ctx'=16,'tp'=8] {'core'}, dimensions={0}, use_global_device_ids=true | all-gather | bytes 786432 | tf_op jit(solution)/shard_map/all_gather | solution.py:241
  52.1 0.0 collective-permute-done.1
  52.1 2.3 %all_gather.20.refs_1_ = bf16[64,2,16,128]{3,2,1,0:T(8,128)(2,1)} all-gather(bf16[32,2,16,128]{3,2,1,0:T(8,128)(2,1)S(1)} %collective-permute-done.1), channel_id=1, replica_groups=mesh['zhi'=2,'core'=2,'ctx'=16,'tp'=8] {'core'}, dimensions={0}, use_global_device_ids=true | all-gather | bytes 786432 | tf_op jit(solution)/shard_map/all_gather | solution.py:241
  54.5 8.5 %collective-permute-done.2 = bf16[32,2,16,128]{3,2,1,0:T(8,128)(2,1)S(1)} collective-permute-done((bf16[32,2,16,128]{3,2,1,0:T(8,128)(2,1)S(1)}, bf16[32,2,16,128]{3,2,1,0:T(8,128)(2,1)S(1)}, u32[]{:S(2)}, u32[]{:S(2)}) %collective-permute-start.2) | collective-permute-done | bytes 262176 | tf_op jit(solution)/shard_map/ppermute | solution.py:235
  62.9 2.3 %all_gather.21.refs_2_ = bf16[64,2,16,128]{3,2,1,0:T(8,128)(2,1)} all-gather(bf16[32,2,16,128]{3,2,1,0:T(8,128)(2,1)S(1)} %collective-permute-done.2), channel_id=1, replica_groups=mesh['zhi'=2,'core'=2,'ctx'=16,'tp'=8] {'core'}, dimensions={0}, use_global_device_ids=true | all-gather | bytes 786432 | tf_op jit(solution)/shard_map/all_gather | solution.py:241
  65.2 0.0 collective-permute-done.3
  65.2 2.3 %all_gather.22.refs_3_ = bf16[64,2,16,128]{3,2,1,0:T(8,128)(2,1)} all-gather(bf16[32,2,16,128]{3,2,1,0:T(8,128)(2,1)S(1)} %collective-permute-done.3), channel_id=1, replica_groups=mesh['zhi'=2,'core'=2,'ctx'=16,'tp'=8] {'core'}, dimensions={0}, use_global_device_ids=true | all-gather | bytes 786432 | tf_op jit(solution)/shard_map/all_gather | solution.py:241
  67.5 0.0 collective-permute-done.4
  67.5 2.3 %all_gather.23.refs_4_ = bf16[64,2,16,128]{3,2,1,0:T(8,128)(2,1)} all-gather(bf16[32,2,16,128]{3,2,1,0:T(8,128)(2,1)S(1)} %collective-permute-done.4), channel_id=1, replica_groups=mesh['zhi'=2,'core'=2,'ctx'=16,'tp'=8] {'core'}, dimensions={0}, use_global_device_ids=true | all-gather | bytes 786432 | tf_op jit(solution)/shard_map/all_gather | solution.py:241
  69.8 7.0 %attend_earlier.1 = bf16[512,256]{1,0:T(8,128)(2,1)} custom-call(s32[4]{0:T(128)} %lengths_ref.3, bf16[512,256]{1,0:T(8,128)(2,1)} %bitcast.17, f32[1,1024]{1,0:T(1,128)} %get-tuple-element.13.m_in, f32[8,1024]{1,0:T(8,128)} %get-tuple-element.14.l_in, f32[128,1024]{1,0:T(8,128)} %get-tuple-element.15.acc_in, bf16[64,2,16,128]{3,2,1,0:T(8,128)(2,1)} %all_gather.19.refs_0_, ...), custom_call_target="tpu_custom_call" | custom-call | tf_op jit(solution)/shard_map/attend_earlier/pallas_call | solution.py:199
  (3 shorter events, 0.1 us)
Async XLA Ops:
  0.0 0.8 %copy-start.1 = (bf16[1,16,1024]{2,1,0:T(8,128)(2,1)S(1)}, bf16[1,16,1024]{2,1,0:T(8,128)(2,1)}, u32[]{:S(2)}) copy-start(bf16[1,16,1024]{2,1,0:T(8,128)(2,1)} %param.6) | copy-start | bytes 98308
  32.9 9.7 %copy-start = (bf16[32,2,16,128]{3,2,1,0:T(8,128)(2,1)}, bf16[32,2,16,128]{3,2,1,0:T(8,128)(2,1)S(1)}, u32[]{:S(2)}) copy-start(bf16[32,2,16,128]{3,2,1,0:T(8,128)(2,1)S(1)} %all_gather.18.blk_ref) | copy-start | bytes 786436
  32.9 12.9 %collective-permute-start = (bf16[32,2,16,128]{3,2,1,0:T(8,128)(2,1)S(1)}, bf16[32,2,16,128]{3,2,1,0:T(8,128)(2,1)S(1)}, u32[]{:S(2)}, u32[]{:S(2)}) collective-permute-start(bf16[32,2,16,128]{3,2,1,0:T(8,128)(2,1)S(1)} %all_gather.18.blk_ref), channel_id=1, source_target_pairs={{0,8},{8,16},{16,24},{24,32},{32,40},{40,48},{48,56},{56,64},{64,7... | collective-permute-start | bytes 786440 | tf_op jit(solution)/shard_map/ppermute | solution.py:235
  35.8 16.4 %collective-permute-start.1 = (bf16[32,2,16,128]{3,2,1,0:T(8,128)(2,1)S(1)}, bf16[32,2,16,128]{3,2,1,0:T(8,128)(2,1)S(1)}, u32[]{:S(2)}, u32[]{:S(2)}) collective-permute-start(bf16[32,2,16,128]{3,2,1,0:T(8,128)(2,1)S(1)} %all_gather.18.blk_ref), channel_id=1, source_target_pairs={{0,16},{8,24},{16,32},{24,40},{32,48},{40,56},{48,64},{56,72},{64,... | collective-permute-start | bytes 786440 | tf_op jit(solution)/shard_map/ppermute | solution.py:235
  37.1 30.5 %collective-permute-start.4 = (bf16[32,2,16,128]{3,2,1,0:T(8,128)(2,1)S(1)}, bf16[32,2,16,128]{3,2,1,0:T(8,128)(2,1)S(1)}, u32[]{:S(2)}, u32[]{:S(2)}) collective-permute-start(bf16[32,2,16,128]{3,2,1,0:T(8,128)(2,1)S(1)} %all_gather.18.blk_ref), channel_id=1, source_target_pairs={{0,72},{8,80},{16,88},{24,96},{32,104},{40,112},{48,120},{128,208}... | collective-permute-start | bytes 786440 | tf_op jit(solution)/shard_map/ppermute | solution.py:235
  37.7 27.5 %collective-permute-start.3 = (bf16[32,2,16,128]{3,2,1,0:T(8,128)(2,1)S(1)}, bf16[32,2,16,128]{3,2,1,0:T(8,128)(2,1)S(1)}, u32[]{:S(2)}, u32[]{:S(2)}) collective-permute-start(bf16[32,2,16,128]{3,2,1,0:T(8,128)(2,1)S(1)} %all_gather.18.blk_ref), channel_id=1, source_target_pairs={{0,40},{8,48},{16,56},{24,64},{32,72},{40,80},{48,88},{56,96},{64,... | collective-permute-start | bytes 786440 | tf_op jit(solution)/shard_map/ppermute | solution.py:235
  41.2 21.7 %collective-permute-start.2 = (bf16[32,2,16,128]{3,2,1,0:T(8,128)(2,1)S(1)}, bf16[32,2,16,128]{3,2,1,0:T(8,128)(2,1)S(1)}, u32[]{:S(2)}, u32[]{:S(2)}) collective-permute-start(bf16[32,2,16,128]{3,2,1,0:T(8,128)(2,1)S(1)} %all_gather.18.blk_ref), channel_id=1, source_target_pairs={{0,24},{8,32},{16,40},{24,48},{32,56},{40,64},{48,72},{56,80},{64,... | collective-permute-start | bytes 786440 | tf_op jit(solution)/shard_map/ppermute | solution.py:235

commit v5 on v4

--- a/solution.py
+++ b/solution.py
@@ -15,6 +15,7 @@
 ROOM = 2.0**60
 STEP = math.log2(math.e) / math.sqrt(HD)
 HOPS = ((1, 4), (2, 8), (3, 7), (5, 6), (9, 10))
+ORDER = (0, 1, 4, 3, 2)
 
 
 def doc_starts(lengths_ref):
@@ -234,13 +235,11 @@
         pairs += [(blocks + b, blocks + b + k1) for b in range(blocks - k1)]
         arrived.append(lax.ppermute(own, ("core", "ctx"), pairs))
     state = attend_own(doc_lengths, queries, own)
-    pieces = []
+    pieces = list(arrived)
     token = state
-    for a in arrived:
-        a, token = lax.optimization_barrier((a, token))
-        both = lax.all_gather(a, "core", axis=0, tiled=True)
-        pieces.append(both)
-        token = both
+    for i in ORDER:
+        a, token = lax.optimization_barrier((arrived[i], token))
+        pieces[i] = token = lax.all_gather(a, "core", axis=0, tiled=True)
     out = attend_earlier(doc_lengths, queries, state, pieces)
     return out.reshape(query_heads.shape)
 

time: 77.3 us -> 76.5 us (0.990)
  waiting for transfers between devices: 8.47 us -> 0.01 us
  blocking collectives: 47.6 us -> 53 us
  Pallas kernels: 10.2 us -> 12.5 us
    ppermute x5, waiting for transfers between devices: 8.47 us -> 0.01 us  [shards(): arrived.append(lax.ppermute(own, ('core', 'ctx'), pairs))]
    all_gather x5, blocking collectives: 15.6 us -> 21 us  [shards(): pieces[i] = token = lax.all_gather(a, 'core', axis=0, tiled=True)]
    pallas_call x1, Pallas kernels: 7.03 us -> 9.36 us  [attend_earlier(): pl.pallas_call(earlier_kernel, out_shape=jax.ShapeDtypeStruct((rows, widt...]
  transfers between devices with their start and end apart: 5 -> 5, of which waited for: 1 -> 0; matrix products, arithmetic and copies ran while one was open for 0% -> 0% of each run, Pallas kernels for 4% -> 4%
where the time goes in v5:
time: 76.5 us; the launch traced here: 76.1 us
  blocking collectives  53 us (69%)
  Pallas kernels  12.5 us (16%)
  starting transfers between devices  9.63 us (13%)
  local copies, waits for them, and re-layouts  0.82 us (1%)
    all_to_all x1, blocking collectives, shards(): lax.all_to_all(send, ('zhi', 'tp'), split_axis=0, concat_axis=0, tiled=True)  26.7 us
    all_gather x5, blocking collectives, shards(): pieces[i] = token = lax.all_gather(a, 'core', axis=0, tiled=True)  21 us
    ppermute x5, starting transfers between devices, shards(): arrived.append(lax.ppermute(own, ('core', 'ctx'), pairs))  9.63 us
    pallas_call x1, Pallas kernels, attend_earlier(): pl.pallas_call(earlier_kernel, out_shape=jax.ShapeDtypeStruct((rows, widt...  9.36 us
    all_gather x1, blocking collectives, shards(): own = lax.all_gather(half, 'core', axis=0, tiled=True)  5.27 us
    pallas_call x1, Pallas kernels, attend_own(): pl.pallas_call(own_kernel, out_shape=tuple((jax.ShapeDtypeStruct((n, colu...  3.17 us
  transfers between devices with their start and end apart: 5, of which 0 were waited for; matrix products, arithmetic and copies ran while one was open for 0% of the time, Pallas kernels for 4%

profile of v5, /device:TPU:19, one launch (start us, length us, event | category | flops | bytes accessed | tf_op | source)
XLA Modules:
  0.0 76.1 jit_solution(6786776864086005773)
XLA Ops:
  0.0 0.0 copy-start.1
  0.0 0.8 %copy.9 = bf16[2,8,8,128]{3,2,1,0:T(8,128)(2,1)S(1)} copy(bf16[2,8,8,128]{3,1,2,0:T(8,128)(2,1)} %bitcast.20) | data formatting | bytes 65536
  0.8 0.0 copy-done.1
  0.9 26.7 %all_to_all.5 = bf16[16,2,16,128]{3,2,1,0:T(8,128)(2,1)S(1)} all-to-all(bf16[16,2,16,128]{3,2,1,0:T(8,128)(2,1)S(1)} %copy.8), channel_id=1, replica_groups=mesh['zhi'=2,'core'=2,'ctx'=16,'tp'=8] {'zhi','tp'}, dimensions={0} | all-to-all | bytes 262144 | tf_op jit(solution)/shard_map/all_to_all | solution.py:229
  27.6 5.3 %all_gather.18.blk_ref = bf16[32,2,16,128]{3,2,1,0:T(8,128)(2,1)S(1)} all-gather(bf16[16,2,16,128]{3,2,1,0:T(8,128)(2,1)S(1)} %all_to_all.5), channel_id=1, replica_groups=mesh['zhi'=2,'core'=2,'ctx'=16,'tp'=8] {'core'}, dimensions={0}, use_global_device_ids=true | all-gather | bytes 393216 | tf_op jit(solution)/shard_map/all_gather | solution.py:230
  32.9 0.0 copy-start
  32.9 2.9 %collective-permute-start = (bf16[32,2,16,128]{3,2,1,0:T(8,128)(2,1)S(1)}, bf16[32,2,16,128]{3,2,1,0:T(8,128)(2,1)S(1)}, u32[]{:S(2)}, u32[]{:S(2)}) collective-permute-start(bf16[32,2,16,128]{3,2,1,0:T(8,128)(2,1)S(1)} %all_gather.18.blk_ref), channel_id=1, source_target_pairs={{0,8},{8,16},{16,24},{24,32},{32,40},{40,48},{48,56},{56,64},{64,7... | collective-permute-start | bytes 786440 | tf_op jit(solution)/shard_map/ppermute | solution.py:236
  35.8 1.3 %collective-permute-start.1 = (bf16[32,2,16,128]{3,2,1,0:T(8,128)(2,1)S(1)}, bf16[32,2,16,128]{3,2,1,0:T(8,128)(2,1)S(1)}, u32[]{:S(2)}, u32[]{:S(2)}) collective-permute-start(bf16[32,2,16,128]{3,2,1,0:T(8,128)(2,1)S(1)} %all_gather.18.blk_ref), channel_id=1, source_target_pairs={{0,16},{8,24},{16,32},{24,40},{32,48},{40,56},{48,64},{56,72},{64,... | collective-permute-start | bytes 786440 | tf_op jit(solution)/shard_map/ppermute | solution.py:236
  37.1 0.7 collective-permute-start.4
  37.7 3.5 %collective-permute-start.3 = (bf16[32,2,16,128]{3,2,1,0:T(8,128)(2,1)S(1)}, bf16[32,2,16,128]{3,2,1,0:T(8,128)(2,1)S(1)}, u32[]{:S(2)}, u32[]{:S(2)}) collective-permute-start(bf16[32,2,16,128]{3,2,1,0:T(8,128)(2,1)S(1)} %all_gather.18.blk_ref), channel_id=1, source_target_pairs={{0,40},{8,48},{16,56},{24,64},{32,72},{40,80},{48,88},{56,96},{64,... | collective-permute-start | bytes 786440 | tf_op jit(solution)/shard_map/ppermute | solution.py:236
  41.2 1.3 %collective-permute-start.2 = (bf16[32,2,16,128]{3,2,1,0:T(8,128)(2,1)S(1)}, bf16[32,2,16,128]{3,2,1,0:T(8,128)(2,1)S(1)}, u32[]{:S(2)}, u32[]{:S(2)}) collective-permute-start(bf16[32,2,16,128]{3,2,1,0:T(8,128)(2,1)S(1)} %all_gather.18.blk_ref), channel_id=1, source_target_pairs={{0,24},{8,32},{16,40},{24,48},{32,56},{40,64},{48,72},{56,80},{64,... | collective-permute-start | bytes 786440 | tf_op jit(solution)/shard_map/ppermute | solution.py:236
  42.5 0.0 copy-done
  42.5 3.2 %attend_own.1 = (f32[1,1024]{1,0:T(1,128)}, f32[8,1024]{1,0:T(8,128)}, f32[128,1024]{1,0:T(8,128)}) custom-call(s32[4]{0:T(128)} %lengths_ref.3, bf16[512,256]{1,0:T(8,128)(2,1)} %bitcast.16, bf16[32,2,16,128]{3,2,1,0:T(8,128)(2,1)} %copy-done), custom_call_target="tpu_custom_call" | custom-call | tf_op jit(solution)/shard_map/attend_own/pallas_call | solution.py:183
  45.7 0.0 collective-permute-done
  45.7 6.4 %all_gather.19.refs_0_ = bf16[64,2,16,128]{3,2,1,0:T(8,128)(2,1)} all-gather(bf16[32,2,16,128]{3,2,1,0:T(8,128)(2,1)S(1)} %collective-permute-done), channel_id=1, replica_groups=mesh['zhi'=2,'core'=2,'ctx'=16,'tp'=8] {'core'}, dimensions={0}, use_global_device_ids=true | all-gather | bytes 786432 | tf_op jit(solution)/shard_map/all_gather | solution.py:242
  52.1 0.0 collective-permute-done.1
  52.1 2.3 %all_gather.20.refs_1_ = bf16[64,2,16,128]{3,2,1,0:T(8,128)(2,1)} all-gather(bf16[32,2,16,128]{3,2,1,0:T(8,128)(2,1)S(1)} %collective-permute-done.1), channel_id=1, replica_groups=mesh['zhi'=2,'core'=2,'ctx'=16,'tp'=8] {'core'}, dimensions={0}, use_global_device_ids=true | all-gather | bytes 786432 | tf_op jit(solution)/shard_map/all_gather | solution.py:242
  54.5 0.0 collective-permute-done.4
  54.5 5.6 %all_gather.21.refs_4_ = bf16[64,2,16,128]{3,2,1,0:T(8,128)(2,1)} all-gather(bf16[32,2,16,128]{3,2,1,0:T(8,128)(2,1)S(1)} %collective-permute-done.4), channel_id=1, replica_groups=mesh['zhi'=2,'core'=2,'ctx'=16,'tp'=8] {'core'}, dimensions={0}, use_global_device_ids=true | all-gather | bytes 786432 | tf_op jit(solution)/shard_map/all_gather | solution.py:242
  60.0 0.0 collective-permute-done.3
  60.0 4.4 %all_gather.22.refs_3_ = bf16[64,2,16,128]{3,2,1,0:T(8,128)(2,1)} all-gather(bf16[32,2,16,128]{3,2,1,0:T(8,128)(2,1)S(1)} %collective-permute-done.3), channel_id=1, replica_groups=mesh['zhi'=2,'core'=2,'ctx'=16,'tp'=8] {'core'}, dimensions={0}, use_global_device_ids=true | all-gather | bytes 786432 | tf_op jit(solution)/shard_map/all_gather | solution.py:242
  64.4 0.0 collective-permute-done.2
  64.4 2.3 %all_gather.23.refs_2_ = bf16[64,2,16,128]{3,2,1,0:T(8,128)(2,1)} all-gather(bf16[32,2,16,128]{3,2,1,0:T(8,128)(2,1)S(1)} %collective-permute-done.2), channel_id=1, replica_groups=mesh['zhi'=2,'core'=2,'ctx'=16,'tp'=8] {'core'}, dimensions={0}, use_global_device_ids=true | all-gather | bytes 786432 | tf_op jit(solution)/shard_map/all_gather | solution.py:242
  66.7 9.4 %attend_earlier.1 = bf16[512,256]{1,0:T(8,128)(2,1)} custom-call(s32[4]{0:T(128)} %lengths_ref.3, bf16[512,256]{1,0:T(8,128)(2,1)} %bitcast.17, f32[1,1024]{1,0:T(1,128)} %get-tuple-element.13.m_in, f32[8,1024]{1,0:T(8,128)} %get-tuple-element.14.l_in, f32[128,1024]{1,0:T(8,128)} %get-tuple-element.15.acc_in, bf16[64,2,16,128]{3,2,1,0:T(8,128)(2,1)} %all_gather.19.refs_0_, ...), custom_call_target="tpu_custom_call" | custom-call | tf_op jit(solution)/shard_map/attend_earlier/pallas_call | solution.py:200
  (3 shorter events, 0.1 us)
Async XLA Ops:
  0.0 0.8 %copy-start.1 = (bf16[1,16,1024]{2,1,0:T(8,128)(2,1)S(1)}, bf16[1,16,1024]{2,1,0:T(8,128)(2,1)}, u32[]{:S(2)}) copy-start(bf16[1,16,1024]{2,1,0:T(8,128)(2,1)} %param.6) | copy-start | bytes 98308
  32.9 9.7 %copy-start = (bf16[32,2,16,128]{3,2,1,0:T(8,128)(2,1)}, bf16[32,2,16,128]{3,2,1,0:T(8,128)(2,1)S(1)}, u32[]{:S(2)}) copy-start(bf16[32,2,16,128]{3,2,1,0:T(8,128)(2,1)S(1)} %all_gather.18.blk_ref) | copy-start | bytes 786436
  32.9 12.9 %collective-permute-start = (bf16[32,2,16,128]{3,2,1,0:T(8,128)(2,1)S(1)}, bf16[32,2,16,128]{3,2,1,0:T(8,128)(2,1)S(1)}, u32[]{:S(2)}, u32[]{:S(2)}) collective-permute-start(bf16[32,2,16,128]{3,2,1,0:T(8,128)(2,1)S(1)} %all_gather.18.blk_ref), channel_id=1, source_target_pairs={{0,8},{8,16},{16,24},{24,32},{32,40},{40,48},{48,56},{56,64},{64,7... | collective-permute-start | bytes 786440 | tf_op jit(solution)/shard_map/ppermute | solution.py:236
  35.8 16.4 %collective-permute-start.1 = (bf16[32,2,16,128]{3,2,1,0:T(8,128)(2,1)S(1)}, bf16[32,2,16,128]{3,2,1,0:T(8,128)(2,1)S(1)}, u32[]{:S(2)}, u32[]{:S(2)}) collective-permute-start(bf16[32,2,16,128]{3,2,1,0:T(8,128)(2,1)S(1)} %all_gather.18.blk_ref), channel_id=1, source_target_pairs={{0,16},{8,24},{16,32},{24,40},{32,48},{40,56},{48,64},{56,72},{64,... | collective-permute-start | bytes 786440 | tf_op jit(solution)/shard_map/ppermute | solution.py:236
  37.1 17.4 %collective-permute-start.4 = (bf16[32,2,16,128]{3,2,1,0:T(8,128)(2,1)S(1)}, bf16[32,2,16,128]{3,2,1,0:T(8,128)(2,1)S(1)}, u32[]{:S(2)}, u32[]{:S(2)}) collective-permute-start(bf16[32,2,16,128]{3,2,1,0:T(8,128)(2,1)S(1)} %all_gather.18.blk_ref), channel_id=1, source_target_pairs={{0,72},{8,80},{16,88},{24,96},{32,104},{40,112},{48,120},{128,208}... | collective-permute-start | bytes 786440 | tf_op jit(solution)/shard_map/ppermute | solution.py:236
  37.7 22.3 %collective-permute-start.3 = (bf16[32,2,16,128]{3,2,1,0:T(8,128)(2,1)S(1)}, bf16[32,2,16,128]{3,2,1,0:T(8,128)(2,1)S(1)}, u32[]{:S(2)}, u32[]{:S(2)}) collective-permute-start(bf16[32,2,16,128]{3,2,1,0:T(8,128)(2,1)S(1)} %all_gather.18.blk_ref), channel_id=1, source_target_pairs={{0,40},{8,48},{16,56},{24,64},{32,72},{40,80},{48,88},{56,96},{64,... | collective-permute-start | bytes 786440 | tf_op jit(solution)/shard_map/ppermute | solution.py:236
  41.2 23.2 %collective-permute-start.2 = (bf16[32,2,16,128]{3,2,1,0:T(8,128)(2,1)S(1)}, bf16[32,2,16,128]{3,2,1,0:T(8,128)(2,1)S(1)}, u32[]{:S(2)}, u32[]{:S(2)}) collective-permute-start(bf16[32,2,16,128]{3,2,1,0:T(8,128)(2,1)S(1)} %all_gather.18.blk_ref), channel_id=1, source_target_pairs={{0,24},{8,32},{16,40},{24,48},{32,56},{40,64},{48,72},{56,80},{64,... | collective-permute-start | bytes 786440 | tf_op jit(solution)/shard_map/ppermute | solution.py:236

commit v6 on v5

--- a/solution.py
+++ b/solution.py
@@ -16,6 +16,7 @@
 STEP = math.log2(math.e) / math.sqrt(HD)
 HOPS = ((1, 4), (2, 8), (3, 7), (5, 6), (9, 10))
 ORDER = (0, 1, 4, 3, 2)
+SPLIT = 2
 
 
 def doc_starts(lengths_ref):
@@ -84,9 +85,14 @@
         acc_ref[:, at] = mix(values, weights)
 
 
-def earlier_kernel(lengths_ref, q_ref, m_in, l_in, acc_in, *refs):
+def earlier_kernel(todo, last, lengths_ref, q_ref, m_in, l_in, acc_in, *refs):
+    if last:
+        l_own, acc_own, refs = refs[0], refs[1], refs[2:]
     pieces, refs = refs[: len(HOPS)], refs[len(HOPS) :]
-    out_ref, stacked_ref, m_ref, l_ref, acc_ref, buf_ref, sems = refs
+    if last:
+        out_ref, m_ref, l_ref, acc_ref, stacked_ref, buf_ref, sems = refs
+    else:
+        l_ref, acc_ref, stacked_ref, buf_ref, sems = refs
     rows, width = q_ref.shape
     heads = width // HD
     block = lax.axis_index("ctx")
@@ -94,29 +100,40 @@
     count = block - start_of(block * rows, starts) // rows
     part = buf_ref.shape[1]
 
-    for piece, hops in zip(pieces, HOPS):
-        for c, k in enumerate(hops):
-
-            @pl.when(k <= count)
-            def _():
-                pltpu.make_async_copy(
-                    piece.at[c * part : (c + 1) * part], buf_ref.at[k - 1], sems.at[k - 1]
-                ).start()
-
+    def fetch(slots, begin):
+        for i in slots:
+            for c, k in enumerate(HOPS[i]):
+
+                @pl.when(k <= count)
+                def _():
+                    copy = pltpu.make_async_copy(
+                        pieces[i].at[c * part : (c + 1) * part],
+                        buf_ref.at[k - 1],
+                        sems.at[k - 1],
+                    )
+                    copy.start() if begin else copy.wait()
+
+    fetch(todo, True)
     stack_heads(q_ref, stacked_ref)
     l_ref[...] = l_in[...]
     acc_ref[...] = acc_in[...]
     query = block * rows + lax.broadcasted_iota(jnp.int32, (1, rows), 1)
     begin = jnp.concatenate([start_of(query, starts)] * heads, axis=1)
-
-    def load(i):
-        keys = buf_ref[i, :, 0].reshape(rows, HD)
-        values = buf_ref[i, :, 1].reshape(rows, HD)
-        return keys, values, (block - 1 - i) * rows
-
-    def step(i, carry):
-        pltpu.make_async_copy(pieces[0].at[0:part], buf_ref.at[i], sems.at[i]).wait()
-        keys, values, base = load(i)
+    hops = sorted(k for i in todo for k in HOPS[i])
+
+    def load(k):
+        keys = buf_ref[k - 1, :, 0].reshape(rows, HD)
+        values = buf_ref[k - 1, :, 1].reshape(rows, HD)
+        return keys, values, (block - k) * rows
+
+    def step(n, carry):
+        k = hops[0]
+        for i, hop in enumerate(hops[1:]):
+            k = jnp.where(n > i, hop, k)
+        pltpu.make_async_copy(
+            pieces[todo[0]].at[0:part], buf_ref.at[k - 1], sems.at[k - 1]
+        ).wait()
+        keys, values, base = load(k)
         cut = False
         for s in starts:
             cut = cut | ((s > base) & (s < base + rows))
@@ -141,18 +158,26 @@
 
         return carry
 
-    lax.fori_loop(0, count, step, 0)
+    here = 0
+    for hop in hops:
+        here = here + jnp.where(hop <= count, 1, 0)
+    lax.fori_loop(0, here, step, 0)
+    if not last:
+        return
 
     fits = jnp.sum(l_ref[...], axis=0, keepdims=True) < ROOM
 
     @pl.when(jnp.min(fits.astype(jnp.float32)) < 0.5)
     def _():
+        rest = [i for i in range(len(HOPS)) if i not in todo]
+        fetch(rest, True)
+        fetch(rest, False)
         m_ref[...] = m_in[...]
-        l_ref[...] = l_in[...]
-        acc_ref[...] = acc_in[...]
-
-        def again(i, carry):
-            keys, values, base = load(i)
+        l_ref[...] = l_own[...]
+        acc_ref[...] = acc_own[...]
+
+        def again(n, carry):
+            keys, values, base = load(n + 1)
             key = key_rows((rows, rows)) + base
             for h in range(heads):
                 at = slice(h * rows, (h + 1) * rows)
@@ -191,27 +216,40 @@
     )(lengths, queries, own)
 
 
-def attend_earlier(lengths, queries, state, pieces):
+def attend_earlier(lengths, queries, own, state, pieces, todo, last):
     rows, width = queries.shape
     columns = rows * (width // HD)
-    shape = pieces[0].shape
+    part, *unit = next(p for p in pieces if p is not None).shape
     count = 2 * len(pieces)
     vmem = pl.BlockSpec(memory_space=pltpu.VMEM)
+    sums = [(n, columns) for n in (8, HD)]
+    scratch = [pltpu.VMEM(shape, jnp.float32) for shape in [(1, columns), *sums]]
+    out = jax.ShapeDtypeStruct((rows, width), jnp.bfloat16)
+    given = [p for p in pieces if p is not None]
+    place = [i for i, p in enumerate(pieces) if p is not None]
+
+    def kernel(*refs):
+        lead = 5 + (2 if last else 0)
+        held = [None] * len(pieces)
+        for i, ref in zip(place, refs[lead : lead + len(given)]):
+            held[i] = ref
+        earlier_kernel(todo, last, *refs[:lead], *held, *refs[lead + len(given) :])
+
     return pl.pallas_call(
-        earlier_kernel,
-        out_shape=jax.ShapeDtypeStruct((rows, width), jnp.bfloat16),
+        kernel,
+        out_shape=out if last else tuple(jax.ShapeDtypeStruct(n, jnp.float32) for n in sums),
         in_specs=[pl.BlockSpec(memory_space=pltpu.SMEM)]
-        + [vmem] * 4
-        + [pl.BlockSpec(memory_space=pl.ANY)] * len(pieces),
-        out_specs=vmem,
-        scratch_shapes=[pltpu.VMEM((columns, HD), jnp.bfloat16)]
-        + [pltpu.VMEM((n, columns), jnp.float32) for n in (1, 8, HD)]
+        + [vmem] * (4 + (2 if last else 0))
+        + [pl.BlockSpec(memory_space=pl.ANY)] * len(given),
+        out_specs=vmem if last else (vmem,) * 2,
+        scratch_shapes=(scratch if last else [])
         + [
-            pltpu.VMEM((count, shape[0] // 2, *shape[1:]), jnp.bfloat16),
+            pltpu.VMEM((columns, HD), jnp.bfloat16),
+            pltpu.VMEM((count, part // 2, *unit), jnp.bfloat16),
             pltpu.SemaphoreType.DMA((count,)),
         ],
-        name="attend_earlier",
-    )(lengths, queries, *state, *pieces)
+        name="attend_last" if last else "attend_earlier",
+    )(lengths, queries, own[0], *state, *(own[1:] if last else ()), *given)
 
 
 def shards(query_heads, key_cache, value_cache, doc_lengths):
@@ -234,13 +272,21 @@
         pairs = [(b, b + k0) for b in range(blocks - k0)]
         pairs += [(blocks + b, blocks + b + k1) for b in range(blocks - k1)]
         arrived.append(lax.ppermute(own, ("core", "ctx"), pairs))
-    state = attend_own(doc_lengths, queries, own)
-    pieces = list(arrived)
+    own_state = attend_own(doc_lengths, queries, own)
+    state = own_state[1:]
+    pieces = [None] * len(HOPS)
     token = state
-    for i in ORDER:
+    for n, i in enumerate(ORDER):
+        if n == SPLIT:
+            state = attend_earlier(
+                doc_lengths, queries, own_state, state, pieces, ORDER[:SPLIT], False
+            )
+            token = (token, state)
         a, token = lax.optimization_barrier((arrived[i], token))
         pieces[i] = token = lax.all_gather(a, "core", axis=0, tiled=True)
-    out = attend_earlier(doc_lengths, queries, state, pieces)
+    out = attend_earlier(
+        doc_lengths, queries, own_state, state, pieces, ORDER[SPLIT:], True
+    )
     return out.reshape(query_heads.shape)
 
 

time: 76.5 us -> 73.9 us (0.966)
  the two profiles are of different devices: /device:TPU:19 before, /device:TPU:25 now
where the time goes in v6:
time: 73.9 us; the launch traced here: 73.4 us
  blocking collectives  49.6 us (67%)
  Pallas kernels  16.4 us (22%)
  starting transfers between devices  6.45 us (9%)
  local copies, waits for them, and re-layouts  0.82 us (1%)
    all_to_all x1, blocking collectives, shards(): lax.all_to_all(send, ('zhi', 'tp'), split_axis=0, concat_axis=0, tiled=True)  26.7 us
    all_gather x5, blocking collectives, shards(): pieces[i] = token = lax.all_gather(a, 'core', axis=0, tiled=True)  17.6 us
    pallas_call x2, Pallas kernels, attend_earlier(): pl.pallas_call(kernel, out_shape=out if last else tuple((jax.ShapeDtypeSt...  13.2 us
    ppermute x5, starting transfers between devices, shards(): arrived.append(lax.ppermute(own, ('core', 'ctx'), pairs))  6.45 us
    all_gather x1, blocking collectives, shards(): own = lax.all_gather(half, 'core', axis=0, tiled=True)  5.27 us
    pallas_call x1, Pallas kernels, attend_own(): pl.pallas_call(own_kernel, out_shape=tuple((jax.ShapeDtypeStruct((n, colu...  3.18 us
  transfers between devices with their start and end apart: 5, of which 0 were waited for; matrix products, arithmetic and copies ran while one was open for 0% of the time, Pallas kernels for 12%

profile of v6, /device:TPU:25, one launch (start us, length us, event | category | flops | bytes accessed | tf_op | source)
XLA Modules:
  0.0 73.4 jit_solution(11877965555779048367)
XLA Ops:
  0.0 0.0 copy-start.1
  0.0 0.8 %copy.9 = bf16[2,8,8,128]{3,2,1,0:T(8,128)(2,1)S(1)} copy(bf16[2,8,8,128]{3,1,2,0:T(8,128)(2,1)} %bitcast.21) | data formatting | bytes 65536
  0.8 0.0 copy-done.1
  0.9 26.7 %all_to_all.5 = bf16[16,2,16,128]{3,2,1,0:T(8,128)(2,1)S(1)} all-to-all(bf16[16,2,16,128]{3,2,1,0:T(8,128)(2,1)S(1)} %copy.8), channel_id=1, replica_groups=mesh['zhi'=2,'core'=2,'ctx'=16,'tp'=8] {'zhi','tp'}, dimensions={0} | all-to-all | bytes 262144 | tf_op jit(solution)/shard_map/all_to_all | solution.py:267
  27.6 5.3 %all_gather.18.blk_ref = bf16[32,2,16,128]{3,2,1,0:T(8,128)(2,1)S(1)} all-gather(bf16[16,2,16,128]{3,2,1,0:T(8,128)(2,1)S(1)} %all_to_all.5), channel_id=1, replica_groups=mesh['zhi'=2,'core'=2,'ctx'=16,'tp'=8] {'core'}, dimensions={0}, use_global_device_ids=true | all-gather | bytes 393216 | tf_op jit(solution)/shard_map/all_gather | solution.py:268
  32.9 1.3 %collective-permute-start = (bf16[32,2,16,128]{3,2,1,0:T(8,128)(2,1)S(1)}, bf16[32,2,16,128]{3,2,1,0:T(8,128)(2,1)S(1)}, u32[]{:S(2)}, u32[]{:S(2)}) collective-permute-start(bf16[32,2,16,128]{3,2,1,0:T(8,128)(2,1)S(1)} %all_gather.18.blk_ref), channel_id=1, source_target_pairs={{0,8},{8,16},{16,24},{24,32},{32,40},{40,48},{48,56},{56,64},{64,7... | collective-permute-start | bytes 786440 | tf_op jit(solution)/shard_map/ppermute | solution.py:274
  34.1 1.3 %collective-permute-start.1 = (bf16[32,2,16,128]{3,2,1,0:T(8,128)(2,1)S(1)}, bf16[32,2,16,128]{3,2,1,0:T(8,128)(2,1)S(1)}, u32[]{:S(2)}, u32[]{:S(2)}) collective-permute-start(bf16[32,2,16,128]{3,2,1,0:T(8,128)(2,1)S(1)} %all_gather.18.blk_ref), channel_id=1, source_target_pairs={{0,16},{8,24},{16,32},{24,40},{32,48},{40,56},{48,64},{56,72},{64,... | collective-permute-start | bytes 786440 | tf_op jit(solution)/shard_map/ppermute | solution.py:274
  35.4 1.3 %collective-permute-start.4 = (bf16[32,2,16,128]{3,2,1,0:T(8,128)(2,1)S(1)}, bf16[32,2,16,128]{3,2,1,0:T(8,128)(2,1)S(1)}, u32[]{:S(2)}, u32[]{:S(2)}) collective-permute-start(bf16[32,2,16,128]{3,2,1,0:T(8,128)(2,1)S(1)} %all_gather.18.blk_ref), channel_id=1, source_target_pairs={{0,72},{8,80},{16,88},{24,96},{32,104},{40,112},{48,120},{128,208}... | collective-permute-start | bytes 786440 | tf_op jit(solution)/shard_map/ppermute | solution.py:274
  36.7 1.3 %collective-permute-start.3 = (bf16[32,2,16,128]{3,2,1,0:T(8,128)(2,1)S(1)}, bf16[32,2,16,128]{3,2,1,0:T(8,128)(2,1)S(1)}, u32[]{:S(2)}, u32[]{:S(2)}) collective-permute-start(bf16[32,2,16,128]{3,2,1,0:T(8,128)(2,1)S(1)} %all_gather.18.blk_ref), channel_id=1, source_target_pairs={{0,40},{8,48},{16,56},{24,64},{32,72},{40,80},{48,88},{56,96},{64,... | collective-permute-start | bytes 786440 | tf_op jit(solution)/shard_map/ppermute | solution.py:274
  38.0 1.3 %collective-permute-start.2 = (bf16[32,2,16,128]{3,2,1,0:T(8,128)(2,1)S(1)}, bf16[32,2,16,128]{3,2,1,0:T(8,128)(2,1)S(1)}, u32[]{:S(2)}, u32[]{:S(2)}) collective-permute-start(bf16[32,2,16,128]{3,2,1,0:T(8,128)(2,1)S(1)} %all_gather.18.blk_ref), channel_id=1, source_target_pairs={{0,24},{8,32},{16,40},{24,48},{32,56},{40,64},{48,72},{56,80},{64,... | collective-permute-start | bytes 786440 | tf_op jit(solution)/shard_map/ppermute | solution.py:274
  39.3 0.0 copy-done
  39.4 3.2 %attend_own.1 = (f32[1,1024]{1,0:T(1,128)}, f32[8,1024]{1,0:T(8,128)}, f32[128,1024]{1,0:T(8,128)}) custom-call(s32[4]{0:T(128)} %refs_0_.3, bf16[512,256]{1,0:T(8,128)(2,1)} %bitcast.16, bf16[32,2,16,128]{3,2,1,0:T(8,128)(2,1)} %copy-done), custom_call_target="tpu_custom_call" | custom-call | tf_op jit(solution)/shard_map/attend_own/pallas_call | solution.py:208
  42.5 0.0 collective-permute-done
  42.5 8.4 %all_gather.19.refs_5_.refs_7_ = bf16[64,2,16,128]{3,2,1,0:T(8,128)(2,1)} all-gather(bf16[32,2,16,128]{3,2,1,0:T(8,128)(2,1)S(1)} %collective-permute-done), channel_id=1, replica_groups=mesh['zhi'=2,'core'=2,'ctx'=16,'tp'=8] {'core'}, dimensions={0}, use_global_device_ids=true | all-gather | bytes 786432 | tf_op jit(solution)/shard_map/all_gather | solution.py:286
  50.9 0.0 collective-permute-done.1
  50.9 2.3 %all_gather.20.refs_6_.refs_8_ = bf16[64,2,16,128]{3,2,1,0:T(8,128)(2,1)} all-gather(bf16[32,2,16,128]{3,2,1,0:T(8,128)(2,1)S(1)} %collective-permute-done.1), channel_id=1, replica_groups=mesh['zhi'=2,'core'=2,'ctx'=16,'tp'=8] {'core'}, dimensions={0}, use_global_device_ids=true | all-gather | bytes 786432 | tf_op jit(solution)/shard_map/all_gather | solution.py:286
  53.2 5.8 %attend_earlier.1 = (f32[8,1024]{1,0:T(8,128)}, f32[128,1024]{1,0:T(8,128)}) custom-call(s32[4]{0:T(128)} %refs_0_.3, bf16[512,256]{1,0:T(8,128)(2,1)} %bitcast.17, f32[1,1024]{1,0:T(1,128)} %get-tuple-element.15.refs_2_, f32[8,1024]{1,0:T(8,128)} %get-tuple-element.16.refs_3_.refs_5_, f32[128,1024]{1,0:T(8,128)} %get-tuple-element.17.refs_4_.refs_6_, ...), custom_call_target="tpu_custom_call" | custom-call | tf_op jit(solution)/shard_map/attend_earlier/pallas_call | solution.py:238
  59.0 0.0 collective-permute-done.4
  59.0 2.3 %all_gather.21.refs_11_ = bf16[64,2,16,128]{3,2,1,0:T(8,128)(2,1)} all-gather(bf16[32,2,16,128]{3,2,1,0:T(8,128)(2,1)S(1)} %collective-permute-done.4), channel_id=1, replica_groups=mesh['zhi'=2,'core'=2,'ctx'=16,'tp'=8] {'core'}, dimensions={0}, use_global_device_ids=true | all-gather | bytes 786432 | tf_op jit(solution)/shard_map/all_gather | solution.py:286
  61.3 0.0 collective-permute-done.3
  61.3 2.3 %all_gather.22.refs_10_ = bf16[64,2,16,128]{3,2,1,0:T(8,128)(2,1)} all-gather(bf16[32,2,16,128]{3,2,1,0:T(8,128)(2,1)S(1)} %collective-permute-done.3), channel_id=1, replica_groups=mesh['zhi'=2,'core'=2,'ctx'=16,'tp'=8] {'core'}, dimensions={0}, use_global_device_ids=true | all-gather | bytes 786432 | tf_op jit(solution)/shard_map/all_gather | solution.py:286
  63.6 0.0 collective-permute-done.2
  63.6 2.3 %all_gather.23.refs_9_ = bf16[64,2,16,128]{3,2,1,0:T(8,128)(2,1)} all-gather(bf16[32,2,16,128]{3,2,1,0:T(8,128)(2,1)S(1)} %collective-permute-done.2), channel_id=1, replica_groups=mesh['zhi'=2,'core'=2,'ctx'=16,'tp'=8] {'core'}, dimensions={0}, use_global_device_ids=true | all-gather | bytes 786432 | tf_op jit(solution)/shard_map/all_gather | solution.py:286
  65.9 7.5 %attend_last.1 = bf16[512,256]{1,0:T(8,128)(2,1)} custom-call(s32[4]{0:T(128)} %refs_0_.3, bf16[512,256]{1,0:T(8,128)(2,1)} %bitcast.18, f32[1,1024]{1,0:T(1,128)} %get-tuple-element.15.refs_2_, f32[8,1024]{1,0:T(8,128)} %get-tuple-element.20.refs_3_, f32[128,1024]{1,0:T(8,128)} %get-tuple-element.21.refs_4_, f32[8,1024]{1,0:T(8,128)} %get-tuple-element.16.refs_3_.refs_5_, ...), custom_call_target="tpu_custom_call" | custom-call | tf_op jit(solution)/shard_map/attend_last/pallas_call | solution.py:238
  (4 shorter events, 0.1 us)
Async XLA Ops:
  0.0 0.8 %copy-start.1 = (bf16[1,16,1024]{2,1,0:T(8,128)(2,1)S(1)}, bf16[1,16,1024]{2,1,0:T(8,128)(2,1)}, u32[]{:S(2)}) copy-start(bf16[1,16,1024]{2,1,0:T(8,128)(2,1)} %param.6) | copy-start | bytes 98308
  32.9 6.5 %copy-start = (bf16[32,2,16,128]{3,2,1,0:T(8,128)(2,1)}, bf16[32,2,16,128]{3,2,1,0:T(8,128)(2,1)S(1)}, u32[]{:S(2)}) copy-start(bf16[32,2,16,128]{3,2,1,0:T(8,128)(2,1)S(1)} %all_gather.18.blk_ref) | copy-start | bytes 786436
  32.9 9.7 %collective-permute-start = (bf16[32,2,16,128]{3,2,1,0:T(8,128)(2,1)S(1)}, bf16[32,2,16,128]{3,2,1,0:T(8,128)(2,1)S(1)}, u32[]{:S(2)}, u32[]{:S(2)}) collective-permute-start(bf16[32,2,16,128]{3,2,1,0:T(8,128)(2,1)S(1)} %all_gather.18.blk_ref), channel_id=1, source_target_pairs={{0,8},{8,16},{16,24},{24,32},{32,40},{40,48},{48,56},{56,64},{64,7... | collective-permute-start | bytes 786440 | tf_op jit(solution)/shard_map/ppermute | solution.py:274
  34.1 16.8 %collective-permute-start.1 = (bf16[32,2,16,128]{3,2,1,0:T(8,128)(2,1)S(1)}, bf16[32,2,16,128]{3,2,1,0:T(8,128)(2,1)S(1)}, u32[]{:S(2)}, u32[]{:S(2)}) collective-permute-start(bf16[32,2,16,128]{3,2,1,0:T(8,128)(2,1)S(1)} %all_gather.18.blk_ref), channel_id=1, source_target_pairs={{0,16},{8,24},{16,32},{24,40},{32,48},{40,56},{48,64},{56,72},{64,... | collective-permute-start | bytes 786440 | tf_op jit(solution)/shard_map/ppermute | solution.py:274
  35.4 23.5 %collective-permute-start.4 = (bf16[32,2,16,128]{3,2,1,0:T(8,128)(2,1)S(1)}, bf16[32,2,16,128]{3,2,1,0:T(8,128)(2,1)S(1)}, u32[]{:S(2)}, u32[]{:S(2)}) collective-permute-start(bf16[32,2,16,128]{3,2,1,0:T(8,128)(2,1)S(1)} %all_gather.18.blk_ref), channel_id=1, source_target_pairs={{0,72},{8,80},{16,88},{24,96},{32,104},{40,112},{48,120},{128,208}... | collective-permute-start | bytes 786440 | tf_op jit(solution)/shard_map/ppermute | solution.py:274
  36.7 24.6 %collective-permute-start.3 = (bf16[32,2,16,128]{3,2,1,0:T(8,128)(2,1)S(1)}, bf16[32,2,16,128]{3,2,1,0:T(8,128)(2,1)S(1)}, u32[]{:S(2)}, u32[]{:S(2)}) collective-permute-start(bf16[32,2,16,128]{3,2,1,0:T(8,128)(2,1)S(1)} %all_gather.18.blk_ref), channel_id=1, source_target_pairs={{0,40},{8,48},{16,56},{24,64},{32,72},{40,80},{48,88},{56,96},{64,... | collective-permute-start | bytes 786440 | tf_op jit(solution)/shard_map/ppermute | solution.py:274
  38.0 25.6 %collective-permute-start.2 = (bf16[32,2,16,128]{3,2,1,0:T(8,128)(2,1)S(1)}, bf16[32,2,16,128]{3,2,1,0:T(8,128)(2,1)S(1)}, u32[]{:S(2)}, u32[]{:S(2)}) collective-permute-start(bf16[32,2,16,128]{3,2,1,0:T(8,128)(2,1)S(1)} %all_gather.18.blk_ref), channel_id=1, source_target_pairs={{0,24},{8,32},{16,40},{24,48},{32,56},{40,64},{48,72},{56,80},{64,... | collective-permute-start | bytes 786440 | tf_op jit(solution)/shard_map/ppermute | solution.py:274

commit v7 on v6

v7 whole, which is shorter than its diff:
```python
import math

import jax
import jax.numpy as jnp
from jax import lax
from jax.experimental import pallas as pl
from jax.experimental.pallas import tpu as pltpu
from jax.sharding import Mesh
from jax.sharding import PartitionSpec as P

HD = 128
NDOC = 4
HIDDEN = -1e30
NEVER = 1e30
ROOM = 2.0**60
STEP = math.log2(math.e) / math.sqrt(HD)
HOPS = ((1, 4), (2, 8), (3, 7), (5, 6), (9, 10))
ORDER = (0, 1, 4, 3, 2)
SPLIT = 2


def doc_starts(lengths_ref):
    starts = []
    total = 0
    for d in range(NDOC - 1):
        total = total + lengths_ref[d]
        starts.append(total)
    return starts


def start_of(position, starts):
    begin = jnp.zeros_like(position)
    for s in starts:
        begin = jnp.where(position >= s, s, begin)
    return begin


def key_rows(shape):
    n = lax.broadcasted_iota(jnp.int32, shape, 0)
    return (n & 127) + ((n >> 7) & 1) * 256 + (n >> 8) * 128


def stack_heads(q_ref, stacked_ref):
    rows, width = q_ref.shape
    for h in range(width // HD):
        stacked_ref[h * rows : (h + 1) * rows] = q_ref[:, h * HD : (h + 1) * HD]


def score(keys, queries):
    return lax.dot_general(
        keys, queries, (((1,), (1,)), ((), ())), preferred_element_type=jnp.float32
    )


def mix(values, weights):
    return lax.dot_general(
        values,
        weights.astype(jnp.bfloat16),
        (((0,), (0,)), ((), ())),
        preferred_element_type=jnp.float32,
    )


def fold(weights):
    n, width = weights.shape
    return jnp.sum(weights.reshape(n // 8, 8, width), axis=0)


def attend_kernel(todo, first, last, lengths_ref, q_ref, own_ref, pieces, before, out_ref, state, scratch):
    m_ref, l_ref, acc_ref = state
    stacked_ref, buf_ref, sems = scratch
    rows, width = q_ref.shape
    heads = width // HD
    block = lax.axis_index("ctx")
    starts = doc_starts(lengths_ref)
    count = block - start_of(block * rows, starts) // rows
    part = buf_ref.shape[1]

    def own_copy():
        return pltpu.make_async_copy(own_ref, buf_ref.at[0], sems.at[0])

    def fetch(slots, begin):
        for i in slots:
            for c, k in enumerate(HOPS[i]):

                @pl.when(k <= count)
                def _():
                    copy = pltpu.make_async_copy(
                        pieces[i].at[c * part : (c + 1) * part], buf_ref.at[k], sems.at[k]
                    )
                    copy.start() if begin else copy.wait()

    if first:
        own_copy().start()
    fetch(todo, True)
    stack_heads(q_ref, stacked_ref)
    query = block * rows + lax.broadcasted_iota(jnp.int32, (1, rows), 1)
    row_begin = start_of(query, starts)
    begin = jnp.concatenate([row_begin] * heads, axis=1)
    hops = sorted(k for i in todo for k in HOPS[i])

    def load(k):
        keys = buf_ref[k, :, 0].reshape(rows, HD)
        values = buf_ref[k, :, 1].reshape(rows, HD)
        return keys, values, (block - k) * rows

    def visit_own():
        keys, values, base = load(0)
        key = key_rows((rows, rows)) + base
        allowed = (key <= query) & (key >= row_begin)
        for h in range(heads):
            at = slice(h * rows, (h + 1) * rows)
            scores = jnp.where(allowed, score(keys, stacked_ref[at]), HIDDEN)
            top = jnp.max(scores, axis=0, keepdims=True)
            weights = jnp.exp2((scores - top) * STEP)
            m_ref[:, at] = top
            l_ref[:, at] = fold(weights)
            acc_ref[:, at] = mix(values, weights)

    if first:
        own_copy().wait()
        visit_own()
    else:
        for ref, was in zip(state, before):
            ref[...] = was[...]

    def step(n, carry):
        k = hops[0]
        for i, hop in enumerate(hops[1:]):
            k = jnp.where(n > i, hop, k)
        pltpu.make_async_copy(
            pieces[todo[0]].at[0:part], buf_ref.at[k], sems.at[k]
        ).wait()
        keys, values, base = load(k)
        cut = False
        for s in starts:
            cut = cut | ((s > base) & (s < base + rows))

        @pl.when(jnp.logical_not(cut))
        def _():
            top = jnp.where(begin <= base, m_ref[...], NEVER)
            weights = jnp.exp2((score(keys, stacked_ref[...]) - top) * STEP)
            l_ref[...] += fold(weights)
            acc_ref[...] += mix(values, weights)

        @pl.when(cut)
        def _():
            key = key_rows((rows, rows)) + base
            for h in range(heads):
                at = slice(h * rows, (h + 1) * rows)
                scores = score(keys, stacked_ref[at])
                weights = jnp.exp2((scores - m_ref[:, at]) * STEP)
                weights = jnp.where(key >= begin[:, at], weights, 0.0)
                l_ref[:, at] += fold(weights)
                acc_ref[:, at] += mix(values, weights)

        return carry

    here = 0
    for hop in hops:
        here = here + jnp.where(hop <= count, 1, 0)
    lax.fori_loop(0, here, step, 0)
    if not last:
        return

    fits = jnp.sum(l_ref[...], axis=0, keepdims=True) < ROOM

    @pl.when(jnp.min(fits.astype(jnp.float32)) < 0.5)
    def _():
        rest = [i for i in range(len(HOPS)) if i not in todo]
        fetch(rest, True)
        fetch(rest, False)
        if not first:
            own_copy().start()
            own_copy().wait()
        visit_own()

        def again(n, carry):
            keys, values, base = load(n + 1)
            key = key_rows((rows, rows)) + base
            for h in range(heads):
                at = slice(h * rows, (h + 1) * rows)
                scores = score(keys, stacked_ref[at])
                scores = jnp.where(key >= begin[:, at], scores, HIDDEN)
                old = m_ref[:, at]
                top = jnp.maximum(old, jnp.max(scores, axis=0, keepdims=True))
                weights = jnp.exp2((scores - top) * STEP)
                shrink = jnp.exp2((old - top) * STEP)
                m_ref[:, at] = top
                l_ref[:, at] = l_ref[:, at] * shrink + fold(weights)
                acc_ref[:, at] = acc_ref[:, at] * shrink + mix(values, weights)
            return carry

        lax.fori_loop(0, count, again, 0)

    total = jnp.sum(l_ref[...], axis=0, keepdims=True)
    for h in range(heads):
        at = slice(h * rows, (h + 1) * rows)
        attended = acc_ref[:, at] / total[:, at]
        out_ref[:, h * HD : (h + 1) * HD] = attended.T.astype(jnp.bfloat16)


def attend(lengths, queries, own, pieces, todo, state, last):
    rows, width = queries.shape
    columns = rows * (width // HD)
    vmem = pl.BlockSpec(memory_space=pltpu.VMEM)
    sums = [(n, columns) for n in (1, 8, HD)]
    out = jax.ShapeDtypeStruct((rows, width), jnp.bfloat16)
    place = [i for i, p in enumerate(pieces) if p is not None]

    def kernel(*refs):
        lead, refs = refs[:3], list(refs[3:])
        held = {i: refs.pop(0) for i in place}
        before = [refs.pop(0) for _ in state]
        out_ref = refs.pop(0) if last else None
        attend_kernel(
            todo, not state, last, *lead, held, before, out_ref, refs[:3], refs[3:]
        )

    return pl.pallas_call(
        kernel,
        out_shape=out if last else tuple(jax.ShapeDtypeStruct(n, jnp.float32) for n in sums),
        in_specs=[pl.BlockSpec(memory_space=pltpu.SMEM), vmem]
        + [pl.BlockSpec(memory_space=pl.ANY)] * (1 + len(place))
        + [vmem] * len(state),
        out_specs=vmem if last else (vmem,) * 3,
        scratch_shapes=([pltpu.VMEM(n, jnp.float32) for n in sums] if last else [])
        + [
            pltpu.VMEM((columns, HD), jnp.bfloat16),
            pltpu.VMEM((1 + 2 * len(HOPS), *own.shape), jnp.bfloat16),
            pltpu.SemaphoreType.DMA((1 + 2 * len(HOPS),)),
        ],
        name="attend_last" if last else "attend_first",
    )(lengths, queries, own, *[pieces[i] for i in place], *state)


def shards(query_heads, key_cache, value_cache, doc_lengths):
    rows, _, width = query_heads.shape
    queries = query_heads.reshape(rows, width)
    part = key_cache.shape[1]
    tp = lax.axis_size("tp")
    blocks = lax.axis_size("ctx")

    def by_head(cache):
        return cache.reshape(part, tp, HD).transpose(1, 0, 2)

    send = jnp.stack((by_head(key_cache), by_head(value_cache)), axis=1)
    send = jnp.concatenate((send, send), axis=0)
    half = lax.all_to_all(send, ("zhi", "tp"), split_axis=0, concat_axis=0, tiled=True)
    own = lax.all_gather(half, "core", axis=0, tiled=True)

    arrived = []
    for k0, k1 in HOPS:
        pairs = [(b, b + k0) for b in range(blocks - k0)]
        pairs += [(blocks + b, blocks + b + k1) for b in range(blocks - k1)]
        arrived.append(lax.ppermute(own, ("core", "ctx"), pairs))
    state = ()
    pieces = [None] * len(HOPS)
    token = own
    for n, i in enumerate(ORDER):
        if n == SPLIT:
            state = attend(doc_lengths, queries, own, pieces, ORDER[:n], (), False)
            token = (token, state)
        a, token = lax.optimization_barrier((arrived[i], token))
        pieces[i] = token = lax.all_gather(a, "core", axis=0, tiled=True)
    todo = ORDER[SPLIT:] if state else ORDER
    out = attend(doc_lengths, queries, own, pieces, todo, state, True)
    return out.reshape(query_heads.shape)


def solution(mesh):
    cut = Mesh(
        mesh.devices.reshape(2, 2, *mesh.devices.shape[1:]), ("zhi", "core", "ctx", "tp")
    )
    cache = P("ctx", ("zhi", "core", "tp"), None)
    heads = P("ctx", "tp", ("zhi", "core"))
    return jax.shard_map(
        shards, mesh=cut, in_specs=(heads, cache, cache, P()), out_specs=heads, check_vma=False
    )
```

time: 73.9 us -> 73.7 us (level)
  the two profiles are of different devices: /device:TPU:25 before, /device:TPU:19 now
where the time goes in v7:
time: 73.7 us; the launch traced here: 73.3 us
  blocking collectives  50 us (68%)
  Pallas kernels  12.8 us (17%)
  starting transfers between devices  9.63 us (13%)
  local copies, waits for them, and re-layouts  0.82 us (1%)
    all_to_all x1, blocking collectives, shards(): lax.all_to_all(send, ('zhi', 'tp'), split_axis=0, concat_axis=0, tiled=True)  26.7 us
    all_gather x5, blocking collectives, shards(): pieces[i] = token = lax.all_gather(a, 'core', axis=0, tiled=True)  18 us
    pallas_call x2, Pallas kernels, attend(): pl.pallas_call(kernel, out_shape=out if last else tuple((jax.ShapeDtypeSt...  12.8 us
    ppermute x5, starting transfers between devices, shards(): arrived.append(lax.ppermute(own, ('core', 'ctx'), pairs))  9.63 us
    all_gather x1, blocking collectives, shards(): own = lax.all_gather(half, 'core', axis=0, tiled=True)  5.27 us
  transfers between devices with their start and end apart: 5, of which 0 were waited for; matrix products, arithmetic and copies ran while one was open for 0% of the time, Pallas kernels for 8%

profile of v7, /device:TPU:19, one launch (start us, length us, event | category | flops | bytes accessed | tf_op | source)
XLA Modules:
  0.0 73.3 jit_solution(8112911016697879126)
XLA Ops:
  0.0 0.0 copy-start.1
  0.0 0.8 %copy.9 = bf16[2,8,8,128]{3,2,1,0:T(8,128)(2,1)S(1)} copy(bf16[2,8,8,128]{3,1,2,0:T(8,128)(2,1)} %bitcast.20) | data formatting | bytes 65536
  0.8 0.0 copy-done.1
  0.9 26.7 %all_to_all.5 = bf16[16,2,16,128]{3,2,1,0:T(8,128)(2,1)S(1)} all-to-all(bf16[16,2,16,128]{3,2,1,0:T(8,128)(2,1)S(1)} %copy.8), channel_id=1, replica_groups=mesh['zhi'=2,'core'=2,'ctx'=16,'tp'=8] {'zhi','tp'}, dimensions={0} | all-to-all | bytes 262144 | tf_op jit(solution)/shard_map/all_to_all | solution.py:249
  27.6 5.3 %all_gather.18.refs_2_ = bf16[32,2,16,128]{3,2,1,0:T(8,128)(2,1)S(1)} all-gather(bf16[16,2,16,128]{3,2,1,0:T(8,128)(2,1)S(1)} %all_to_all.5), channel_id=1, replica_groups=mesh['zhi'=2,'core'=2,'ctx'=16,'tp'=8] {'core'}, dimensions={0}, use_global_device_ids=true | all-gather | bytes 393216 | tf_op jit(solution)/shard_map/all_gather | solution.py:250
  32.9 0.0 copy-start
  32.9 2.9 %collective-permute-start = (bf16[32,2,16,128]{3,2,1,0:T(8,128)(2,1)S(1)}, bf16[32,2,16,128]{3,2,1,0:T(8,128)(2,1)S(1)}, u32[]{:S(2)}, u32[]{:S(2)}) collective-permute-start(bf16[32,2,16,128]{3,2,1,0:T(8,128)(2,1)S(1)} %all_gather.18.refs_2_), channel_id=1, source_target_pairs={{0,8},{8,16},{16,24},{24,32},{32,40},{40,48},{48,56},{56,64},{64,7... | collective-permute-start | bytes 786440 | tf_op jit(solution)/shard_map/ppermute | solution.py:256
  35.8 1.3 %collective-permute-start.1 = (bf16[32,2,16,128]{3,2,1,0:T(8,128)(2,1)S(1)}, bf16[32,2,16,128]{3,2,1,0:T(8,128)(2,1)S(1)}, u32[]{:S(2)}, u32[]{:S(2)}) collective-permute-start(bf16[32,2,16,128]{3,2,1,0:T(8,128)(2,1)S(1)} %all_gather.18.refs_2_), channel_id=1, source_target_pairs={{0,16},{8,24},{16,32},{24,40},{32,48},{40,56},{48,64},{56,72},{64,... | collective-permute-start | bytes 786440 | tf_op jit(solution)/shard_map/ppermute | solution.py:256
  37.1 0.7 collective-permute-start.4
  37.7 3.5 %collective-permute-start.3 = (bf16[32,2,16,128]{3,2,1,0:T(8,128)(2,1)S(1)}, bf16[32,2,16,128]{3,2,1,0:T(8,128)(2,1)S(1)}, u32[]{:S(2)}, u32[]{:S(2)}) collective-permute-start(bf16[32,2,16,128]{3,2,1,0:T(8,128)(2,1)S(1)} %all_gather.18.refs_2_), channel_id=1, source_target_pairs={{0,40},{8,48},{16,56},{24,64},{32,72},{40,80},{48,88},{56,96},{64,... | collective-permute-start | bytes 786440 | tf_op jit(solution)/shard_map/ppermute | solution.py:256
  41.2 1.3 %collective-permute-start.2 = (bf16[32,2,16,128]{3,2,1,0:T(8,128)(2,1)S(1)}, bf16[32,2,16,128]{3,2,1,0:T(8,128)(2,1)S(1)}, u32[]{:S(2)}, u32[]{:S(2)}) collective-permute-start(bf16[32,2,16,128]{3,2,1,0:T(8,128)(2,1)S(1)} %all_gather.18.refs_2_), channel_id=1, source_target_pairs={{0,24},{8,32},{16,40},{24,48},{32,56},{40,64},{48,72},{56,80},{64,... | collective-permute-start | bytes 786440 | tf_op jit(solution)/shard_map/ppermute | solution.py:256
  42.5 0.0 collective-permute-done
  42.5 6.4 %all_gather.19.refs_3_ = bf16[64,2,16,128]{3,2,1,0:T(8,128)(2,1)} all-gather(bf16[32,2,16,128]{3,2,1,0:T(8,128)(2,1)S(1)} %collective-permute-done), channel_id=1, replica_groups=mesh['zhi'=2,'core'=2,'ctx'=16,'tp'=8] {'core'}, dimensions={0}, use_global_device_ids=true | all-gather | bytes 786432 | tf_op jit(solution)/shard_map/all_gather | solution.py:265
  49.0 0.0 copy-done
  49.0 0.0 collective-permute-done.1
  49.0 2.9 %all_gather.20.refs_4_ = bf16[64,2,16,128]{3,2,1,0:T(8,128)(2,1)} all-gather(bf16[32,2,16,128]{3,2,1,0:T(8,128)(2,1)S(1)} %collective-permute-done.1), channel_id=1, replica_groups=mesh['zhi'=2,'core'=2,'ctx'=16,'tp'=8] {'core'}, dimensions={0}, use_global_device_ids=true | all-gather | bytes 786432 | tf_op jit(solution)/shard_map/all_gather | solution.py:265
  51.9 6.2 %attend_first.1 = (f32[1,1024]{1,0:T(1,128)}, f32[8,1024]{1,0:T(8,128)}, f32[128,1024]{1,0:T(8,128)}) custom-call(s32[4]{0:T(128)} %refs_0_.3, bf16[512,256]{1,0:T(8,128)(2,1)} %bitcast.16, bf16[32,2,16,128]{3,2,1,0:T(8,128)(2,1)} %copy-done, bf16[64,2,16,128]{3,2,1,0:T(8,128)(2,1)} %all_gather.19.refs_3_, bf16[64,2,16,128]{3,2,1,0:T(8,128)(2,1)} %all_gather.20.refs_4_), custom_call_target="tpu_custom_call" | custom-call | tf_op jit(solution)/shard_map/attend_first/pallas_call | solution.py:220
  58.1 0.0 collective-permute-done.4
  58.1 2.3 %all_gather.21.refs_7_ = bf16[64,2,16,128]{3,2,1,0:T(8,128)(2,1)} all-gather(bf16[32,2,16,128]{3,2,1,0:T(8,128)(2,1)S(1)} %collective-permute-done.4), channel_id=1, replica_groups=mesh['zhi'=2,'core'=2,'ctx'=16,'tp'=8] {'core'}, dimensions={0}, use_global_device_ids=true | all-gather | bytes 786432 | tf_op jit(solution)/shard_map/all_gather | solution.py:265
  60.5 0.0 collective-permute-done.3
  60.5 4.0 %all_gather.22.refs_6_ = bf16[64,2,16,128]{3,2,1,0:T(8,128)(2,1)} all-gather(bf16[32,2,16,128]{3,2,1,0:T(8,128)(2,1)S(1)} %collective-permute-done.3), channel_id=1, replica_groups=mesh['zhi'=2,'core'=2,'ctx'=16,'tp'=8] {'core'}, dimensions={0}, use_global_device_ids=true | all-gather | bytes 786432 | tf_op jit(solution)/shard_map/all_gather | solution.py:265
  64.4 0.0 collective-permute-done.2
  64.4 2.3 %all_gather.23.refs_5_ = bf16[64,2,16,128]{3,2,1,0:T(8,128)(2,1)} all-gather(bf16[32,2,16,128]{3,2,1,0:T(8,128)(2,1)S(1)} %collective-permute-done.2), channel_id=1, replica_groups=mesh['zhi'=2,'core'=2,'ctx'=16,'tp'=8] {'core'}, dimensions={0}, use_global_device_ids=true | all-gather | bytes 786432 | tf_op jit(solution)/shard_map/all_gather | solution.py:265
  66.7 6.5 %attend_last.1 = bf16[512,256]{1,0:T(8,128)(2,1)} custom-call(s32[4]{0:T(128)} %refs_0_.3, bf16[512,256]{1,0:T(8,128)(2,1)} %bitcast.17, bf16[32,2,16,128]{3,2,1,0:T(8,128)(2,1)} %copy-done, bf16[64,2,16,128]{3,2,1,0:T(8,128)(2,1)} %all_gather.19.refs_3_, bf16[64,2,16,128]{3,2,1,0:T(8,128)(2,1)} %all_gather.20.refs_4_, ...), custom_call_target="tpu_custom_call" | custom-call | tf_op jit(solution)/shard_map/attend_last/pallas_call | solution.py:220
  (3 shorter events, 0.1 us)
Async XLA Ops:
  0.0 0.8 %copy-start.1 = (bf16[1,16,1024]{2,1,0:T(8,128)(2,1)S(1)}, bf16[1,16,1024]{2,1,0:T(8,128)(2,1)}, u32[]{:S(2)}) copy-start(bf16[1,16,1024]{2,1,0:T(8,128)(2,1)} %param.6) | copy-start | bytes 98308
  32.9 16.1 %copy-start = (bf16[32,2,16,128]{3,2,1,0:T(8,128)(2,1)}, bf16[32,2,16,128]{3,2,1,0:T(8,128)(2,1)S(1)}, u32[]{:S(2)}) copy-start(bf16[32,2,16,128]{3,2,1,0:T(8,128)(2,1)S(1)} %all_gather.18.refs_2_) | copy-start | bytes 786436
  32.9 9.7 %collective-permute-start = (bf16[32,2,16,128]{3,2,1,0:T(8,128)(2,1)S(1)}, bf16[32,2,16,128]{3,2,1,0:T(8,128)(2,1)S(1)}, u32[]{:S(2)}, u32[]{:S(2)}) collective-permute-start(bf16[32,2,16,128]{3,2,1,0:T(8,128)(2,1)S(1)} %all_gather.18.refs_2_), channel_id=1, source_target_pairs={{0,8},{8,16},{16,24},{24,32},{32,40},{40,48},{48,56},{56,64},{64,7... | collective-permute-start | bytes 786440 | tf_op jit(solution)/shard_map/ppermute | solution.py:256
  35.8 13.2 %collective-permute-start.1 = (bf16[32,2,16,128]{3,2,1,0:T(8,128)(2,1)S(1)}, bf16[32,2,16,128]{3,2,1,0:T(8,128)(2,1)S(1)}, u32[]{:S(2)}, u32[]{:S(2)}) collective-permute-start(bf16[32,2,16,128]{3,2,1,0:T(8,128)(2,1)S(1)} %all_gather.18.refs_2_), channel_id=1, source_target_pairs={{0,16},{8,24},{16,32},{24,40},{32,48},{40,56},{48,64},{56,72},{64,... | collective-permute-start | bytes 786440 | tf_op jit(solution)/shard_map/ppermute | solution.py:256
  37.1 21.1 %collective-permute-start.4 = (bf16[32,2,16,128]{3,2,1,0:T(8,128)(2,1)S(1)}, bf16[32,2,16,128]{3,2,1,0:T(8,128)(2,1)S(1)}, u32[]{:S(2)}, u32[]{:S(2)}) collective-permute-start(bf16[32,2,16,128]{3,2,1,0:T(8,128)(2,1)S(1)} %all_gather.18.refs_2_), channel_id=1, source_target_pairs={{0,72},{8,80},{16,88},{24,96},{32,104},{40,112},{48,120},{128,208}... | collective-permute-start | bytes 786440 | tf_op jit(solution)/shard_map/ppermute | solution.py:256
  37.7 22.7 %collective-permute-start.3 = (bf16[32,2,16,128]{3,2,1,0:T(8,128)(2,1)S(1)}, bf16[32,2,16,128]{3,2,1,0:T(8,128)(2,1)S(1)}, u32[]{:S(2)}, u32[]{:S(2)}) collective-permute-start(bf16[32,2,16,128]{3,2,1,0:T(8,128)(2,1)S(1)} %all_gather.18.refs_2_), channel_id=1, source_target_pairs={{0,40},{8,48},{16,56},{24,64},{32,72},{40,80},{48,88},{56,96},{64,... | collective-permute-start | bytes 786440 | tf_op jit(solution)/shard_map/ppermute | solution.py:256
  41.2 23.2 %collective-permute-start.2 = (bf16[32,2,16,128]{3,2,1,0:T(8,128)(2,1)S(1)}, bf16[32,2,16,128]{3,2,1,0:T(8,128)(2,1)S(1)}, u32[]{:S(2)}, u32[]{:S(2)}) collective-permute-start(bf16[32,2,16,128]{3,2,1,0:T(8,128)(2,1)S(1)} %all_gather.18.refs_2_), channel_id=1, source_target_pairs={{0,24},{8,32},{16,40},{24,48},{32,56},{40,64},{48,72},{56,80},{64,... | collective-permute-start | bytes 786440 | tf_op jit(solution)/shard_map/ppermute | solution.py:256

commit v8 on v7

--- a/solution.py
+++ b/solution.py
@@ -40,12 +40,6 @@
     return (n & 127) + ((n >> 7) & 1) * 256 + (n >> 8) * 128
 
 
-def stack_heads(q_ref, stacked_ref):
-    rows, width = q_ref.shape
-    for h in range(width // HD):
-        stacked_ref[h * rows : (h + 1) * rows] = q_ref[:, h * HD : (h + 1) * HD]
-
-
 def score(keys, queries):
     return lax.dot_general(
         keys, queries, (((1,), (1,)), ((), ())), preferred_element_type=jnp.float32
@@ -68,7 +62,7 @@
 
 def attend_kernel(todo, first, last, lengths_ref, q_ref, own_ref, pieces, before, out_ref, state, scratch):
     m_ref, l_ref, acc_ref = state
-    stacked_ref, buf_ref, sems = scratch
+    stacked_ref, buf_ref, sems, lead_sems = scratch
     rows, width = q_ref.shape
     heads = width // HD
     block = lax.axis_index("ctx")
@@ -90,10 +84,23 @@
                     )
                     copy.start() if begin else copy.wait()
 
+    lead = [
+        pltpu.make_async_copy(
+            q_ref.at[:, h * HD : (h + 1) * HD],
+            stacked_ref.at[h * rows : (h + 1) * rows],
+            lead_sems.at[h],
+        )
+        for h in range(heads)
+    ]
+    lead += [
+        pltpu.make_async_copy(was, ref, lead_sems.at[heads + n])
+        for n, (was, ref) in enumerate(zip(before, state))
+    ]
+    for copy in lead:
+        copy.start()
     if first:
         own_copy().start()
     fetch(todo, True)
-    stack_heads(q_ref, stacked_ref)
     query = block * rows + lax.broadcasted_iota(jnp.int32, (1, rows), 1)
     row_begin = start_of(query, starts)
     begin = jnp.concatenate([row_begin] * heads, axis=1)
@@ -117,12 +124,11 @@
             l_ref[:, at] = fold(weights)
             acc_ref[:, at] = mix(values, weights)
 
+    for copy in lead:
+        copy.wait()
     if first:
         own_copy().wait()
         visit_own()
-    else:
-        for ref, was in zip(state, before):
-            ref[...] = was[...]
 
     def step(n, carry):
         k = hops[0]
@@ -220,15 +226,15 @@
     return pl.pallas_call(
         kernel,
         out_shape=out if last else tuple(jax.ShapeDtypeStruct(n, jnp.float32) for n in sums),
-        in_specs=[pl.BlockSpec(memory_space=pltpu.SMEM), vmem]
-        + [pl.BlockSpec(memory_space=pl.ANY)] * (1 + len(place))
-        + [vmem] * len(state),
+        in_specs=[pl.BlockSpec(memory_space=pltpu.SMEM)]
+        + [pl.BlockSpec(memory_space=pl.ANY)] * (2 + len(place) + len(state)),
         out_specs=vmem if last else (vmem,) * 3,
         scratch_shapes=([pltpu.VMEM(n, jnp.float32) for n in sums] if last else [])
         + [
             pltpu.VMEM((columns, HD), jnp.bfloat16),
             pltpu.VMEM((1 + 2 * len(HOPS), *own.shape), jnp.bfloat16),
             pltpu.SemaphoreType.DMA((1 + 2 * len(HOPS),)),
+            pltpu.SemaphoreType.DMA((width // HD + len(sums),)),
         ],
         name="attend_last" if last else "attend_first",
     )(lengths, queries, own, *[pieces[i] for i in place], *state)

time: 73.7 us -> 73.9 us (level)
  transfers between devices with their start and end apart: 5 -> 5, of which waited for: 0 -> 0; matrix products, arithmetic and copies ran while one was open for 0% -> 0% of each run, Pallas kernels for 8% -> 9%
where the time goes in v8:
time: 73.9 us; the launch traced here: 73.5 us
  blocking collectives  49.4 us (67%)
  Pallas kernels  13.5 us (18%)
  starting transfers between devices  9.63 us (13%)
  local copies, waits for them, and re-layouts  0.82 us (1%)
    all_to_all x1, blocking collectives, shards(): lax.all_to_all(send, ('zhi', 'tp'), split_axis=0, concat_axis=0, tiled=True)  26.7 us
    all_gather x5, blocking collectives, shards(): pieces[i] = token = lax.all_gather(a, 'core', axis=0, tiled=True)  17.4 us
    pallas_call x2, Pallas kernels, attend(): pl.pallas_call(kernel, out_shape=out if last else tuple((jax.ShapeDtypeSt...  13.5 us
    ppermute x5, starting transfers between devices, shards(): arrived.append(lax.ppermute(own, ('core', 'ctx'), pairs))  9.63 us
    all_gather x1, blocking collectives, shards(): own = lax.all_gather(half, 'core', axis=0, tiled=True)  5.27 us
  transfers between devices with their start and end apart: 5, of which 0 were waited for; matrix products, arithmetic and copies ran while one was open for 0% of the time, Pallas kernels for 9%

profile of v8, /device:TPU:19, one launch (start us, length us, event | category | flops | bytes accessed | tf_op | source)
XLA Modules:
  0.0 73.5 jit_solution(3766757560940670910)
XLA Ops:
  0.0 0.0 copy-start.1
  0.0 0.8 %copy.9 = bf16[2,8,8,128]{3,2,1,0:T(8,128)(2,1)S(1)} copy(bf16[2,8,8,128]{3,1,2,0:T(8,128)(2,1)} %bitcast.20) | data formatting | bytes 65536
  0.8 0.0 copy-done.1
  0.9 26.7 %all_to_all.5 = bf16[16,2,16,128]{3,2,1,0:T(8,128)(2,1)S(1)} all-to-all(bf16[16,2,16,128]{3,2,1,0:T(8,128)(2,1)S(1)} %copy.8), channel_id=1, replica_groups=mesh['zhi'=2,'core'=2,'ctx'=16,'tp'=8] {'zhi','tp'}, dimensions={0} | all-to-all | bytes 262144 | tf_op jit(solution)/shard_map/all_to_all | solution.py:255
  27.6 5.3 %all_gather.18.refs_2_ = bf16[32,2,16,128]{3,2,1,0:T(8,128)(2,1)S(1)} all-gather(bf16[16,2,16,128]{3,2,1,0:T(8,128)(2,1)S(1)} %all_to_all.5), channel_id=1, replica_groups=mesh['zhi'=2,'core'=2,'ctx'=16,'tp'=8] {'core'}, dimensions={0}, use_global_device_ids=true | all-gather | bytes 393216 | tf_op jit(solution)/shard_map/all_gather | solution.py:256
  32.9 0.0 copy-start
  32.9 2.9 %collective-permute-start = (bf16[32,2,16,128]{3,2,1,0:T(8,128)(2,1)S(1)}, bf16[32,2,16,128]{3,2,1,0:T(8,128)(2,1)S(1)}, u32[]{:S(2)}, u32[]{:S(2)}) collective-permute-start(bf16[32,2,16,128]{3,2,1,0:T(8,128)(2,1)S(1)} %all_gather.18.refs_2_), channel_id=1, source_target_pairs={{0,8},{8,16},{16,24},{24,32},{32,40},{40,48},{48,56},{56,64},{64,7... | collective-permute-start | bytes 786440 | tf_op jit(solution)/shard_map/ppermute | solution.py:262
  35.8 1.3 %collective-permute-start.1 = (bf16[32,2,16,128]{3,2,1,0:T(8,128)(2,1)S(1)}, bf16[32,2,16,128]{3,2,1,0:T(8,128)(2,1)S(1)}, u32[]{:S(2)}, u32[]{:S(2)}) collective-permute-start(bf16[32,2,16,128]{3,2,1,0:T(8,128)(2,1)S(1)} %all_gather.18.refs_2_), channel_id=1, source_target_pairs={{0,16},{8,24},{16,32},{24,40},{32,48},{40,56},{48,64},{56,72},{64,... | collective-permute-start | bytes 786440 | tf_op jit(solution)/shard_map/ppermute | solution.py:262
  37.1 0.7 collective-permute-start.4
  37.7 3.5 %collective-permute-start.3 = (bf16[32,2,16,128]{3,2,1,0:T(8,128)(2,1)S(1)}, bf16[32,2,16,128]{3,2,1,0:T(8,128)(2,1)S(1)}, u32[]{:S(2)}, u32[]{:S(2)}) collective-permute-start(bf16[32,2,16,128]{3,2,1,0:T(8,128)(2,1)S(1)} %all_gather.18.refs_2_), channel_id=1, source_target_pairs={{0,40},{8,48},{16,56},{24,64},{32,72},{40,80},{48,88},{56,96},{64,... | collective-permute-start | bytes 786440 | tf_op jit(solution)/shard_map/ppermute | solution.py:262
  41.2 1.3 %collective-permute-start.2 = (bf16[32,2,16,128]{3,2,1,0:T(8,128)(2,1)S(1)}, bf16[32,2,16,128]{3,2,1,0:T(8,128)(2,1)S(1)}, u32[]{:S(2)}, u32[]{:S(2)}) collective-permute-start(bf16[32,2,16,128]{3,2,1,0:T(8,128)(2,1)S(1)} %all_gather.18.refs_2_), channel_id=1, source_target_pairs={{0,24},{8,32},{16,40},{24,48},{32,56},{40,64},{48,72},{56,80},{64,... | collective-permute-start | bytes 786440 | tf_op jit(solution)/shard_map/ppermute | solution.py:262
  42.5 0.0 collective-permute-done
  42.5 6.4 %all_gather.19.refs_3_ = bf16[64,2,16,128]{3,2,1,0:T(8,128)(2,1)} all-gather(bf16[32,2,16,128]{3,2,1,0:T(8,128)(2,1)S(1)} %collective-permute-done), channel_id=1, replica_groups=mesh['zhi'=2,'core'=2,'ctx'=16,'tp'=8] {'core'}, dimensions={0}, use_global_device_ids=true | all-gather | bytes 786432 | tf_op jit(solution)/shard_map/all_gather | solution.py:271
  49.0 0.0 copy-done
  49.0 0.0 collective-permute-done.1
  49.0 2.9 %all_gather.20.refs_4_ = bf16[64,2,16,128]{3,2,1,0:T(8,128)(2,1)} all-gather(bf16[32,2,16,128]{3,2,1,0:T(8,128)(2,1)S(1)} %collective-permute-done.1), channel_id=1, replica_groups=mesh['zhi'=2,'core'=2,'ctx'=16,'tp'=8] {'core'}, dimensions={0}, use_global_device_ids=true | all-gather | bytes 786432 | tf_op jit(solution)/shard_map/all_gather | solution.py:271
  51.9 6.7 %attend_first.1 = (f32[1,1024]{1,0:T(1,128)}, f32[8,1024]{1,0:T(8,128)}, f32[128,1024]{1,0:T(8,128)}) custom-call(s32[4]{0:T(128)} %refs_0_.3, bf16[512,256]{1,0:T(8,128)(2,1)} %bitcast.16, bf16[32,2,16,128]{3,2,1,0:T(8,128)(2,1)} %copy-done, bf16[64,2,16,128]{3,2,1,0:T(8,128)(2,1)} %all_gather.19.refs_3_, bf16[64,2,16,128]{3,2,1,0:T(8,128)(2,1)} %all_gather.20.refs_4_), custom_call_target="tpu_custom_call" | custom-call | tf_op jit(solution)/shard_map/attend_first/pallas_call | solution.py:226
  58.7 0.0 collective-permute-done.4
  58.7 2.3 %all_gather.21.refs_7_ = bf16[64,2,16,128]{3,2,1,0:T(8,128)(2,1)} all-gather(bf16[32,2,16,128]{3,2,1,0:T(8,128)(2,1)S(1)} %collective-permute-done.4), channel_id=1, replica_groups=mesh['zhi'=2,'core'=2,'ctx'=16,'tp'=8] {'core'}, dimensions={0}, use_global_device_ids=true | all-gather | bytes 786432 | tf_op jit(solution)/shard_map/all_gather | solution.py:271
  61.0 0.0 collective-permute-done.3
  61.0 3.5 %all_gather.22.refs_6_ = bf16[64,2,16,128]{3,2,1,0:T(8,128)(2,1)} all-gather(bf16[32,2,16,128]{3,2,1,0:T(8,128)(2,1)S(1)} %collective-permute-done.3), channel_id=1, replica_groups=mesh['zhi'=2,'core'=2,'ctx'=16,'tp'=8] {'core'}, dimensions={0}, use_global_device_ids=true | all-gather | bytes 786432 | tf_op jit(solution)/shard_map/all_gather | solution.py:271
  64.4 0.0 collective-permute-done.2
  64.4 2.3 %all_gather.23.refs_5_ = bf16[64,2,16,128]{3,2,1,0:T(8,128)(2,1)} all-gather(bf16[32,2,16,128]{3,2,1,0:T(8,128)(2,1)S(1)} %collective-permute-done.2), channel_id=1, replica_groups=mesh['zhi'=2,'core'=2,'ctx'=16,'tp'=8] {'core'}, dimensions={0}, use_global_device_ids=true | all-gather | bytes 786432 | tf_op jit(solution)/shard_map/all_gather | solution.py:271
  66.7 6.7 %attend_last.1 = bf16[512,256]{1,0:T(8,128)(2,1)} custom-call(s32[4]{0:T(128)} %refs_0_.3, bf16[512,256]{1,0:T(8,128)(2,1)} %bitcast.17, bf16[32,2,16,128]{3,2,1,0:T(8,128)(2,1)} %copy-done, bf16[64,2,16,128]{3,2,1,0:T(8,128)(2,1)} %all_gather.19.refs_3_, bf16[64,2,16,128]{3,2,1,0:T(8,128)(2,1)} %all_gather.20.refs_4_, ...), custom_call_target="tpu_custom_call" | custom-call | tf_op jit(solution)/shard_map/attend_last/pallas_call | solution.py:226
  (3 shorter events, 0.1 us)
Async XLA Ops:
  0.0 0.8 %copy-start.1 = (bf16[1,16,1024]{2,1,0:T(8,128)(2,1)S(1)}, bf16[1,16,1024]{2,1,0:T(8,128)(2,1)}, u32[]{:S(2)}) copy-start(bf16[1,16,1024]{2,1,0:T(8,128)(2,1)} %param.6) | copy-start | bytes 98308
  32.9 16.1 %copy-start = (bf16[32,2,16,128]{3,2,1,0:T(8,128)(2,1)}, bf16[32,2,16,128]{3,2,1,0:T(8,128)(2,1)S(1)}, u32[]{:S(2)}) copy-start(bf16[32,2,16,128]{3,2,1,0:T(8,128)(2,1)S(1)} %all_gather.18.refs_2_) | copy-start | bytes 786436
  32.9 9.7 %collective-permute-start = (bf16[32,2,16,128]{3,2,1,0:T(8,128)(2,1)S(1)}, bf16[32,2,16,128]{3,2,1,0:T(8,128)(2,1)S(1)}, u32[]{:S(2)}, u32[]{:S(2)}) collective-permute-start(bf16[32,2,16,128]{3,2,1,0:T(8,128)(2,1)S(1)} %all_gather.18.refs_2_), channel_id=1, source_target_pairs={{0,8},{8,16},{16,24},{24,32},{32,40},{40,48},{48,56},{56,64},{64,7... | collective-permute-start | bytes 786440 | tf_op jit(solution)/shard_map/ppermute | solution.py:262
  35.8 13.2 %collective-permute-start.1 = (bf16[32,2,16,128]{3,2,1,0:T(8,128)(2,1)S(1)}, bf16[32,2,16,128]{3,2,1,0:T(8,128)(2,1)S(1)}, u32[]{:S(2)}, u32[]{:S(2)}) collective-permute-start(bf16[32,2,16,128]{3,2,1,0:T(8,128)(2,1)S(1)} %all_gather.18.refs_2_), channel_id=1, source_target_pairs={{0,16},{8,24},{16,32},{24,40},{32,48},{40,56},{48,64},{56,72},{64,... | collective-permute-start | bytes 786440 | tf_op jit(solution)/shard_map/ppermute | solution.py:262
  37.1 21.6 %collective-permute-start.4 = (bf16[32,2,16,128]{3,2,1,0:T(8,128)(2,1)S(1)}, bf16[32,2,16,128]{3,2,1,0:T(8,128)(2,1)S(1)}, u32[]{:S(2)}, u32[]{:S(2)}) collective-permute-start(bf16[32,2,16,128]{3,2,1,0:T(8,128)(2,1)S(1)} %all_gather.18.refs_2_), channel_id=1, source_target_pairs={{0,72},{8,80},{16,88},{24,96},{32,104},{40,112},{48,120},{128,208}... | collective-permute-start | bytes 786440 | tf_op jit(solution)/shard_map/ppermute | solution.py:262
  37.7 23.2 %collective-permute-start.3 = (bf16[32,2,16,128]{3,2,1,0:T(8,128)(2,1)S(1)}, bf16[32,2,16,128]{3,2,1,0:T(8,128)(2,1)S(1)}, u32[]{:S(2)}, u32[]{:S(2)}) collective-permute-start(bf16[32,2,16,128]{3,2,1,0:T(8,128)(2,1)S(1)} %all_gather.18.refs_2_), channel_id=1, source_target_pairs={{0,40},{8,48},{16,56},{24,64},{32,72},{40,80},{48,88},{56,96},{64,... | collective-permute-start | bytes 786440 | tf_op jit(solution)/shard_map/ppermute | solution.py:262
  41.2 23.2 %collective-permute-start.2 = (bf16[32,2,16,128]{3,2,1,0:T(8,128)(2,1)S(1)}, bf16[32,2,16,128]{3,2,1,0:T(8,128)(2,1)S(1)}, u32[]{:S(2)}, u32[]{:S(2)}) collective-permute-start(bf16[32,2,16,128]{3,2,1,0:T(8,128)(2,1)S(1)} %all_gather.18.refs_2_), channel_id=1, source_target_pairs={{0,24},{8,32},{16,40},{24,48},{32,56},{40,64},{48,72},{56,80},{64,... | collective-permute-start | bytes 786440 | tf_op jit(solution)/shard_map/ppermute | solution.py:262

commit v9 on v8

--- a/solution.py
+++ b/solution.py
@@ -130,27 +130,36 @@
         own_copy().wait()
         visit_own()
 
+    def is_cut(base):
+        cut = False
+        for s in starts:
+            cut = cut | ((s > base) & (s < base + rows))
+        return cut
+
+    for k in hops:
+
+        @pl.when(k <= count)
+        def _():
+            pltpu.make_async_copy(
+                pieces[todo[0]].at[0:part], buf_ref.at[k], sems.at[k]
+            ).wait()
+
+            @pl.when(jnp.logical_not(is_cut((block - k) * rows)))
+            def _():
+                keys, values, base = load(k)
+                top = jnp.where(begin <= base, m_ref[...], NEVER)
+                weights = jnp.exp2((score(keys, stacked_ref[...]) - top) * STEP)
+                l_ref[...] += fold(weights)
+                acc_ref[...] += mix(values, weights)
+
     def step(n, carry):
         k = hops[0]
         for i, hop in enumerate(hops[1:]):
             k = jnp.where(n > i, hop, k)
-        pltpu.make_async_copy(
-            pieces[todo[0]].at[0:part], buf_ref.at[k], sems.at[k]
-        ).wait()
-        keys, values, base = load(k)
-        cut = False
-        for s in starts:
-            cut = cut | ((s > base) & (s < base + rows))
-
-        @pl.when(jnp.logical_not(cut))
+
+        @pl.when(is_cut((block - k) * rows))
         def _():
-            top = jnp.where(begin <= base, m_ref[...], NEVER)
-            weights = jnp.exp2((score(keys, stacked_ref[...]) - top) * STEP)
-            l_ref[...] += fold(weights)
-            acc_ref[...] += mix(values, weights)
-
-        @pl.when(cut)
-        def _():
+            keys, values, base = load(k)
             key = key_rows((rows, rows)) + base
             for h in range(heads):
                 at = slice(h * rows, (h + 1) * rows)

time: 73.9 us -> 74 us (level)
  no operation moved by 1% of the time
where the time goes in v9:
time: 74 us; the launch traced here: 73.5 us
  blocking collectives  49.4 us (67%)
  Pallas kernels  13.6 us (18%)
  starting transfers between devices  9.63 us (13%)
  local copies, waits for them, and re-layouts  0.82 us (1%)
    all_to_all x1, blocking collectives, shards(): lax.all_to_all(send, ('zhi', 'tp'), split_axis=0, concat_axis=0, tiled=True)  26.7 us
    all_gather x5, blocking collectives, shards(): pieces[i] = token = lax.all_gather(a, 'core', axis=0, tiled=True)  17.4 us
    pallas_call x2, Pallas kernels, attend(): pl.pallas_call(kernel, out_shape=out if last else tuple((jax.ShapeDtypeSt...  13.6 us
    ppermute x5, starting transfers between devices, shards(): arrived.append(lax.ppermute(own, ('core', 'ctx'), pairs))  9.63 us
    all_gather x1, blocking collectives, shards(): own = lax.all_gather(half, 'core', axis=0, tiled=True)  5.27 us
  transfers between devices with their start and end apart: 5, of which 0 were waited for; matrix products, arithmetic and copies ran while one was open for 0% of the time, Pallas kernels for 9%

profile of v9, /device:TPU:19, one launch (start us, length us, event | category | flops | bytes accessed | tf_op | source)
XLA Modules:
  0.0 73.5 jit_solution(6409366467170093611)
XLA Ops:
  0.0 0.0 copy-start.1
  0.0 0.8 %copy.9 = bf16[2,8,8,128]{3,2,1,0:T(8,128)(2,1)S(1)} copy(bf16[2,8,8,128]{3,1,2,0:T(8,128)(2,1)} %bitcast.20) | data formatting | bytes 65536
  0.8 0.0 copy-done.1
  0.9 26.7 %all_to_all.5 = bf16[16,2,16,128]{3,2,1,0:T(8,128)(2,1)S(1)} all-to-all(bf16[16,2,16,128]{3,2,1,0:T(8,128)(2,1)S(1)} %copy.8), channel_id=1, replica_groups=mesh['zhi'=2,'core'=2,'ctx'=16,'tp'=8] {'zhi','tp'}, dimensions={0} | all-to-all | bytes 262144 | tf_op jit(solution)/shard_map/all_to_all | solution.py:264
  27.6 5.3 %all_gather.18.refs_2_ = bf16[32,2,16,128]{3,2,1,0:T(8,128)(2,1)S(1)} all-gather(bf16[16,2,16,128]{3,2,1,0:T(8,128)(2,1)S(1)} %all_to_all.5), channel_id=1, replica_groups=mesh['zhi'=2,'core'=2,'ctx'=16,'tp'=8] {'core'}, dimensions={0}, use_global_device_ids=true | all-gather | bytes 393216 | tf_op jit(solution)/shard_map/all_gather | solution.py:265
  32.9 0.0 copy-start
  32.9 2.9 %collective-permute-start = (bf16[32,2,16,128]{3,2,1,0:T(8,128)(2,1)S(1)}, bf16[32,2,16,128]{3,2,1,0:T(8,128)(2,1)S(1)}, u32[]{:S(2)}, u32[]{:S(2)}) collective-permute-start(bf16[32,2,16,128]{3,2,1,0:T(8,128)(2,1)S(1)} %all_gather.18.refs_2_), channel_id=1, source_target_pairs={{0,8},{8,16},{16,24},{24,32},{32,40},{40,48},{48,56},{56,64},{64,7... | collective-permute-start | bytes 786440 | tf_op jit(solution)/shard_map/ppermute | solution.py:271
  35.8 1.3 %collective-permute-start.1 = (bf16[32,2,16,128]{3,2,1,0:T(8,128)(2,1)S(1)}, bf16[32,2,16,128]{3,2,1,0:T(8,128)(2,1)S(1)}, u32[]{:S(2)}, u32[]{:S(2)}) collective-permute-start(bf16[32,2,16,128]{3,2,1,0:T(8,128)(2,1)S(1)} %all_gather.18.refs_2_), channel_id=1, source_target_pairs={{0,16},{8,24},{16,32},{24,40},{32,48},{40,56},{48,64},{56,72},{64,... | collective-permute-start | bytes 786440 | tf_op jit(solution)/shard_map/ppermute | solution.py:271
  37.1 0.7 collective-permute-start.4
  37.7 3.5 %collective-permute-start.3 = (bf16[32,2,16,128]{3,2,1,0:T(8,128)(2,1)S(1)}, bf16[32,2,16,128]{3,2,1,0:T(8,128)(2,1)S(1)}, u32[]{:S(2)}, u32[]{:S(2)}) collective-permute-start(bf16[32,2,16,128]{3,2,1,0:T(8,128)(2,1)S(1)} %all_gather.18.refs_2_), channel_id=1, source_target_pairs={{0,40},{8,48},{16,56},{24,64},{32,72},{40,80},{48,88},{56,96},{64,... | collective-permute-start | bytes 786440 | tf_op jit(solution)/shard_map/ppermute | solution.py:271
  41.2 1.3 %collective-permute-start.2 = (bf16[32,2,16,128]{3,2,1,0:T(8,128)(2,1)S(1)}, bf16[32,2,16,128]{3,2,1,0:T(8,128)(2,1)S(1)}, u32[]{:S(2)}, u32[]{:S(2)}) collective-permute-start(bf16[32,2,16,128]{3,2,1,0:T(8,128)(2,1)S(1)} %all_gather.18.refs_2_), channel_id=1, source_target_pairs={{0,24},{8,32},{16,40},{24,48},{32,56},{40,64},{48,72},{56,80},{64,... | collective-permute-start | bytes 786440 | tf_op jit(solution)/shard_map/ppermute | solution.py:271
  42.5 0.0 collective-permute-done
  42.5 6.4 %all_gather.19.refs_3_ = bf16[64,2,16,128]{3,2,1,0:T(8,128)(2,1)} all-gather(bf16[32,2,16,128]{3,2,1,0:T(8,128)(2,1)S(1)} %collective-permute-done), channel_id=1, replica_groups=mesh['zhi'=2,'core'=2,'ctx'=16,'tp'=8] {'core'}, dimensions={0}, use_global_device_ids=true | all-gather | bytes 786432 | tf_op jit(solution)/shard_map/all_gather | solution.py:280
  49.0 0.0 copy-done
  49.0 0.0 collective-permute-done.1
  49.0 2.9 %all_gather.20.refs_4_ = bf16[64,2,16,128]{3,2,1,0:T(8,128)(2,1)} all-gather(bf16[32,2,16,128]{3,2,1,0:T(8,128)(2,1)S(1)} %collective-permute-done.1), channel_id=1, replica_groups=mesh['zhi'=2,'core'=2,'ctx'=16,'tp'=8] {'core'}, dimensions={0}, use_global_device_ids=true | all-gather | bytes 786432 | tf_op jit(solution)/shard_map/all_gather | solution.py:280
  51.9 6.8 %attend_first.1 = (f32[1,1024]{1,0:T(1,128)}, f32[8,1024]{1,0:T(8,128)}, f32[128,1024]{1,0:T(8,128)}) custom-call(s32[4]{0:T(128)} %refs_0_.3, bf16[512,256]{1,0:T(8,128)(2,1)} %bitcast.16, bf16[32,2,16,128]{3,2,1,0:T(8,128)(2,1)} %copy-done, bf16[64,2,16,128]{3,2,1,0:T(8,128)(2,1)} %all_gather.19.refs_3_, bf16[64,2,16,128]{3,2,1,0:T(8,128)(2,1)} %all_gather.20.refs_4_), custom_call_target="tpu_custom_call" | custom-call | tf_op jit(solution)/shard_map/attend_first/pallas_call | solution.py:235
  58.7 0.0 collective-permute-done.4
  58.7 2.3 %all_gather.21.refs_7_ = bf16[64,2,16,128]{3,2,1,0:T(8,128)(2,1)} all-gather(bf16[32,2,16,128]{3,2,1,0:T(8,128)(2,1)S(1)} %collective-permute-done.4), channel_id=1, replica_groups=mesh['zhi'=2,'core'=2,'ctx'=16,'tp'=8] {'core'}, dimensions={0}, use_global_device_ids=true | all-gather | bytes 786432 | tf_op jit(solution)/shard_map/all_gather | solution.py:280
  61.0 0.0 collective-permute-done.3
  61.0 3.4 %all_gather.22.refs_6_ = bf16[64,2,16,128]{3,2,1,0:T(8,128)(2,1)} all-gather(bf16[32,2,16,128]{3,2,1,0:T(8,128)(2,1)S(1)} %collective-permute-done.3), channel_id=1, replica_groups=mesh['zhi'=2,'core'=2,'ctx'=16,'tp'=8] {'core'}, dimensions={0}, use_global_device_ids=true | all-gather | bytes 786432 | tf_op jit(solution)/shard_map/all_gather | solution.py:280
  64.4 0.0 collective-permute-done.2
  64.4 2.3 %all_gather.23.refs_5_ = bf16[64,2,16,128]{3,2,1,0:T(8,128)(2,1)} all-gather(bf16[32,2,16,128]{3,2,1,0:T(8,128)(2,1)S(1)} %collective-permute-done.2), channel_id=1, replica_groups=mesh['zhi'=2,'core'=2,'ctx'=16,'tp'=8] {'core'}, dimensions={0}, use_global_device_ids=true | all-gather | bytes 786432 | tf_op jit(solution)/shard_map/all_gather | solution.py:280
  66.7 6.8 %attend_last.1 = bf16[512,256]{1,0:T(8,128)(2,1)} custom-call(s32[4]{0:T(128)} %refs_0_.3, bf16[512,256]{1,0:T(8,128)(2,1)} %bitcast.17, bf16[32,2,16,128]{3,2,1,0:T(8,128)(2,1)} %copy-done, bf16[64,2,16,128]{3,2,1,0:T(8,128)(2,1)} %all_gather.19.refs_3_, bf16[64,2,16,128]{3,2,1,0:T(8,128)(2,1)} %all_gather.20.refs_4_, ...), custom_call_target="tpu_custom_call" | custom-call | tf_op jit(solution)/shard_map/attend_last/pallas_call | solution.py:235
  (3 shorter events, 0.1 us)
Async XLA Ops:
  0.0 0.8 %copy-start.1 = (bf16[1,16,1024]{2,1,0:T(8,128)(2,1)S(1)}, bf16[1,16,1024]{2,1,0:T(8,128)(2,1)}, u32[]{:S(2)}) copy-start(bf16[1,16,1024]{2,1,0:T(8,128)(2,1)} %param.6) | copy-start | bytes 98308
  32.9 16.1 %copy-start = (bf16[32,2,16,128]{3,2,1,0:T(8,128)(2,1)}, bf16[32,2,16,128]{3,2,1,0:T(8,128)(2,1)S(1)}, u32[]{:S(2)}) copy-start(bf16[32,2,16,128]{3,2,1,0:T(8,128)(2,1)S(1)} %all_gather.18.refs_2_) | copy-start | bytes 786436
  32.9 9.7 %collective-permute-start = (bf16[32,2,16,128]{3,2,1,0:T(8,128)(2,1)S(1)}, bf16[32,2,16,128]{3,2,1,0:T(8,128)(2,1)S(1)}, u32[]{:S(2)}, u32[]{:S(2)}) collective-permute-start(bf16[32,2,16,128]{3,2,1,0:T(8,128)(2,1)S(1)} %all_gather.18.refs_2_), channel_id=1, source_target_pairs={{0,8},{8,16},{16,24},{24,32},{32,40},{40,48},{48,56},{56,64},{64,7... | collective-permute-start | bytes 786440 | tf_op jit(solution)/shard_map/ppermute | solution.py:271
  35.8 13.2 %collective-permute-start.1 = (bf16[32,2,16,128]{3,2,1,0:T(8,128)(2,1)S(1)}, bf16[32,2,16,128]{3,2,1,0:T(8,128)(2,1)S(1)}, u32[]{:S(2)}, u32[]{:S(2)}) collective-permute-start(bf16[32,2,16,128]{3,2,1,0:T(8,128)(2,1)S(1)} %all_gather.18.refs_2_), channel_id=1, source_target_pairs={{0,16},{8,24},{16,32},{24,40},{32,48},{40,56},{48,64},{56,72},{64,... | collective-permute-start | bytes 786440 | tf_op jit(solution)/shard_map/ppermute | solution.py:271
  37.1 21.6 %collective-permute-start.4 = (bf16[32,2,16,128]{3,2,1,0:T(8,128)(2,1)S(1)}, bf16[32,2,16,128]{3,2,1,0:T(8,128)(2,1)S(1)}, u32[]{:S(2)}, u32[]{:S(2)}) collective-permute-start(bf16[32,2,16,128]{3,2,1,0:T(8,128)(2,1)S(1)} %all_gather.18.refs_2_), channel_id=1, source_target_pairs={{0,72},{8,80},{16,88},{24,96},{32,104},{40,112},{48,120},{128,208}... | collective-permute-start | bytes 786440 | tf_op jit(solution)/shard_map/ppermute | solution.py:271
  37.7 23.3 %collective-permute-start.3 = (bf16[32,2,16,128]{3,2,1,0:T(8,128)(2,1)S(1)}, bf16[32,2,16,128]{3,2,1,0:T(8,128)(2,1)S(1)}, u32[]{:S(2)}, u32[]{:S(2)}) collective-permute-start(bf16[32,2,16,128]{3,2,1,0:T(8,128)(2,1)S(1)} %all_gather.18.refs_2_), channel_id=1, source_target_pairs={{0,40},{8,48},{16,56},{24,64},{32,72},{40,80},{48,88},{56,96},{64,... | collective-permute-start | bytes 786440 | tf_op jit(solution)/shard_map/ppermute | solution.py:271
  41.2 23.2 %collective-permute-start.2 = (bf16[32,2,16,128]{3,2,1,0:T(8,128)(2,1)S(1)}, bf16[32,2,16,128]{3,2,1,0:T(8,128)(2,1)S(1)}, u32[]{:S(2)}, u32[]{:S(2)}) collective-permute-start(bf16[32,2,16,128]{3,2,1,0:T(8,128)(2,1)S(1)} %all_gather.18.refs_2_), channel_id=1, source_target_pairs={{0,24},{8,32},{16,40},{24,48},{32,56},{40,64},{48,72},{56,80},{64,... | collective-permute-start | bytes 786440 | tf_op jit(solution)/shard_map/ppermute | solution.py:271

commit v10 on v9

--- a/solution.py
+++ b/solution.py
@@ -208,10 +208,10 @@
 
         lax.fori_loop(0, count, again, 0)
 
-    total = jnp.sum(l_ref[...], axis=0, keepdims=True)
+    share = 1.0 / jnp.sum(l_ref[...], axis=0, keepdims=True)
     for h in range(heads):
         at = slice(h * rows, (h + 1) * rows)
-        attended = acc_ref[:, at] / total[:, at]
+        attended = acc_ref[:, at] * share[:, at]
         out_ref[:, h * HD : (h + 1) * HD] = attended.T.astype(jnp.bfloat16)
 
 

time: 74 us -> 73.9 us (level)
  the two profiles are of different devices: /device:TPU:19 before, /device:TPU:21 now
where the time goes in v10:
time: 73.9 us; the launch traced here: 72.6 us
  blocking collectives  50.4 us (68%)
  Pallas kernels  13.2 us (18%)
  starting transfers between devices  8.07 us (11%)
  local copies, waits for them, and re-layouts  0.82 us (1%)
    all_to_all x1, blocking collectives, shards(): lax.all_to_all(send, ('zhi', 'tp'), split_axis=0, concat_axis=0, tiled=True)  26.7 us
    all_gather x5, blocking collectives, shards(): pieces[i] = token = lax.all_gather(a, 'core', axis=0, tiled=True)  18.4 us
    pallas_call x2, Pallas kernels, attend(): pl.pallas_call(kernel, out_shape=out if last else tuple((jax.ShapeDtypeSt...  13.2 us
    ppermute x5, starting transfers between devices, shards(): arrived.append(lax.ppermute(own, ('core', 'ctx'), pairs))  8.07 us
    all_gather x1, blocking collectives, shards(): own = lax.all_gather(half, 'core', axis=0, tiled=True)  5.27 us
  transfers between devices with their start and end apart: 5, of which 0 were waited for; matrix products, arithmetic and copies ran while one was open for 0% of the time, Pallas kernels for 10%

profile of v10, /device:TPU:21, one launch (start us, length us, event | category | flops | bytes accessed | tf_op | source)
XLA Modules:
  0.0 72.6 jit_solution(6409366467170093611)
XLA Ops:
  0.0 0.0 copy-start.1
  0.0 0.8 %copy.9 = bf16[2,8,8,128]{3,2,1,0:T(8,128)(2,1)S(1)} copy(bf16[2,8,8,128]{3,1,2,0:T(8,128)(2,1)} %bitcast.20) | data formatting | bytes 65536
  0.8 0.0 copy-done.1
  0.9 26.7 %all_to_all.5 = bf16[16,2,16,128]{3,2,1,0:T(8,128)(2,1)S(1)} all-to-all(bf16[16,2,16,128]{3,2,1,0:T(8,128)(2,1)S(1)} %copy.8), channel_id=1, replica_groups=mesh['zhi'=2,'core'=2,'ctx'=16,'tp'=8] {'zhi','tp'}, dimensions={0} | all-to-all | bytes 262144 | tf_op jit(solution)/shard_map/all_to_all | solution.py:264
  27.6 5.3 %all_gather.18.refs_2_ = bf16[32,2,16,128]{3,2,1,0:T(8,128)(2,1)S(1)} all-gather(bf16[16,2,16,128]{3,2,1,0:T(8,128)(2,1)S(1)} %all_to_all.5), channel_id=1, replica_groups=mesh['zhi'=2,'core'=2,'ctx'=16,'tp'=8] {'core'}, dimensions={0}, use_global_device_ids=true | all-gather | bytes 393216 | tf_op jit(solution)/shard_map/all_gather | solution.py:265
  32.9 0.0 copy-start
  32.9 2.9 %collective-permute-start = (bf16[32,2,16,128]{3,2,1,0:T(8,128)(2,1)S(1)}, bf16[32,2,16,128]{3,2,1,0:T(8,128)(2,1)S(1)}, u32[]{:S(2)}, u32[]{:S(2)}) collective-permute-start(bf16[32,2,16,128]{3,2,1,0:T(8,128)(2,1)S(1)} %all_gather.18.refs_2_), channel_id=1, source_target_pairs={{0,8},{8,16},{16,24},{24,32},{32,40},{40,48},{48,56},{56,64},{64,7... | collective-permute-start | bytes 786440 | tf_op jit(solution)/shard_map/ppermute | solution.py:271
  35.8 1.3 %collective-permute-start.1 = (bf16[32,2,16,128]{3,2,1,0:T(8,128)(2,1)S(1)}, bf16[32,2,16,128]{3,2,1,0:T(8,128)(2,1)S(1)}, u32[]{:S(2)}, u32[]{:S(2)}) collective-permute-start(bf16[32,2,16,128]{3,2,1,0:T(8,128)(2,1)S(1)} %all_gather.18.refs_2_), channel_id=1, source_target_pairs={{0,16},{8,24},{16,32},{24,40},{32,48},{40,56},{48,64},{56,72},{64,... | collective-permute-start | bytes 786440 | tf_op jit(solution)/shard_map/ppermute | solution.py:271
  37.1 1.3 %collective-permute-start.4 = (bf16[32,2,16,128]{3,2,1,0:T(8,128)(2,1)S(1)}, bf16[32,2,16,128]{3,2,1,0:T(8,128)(2,1)S(1)}, u32[]{:S(2)}, u32[]{:S(2)}) collective-permute-start(bf16[32,2,16,128]{3,2,1,0:T(8,128)(2,1)S(1)} %all_gather.18.refs_2_), channel_id=1, source_target_pairs={{0,72},{8,80},{16,88},{24,96},{32,104},{40,112},{48,120},{128,208}... | collective-permute-start | bytes 786440 | tf_op jit(solution)/shard_map/ppermute | solution.py:271
  38.4 1.3 %collective-permute-start.3 = (bf16[32,2,16,128]{3,2,1,0:T(8,128)(2,1)S(1)}, bf16[32,2,16,128]{3,2,1,0:T(8,128)(2,1)S(1)}, u32[]{:S(2)}, u32[]{:S(2)}) collective-permute-start(bf16[32,2,16,128]{3,2,1,0:T(8,128)(2,1)S(1)} %all_gather.18.refs_2_), channel_id=1, source_target_pairs={{0,40},{8,48},{16,56},{24,64},{32,72},{40,80},{48,88},{56,96},{64,... | collective-permute-start | bytes 786440 | tf_op jit(solution)/shard_map/ppermute | solution.py:271
  39.7 1.3 %collective-permute-start.2 = (bf16[32,2,16,128]{3,2,1,0:T(8,128)(2,1)S(1)}, bf16[32,2,16,128]{3,2,1,0:T(8,128)(2,1)S(1)}, u32[]{:S(2)}, u32[]{:S(2)}) collective-permute-start(bf16[32,2,16,128]{3,2,1,0:T(8,128)(2,1)S(1)} %all_gather.18.refs_2_), channel_id=1, source_target_pairs={{0,24},{8,32},{16,40},{24,48},{32,56},{40,64},{48,72},{56,80},{64,... | collective-permute-start | bytes 786440 | tf_op jit(solution)/shard_map/ppermute | solution.py:271
  41.0 0.0 collective-permute-done
  41.0 5.9 %all_gather.19.refs_3_ = bf16[64,2,16,128]{3,2,1,0:T(8,128)(2,1)} all-gather(bf16[32,2,16,128]{3,2,1,0:T(8,128)(2,1)S(1)} %collective-permute-done), channel_id=1, replica_groups=mesh['zhi'=2,'core'=2,'ctx'=16,'tp'=8] {'core'}, dimensions={0}, use_global_device_ids=true | all-gather | bytes 786432 | tf_op jit(solution)/shard_map/all_gather | solution.py:280
  46.9 0.0 copy-done
  46.9 0.0 collective-permute-done.1
  46.9 3.4 %all_gather.20.refs_4_ = bf16[64,2,16,128]{3,2,1,0:T(8,128)(2,1)} all-gather(bf16[32,2,16,128]{3,2,1,0:T(8,128)(2,1)S(1)} %collective-permute-done.1), channel_id=1, replica_groups=mesh['zhi'=2,'core'=2,'ctx'=16,'tp'=8] {'core'}, dimensions={0}, use_global_device_ids=true | all-gather | bytes 786432 | tf_op jit(solution)/shard_map/all_gather | solution.py:280
  50.3 7.2 %attend_first.1 = (f32[1,1024]{1,0:T(1,128)}, f32[8,1024]{1,0:T(8,128)}, f32[128,1024]{1,0:T(8,128)}) custom-call(s32[4]{0:T(128)} %refs_0_.3, bf16[512,256]{1,0:T(8,128)(2,1)} %bitcast.16, bf16[32,2,16,128]{3,2,1,0:T(8,128)(2,1)} %copy-done, bf16[64,2,16,128]{3,2,1,0:T(8,128)(2,1)} %all_gather.19.refs_3_, bf16[64,2,16,128]{3,2,1,0:T(8,128)(2,1)} %all_gather.20.refs_4_), custom_call_target="tpu_custom_call" | custom-call | tf_op jit(solution)/shard_map/attend_first/pallas_call | solution.py:235
  57.5 0.0 collective-permute-done.4
  57.5 2.3 %all_gather.21.refs_7_ = bf16[64,2,16,128]{3,2,1,0:T(8,128)(2,1)} all-gather(bf16[32,2,16,128]{3,2,1,0:T(8,128)(2,1)S(1)} %collective-permute-done.4), channel_id=1, replica_groups=mesh['zhi'=2,'core'=2,'ctx'=16,'tp'=8] {'core'}, dimensions={0}, use_global_device_ids=true | all-gather | bytes 786432 | tf_op jit(solution)/shard_map/all_gather | solution.py:280
  59.8 0.0 collective-permute-done.3
  59.8 4.5 %all_gather.22.refs_6_ = bf16[64,2,16,128]{3,2,1,0:T(8,128)(2,1)} all-gather(bf16[32,2,16,128]{3,2,1,0:T(8,128)(2,1)S(1)} %collective-permute-done.3), channel_id=1, replica_groups=mesh['zhi'=2,'core'=2,'ctx'=16,'tp'=8] {'core'}, dimensions={0}, use_global_device_ids=true | all-gather | bytes 786432 | tf_op jit(solution)/shard_map/all_gather | solution.py:280
  64.3 0.0 collective-permute-done.2
  64.3 2.3 %all_gather.23.refs_5_ = bf16[64,2,16,128]{3,2,1,0:T(8,128)(2,1)} all-gather(bf16[32,2,16,128]{3,2,1,0:T(8,128)(2,1)S(1)} %collective-permute-done.2), channel_id=1, replica_groups=mesh['zhi'=2,'core'=2,'ctx'=16,'tp'=8] {'core'}, dimensions={0}, use_global_device_ids=true | all-gather | bytes 786432 | tf_op jit(solution)/shard_map/all_gather | solution.py:280
  66.6 6.0 %attend_last.1 = bf16[512,256]{1,0:T(8,128)(2,1)} custom-call(s32[4]{0:T(128)} %refs_0_.3, bf16[512,256]{1,0:T(8,128)(2,1)} %bitcast.17, bf16[32,2,16,128]{3,2,1,0:T(8,128)(2,1)} %copy-done, bf16[64,2,16,128]{3,2,1,0:T(8,128)(2,1)} %all_gather.19.refs_3_, bf16[64,2,16,128]{3,2,1,0:T(8,128)(2,1)} %all_gather.20.refs_4_, ...), custom_call_target="tpu_custom_call" | custom-call | tf_op jit(solution)/shard_map/attend_last/pallas_call | solution.py:235
  (3 shorter events, 0.1 us)
Async XLA Ops:
  0.0 0.8 %copy-start.1 = (bf16[1,16,1024]{2,1,0:T(8,128)(2,1)S(1)}, bf16[1,16,1024]{2,1,0:T(8,128)(2,1)}, u32[]{:S(2)}) copy-start(bf16[1,16,1024]{2,1,0:T(8,128)(2,1)} %param.6) | copy-start | bytes 98308
  32.9 14.0 %copy-start = (bf16[32,2,16,128]{3,2,1,0:T(8,128)(2,1)}, bf16[32,2,16,128]{3,2,1,0:T(8,128)(2,1)S(1)}, u32[]{:S(2)}) copy-start(bf16[32,2,16,128]{3,2,1,0:T(8,128)(2,1)S(1)} %all_gather.18.refs_2_) | copy-start | bytes 786436
  32.9 8.1 %collective-permute-start = (bf16[32,2,16,128]{3,2,1,0:T(8,128)(2,1)S(1)}, bf16[32,2,16,128]{3,2,1,0:T(8,128)(2,1)S(1)}, u32[]{:S(2)}, u32[]{:S(2)}) collective-permute-start(bf16[32,2,16,128]{3,2,1,0:T(8,128)(2,1)S(1)} %all_gather.18.refs_2_), channel_id=1, source_target_pairs={{0,8},{8,16},{16,24},{24,32},{32,40},{40,48},{48,56},{56,64},{64,7... | collective-permute-start | bytes 786440 | tf_op jit(solution)/shard_map/ppermute | solution.py:271
  35.8 11.1 %collective-permute-start.1 = (bf16[32,2,16,128]{3,2,1,0:T(8,128)(2,1)S(1)}, bf16[32,2,16,128]{3,2,1,0:T(8,128)(2,1)S(1)}, u32[]{:S(2)}, u32[]{:S(2)}) collective-permute-start(bf16[32,2,16,128]{3,2,1,0:T(8,128)(2,1)S(1)} %all_gather.18.refs_2_), channel_id=1, source_target_pairs={{0,16},{8,24},{16,32},{24,40},{32,48},{40,56},{48,64},{56,72},{64,... | collective-permute-start | bytes 786440 | tf_op jit(solution)/shard_map/ppermute | solution.py:271
  37.1 20.4 %collective-permute-start.4 = (bf16[32,2,16,128]{3,2,1,0:T(8,128)(2,1)S(1)}, bf16[32,2,16,128]{3,2,1,0:T(8,128)(2,1)S(1)}, u32[]{:S(2)}, u32[]{:S(2)}) collective-permute-start(bf16[32,2,16,128]{3,2,1,0:T(8,128)(2,1)S(1)} %all_gather.18.refs_2_), channel_id=1, source_target_pairs={{0,72},{8,80},{16,88},{24,96},{32,104},{40,112},{48,120},{128,208}... | collective-permute-start | bytes 786440 | tf_op jit(solution)/shard_map/ppermute | solution.py:271
  38.4 21.4 %collective-permute-start.3 = (bf16[32,2,16,128]{3,2,1,0:T(8,128)(2,1)S(1)}, bf16[32,2,16,128]{3,2,1,0:T(8,128)(2,1)S(1)}, u32[]{:S(2)}, u32[]{:S(2)}) collective-permute-start(bf16[32,2,16,128]{3,2,1,0:T(8,128)(2,1)S(1)} %all_gather.18.refs_2_), channel_id=1, source_target_pairs={{0,40},{8,48},{16,56},{24,64},{32,72},{40,80},{48,88},{56,96},{64,... | collective-permute-start | bytes 786440 | tf_op jit(solution)/shard_map/ppermute | solution.py:271
  39.7 24.6 %collective-permute-start.2 = (bf16[32,2,16,128]{3,2,1,0:T(8,128)(2,1)S(1)}, bf16[32,2,16,128]{3,2,1,0:T(8,128)(2,1)S(1)}, u32[]{:S(2)}, u32[]{:S(2)}) collective-permute-start(bf16[32,2,16,128]{3,2,1,0:T(8,128)(2,1)S(1)} %all_gather.18.refs_2_), channel_id=1, source_target_pairs={{0,24},{8,32},{16,40},{24,48},{32,56},{40,64},{48,72},{56,80},{64,... | collective-permute-start | bytes 786440 | tf_op jit(solution)/shard_map/ppermute | solution.py:271
